TPU v7x, 32 devices: a whole 2x2x4 slice. The times are simulated.
32 devices in a mesh: seq: 16 (over z, y, core), tp: 2 (over x).
Axes of the slice: x: 2, y: 2, z: 4, core: 2. Of those that a mesh axis runs over, the one named last changes fastest.
Arguments:
- layer_in: bfloat16 [32768, 768], P(('seq', 'tp')), may hold values from -6 to 6
- skip_values: bfloat16 [32768, 384], P('seq', 'tp'), may hold values from -6 to 6
- block_slot: int32 [16, 8], replicated, may hold values from 0 to 3, as said below
- doc_lengths: int32 [32, 4], replicated, may hold values from 1 to 512, 1024 in all within a row
- gain_attention: float32 [768], replicated, may hold values from 0.5 to 1.5
- shift_attention: float32 [768], replicated, may hold values from -1.5 to 1.5
- query_weight: bfloat16 [768, 768], P(None, 'tp'), may hold values from -0.21875 to 0.21875
- query_bias: float32 [768], P('tp'), may hold values from -1.5 to 1.5
- key_weight: bfloat16 [768, 768], P(None, 'tp'), may hold values from -0.21875 to 0.21875
- value_weight: bfloat16 [768, 384], P(None, 'tp'), may hold values from -0.21875 to 0.21875
- value_bias: float32 [384], P('tp'), may hold values from -1.5 to 1.5
- out_weight: bfloat16 [768, 768], P('tp'), may hold values from -1.75 to 1.75
- out_bias: float32 [768], replicated, may hold values from -1.5 to 1.5
- gain_feed: float32 [768], replicated, may hold values from 0.5 to 1.5
- shift_feed: float32 [768], replicated, may hold values from -1.5 to 1.5
- up_weight: bfloat16 [768, 3072], P(None, 'tp'), may hold values from -0.21875 to 0.21875
- up_bias: float32 [3072], P('tp'), may hold values from -1.5 to 1.5
- down_weight: bfloat16 [3072, 768], P('tp'), may hold values from -0.109375 to 0.109375
- down_bias: float32 [768], replicated, may hold values from -1.5 to 1.5
- out_grad: bfloat16 [32768, 768], P(('seq', 'tp')), may hold values from -6 to 6
Outputs:
- layer_out: bfloat16 [32768, 768], P(('seq', 'tp'))
- input_grad: float32 [32768, 768], P(('seq', 'tp'))
- skip_grad: float32 [32768, 384], P('seq', 'tp')
- grad_gain_attention: float32 [768], replicated
- grad_shift_attention: float32 [768], replicated
- grad_query_weight: float32 [768, 768], P(None, 'tp')
- grad_query_bias: float32 [768], P('tp')
- grad_key_weight: float32 [768, 768], P(None, 'tp')
- grad_value_weight: float32 [768, 384], P(None, 'tp')
- grad_value_bias: float32 [384], P('tp')
- grad_out_weight: float32 [768, 768], P('tp')
- grad_out_bias: float32 [768], replicated
- grad_gain_feed: float32 [768], replicated
- grad_shift_feed: float32 [768], replicated
- grad_up_weight: float32 [768, 3072], P(None, 'tp')
- grad_up_bias: float32 [3072], P('tp')
- grad_down_weight: float32 [3072, 768], P('tp')
- grad_down_bias: float32 [768], replicated
Inputs may be any that keep to these rules, and one draw needn't show every extreme that they name: `block_slot`: for each group of 4 consecutive rows (the seq indices that hold one set of sequences) and each column, the entries are a permutation of 0 to 3. `doc_lengths`: each row gives the lengths of the documents of one sequence in order; a row sums to 1024.
All inputs are finite; a program needn't handle non-finite values.
Results may differ from a plain program's by a relative error of at most 0.015.
Values may be sent and summed in bfloat16 or wider, within the bound.
No kernel may reach another device: no remote copies, remote signals or barrier semaphores. Data moves between devices by JAX's collectives and lax.ppermute only.
A program may use at most 320 MiB of HBM per device.

v0:
```python
from functools import partial
from functools import reduce

import jax
import jax.numpy as jnp
from jax import lax
from jax.sharding import PartitionSpec as P

HEAD = 64
SEQ_LEN = 1024
BLOCK = 256


EPSILON = 1e-05


def from_partner(block, axis, apart):
    count = lax.axis_size(axis)
    route = []
    for low in range(count):
        high = low | 1 << apart
        if high != low and high < count:
            route += [(low, high), (high, low)]
    return lax.ppermute(block, axis, route)


def product(left, right):
    return jnp.dot(left, right, preferred_element_type=jnp.float32)


def product_rt(left, right):
    return lax.dot_general(
        left, right, (((1,), (1,)), ((), ())), preferred_element_type=jnp.float32
    )


def product_lt(left, right):
    return lax.dot_general(
        left, right, (((0,), (0,)), ((), ())), preferred_element_type=jnp.float32
    )


def norm_rows(rows, gain, shift):
    centred = rows - jnp.mean(rows, axis=-1, keepdims=True)
    inverse = lax.rsqrt(jnp.mean(centred * centred, axis=-1, keepdims=True) + EPSILON)
    scaled = centred * inverse
    return (scaled * gain + shift, scaled, inverse)


def norm_back(grad_out, scaled, inverse, gain):
    grad_scaled = grad_out * gain
    first_mean = jnp.mean(grad_scaled, axis=-1, keepdims=True)
    second_mean = jnp.mean(grad_scaled * scaled, axis=-1, keepdims=True)
    return inverse * (grad_scaled - first_mean - scaled * second_mean)


def block_places(slots, bounds):
    within = jnp.arange(BLOCK, dtype=jnp.int32)
    places = slots[:, None] * BLOCK + within[None, :]
    doc_ids = jnp.sum((places[:, :, None] >= bounds[:, None, :]).astype(jnp.int32), axis=2)
    return (places, doc_ids)


def swap_blocks(held, level):
    return from_partner(held, "seq", level)


def swap_grads(held, level):
    return from_partner(held.astype(jnp.bfloat16), "seq", level).astype(held.dtype)


def per_device(
    layer_in,
    skip_values,
    block_slot,
    doc_lengths,
    gain_attention,
    shift_attention,
    query_weight,
    query_bias,
    key_weight,
    value_weight,
    value_bias,
    out_weight,
    out_bias,
    gain_feed,
    shift_feed,
    up_weight,
    up_bias,
    down_weight,
    down_bias,
    out_grad,
):
    seq_span = SEQ_LEN // BLOCK
    span_levels = seq_span.bit_length() - 1
    level_order = list(range(span_levels))
    seq_batch = skip_values.shape[0] // BLOCK
    rows_all = seq_batch * BLOCK
    heads_here = query_weight.shape[1] // HEAD
    fresh_cols = value_weight.shape[1]
    score_scale = HEAD ** (-0.5)
    my_index = lax.axis_index("seq")
    my_member = my_index % seq_span
    group_id = my_index // seq_span
    lengths_here = lax.dynamic_slice_in_dim(doc_lengths, group_id * seq_batch, seq_batch, 0)
    bounds = jnp.cumsum(lengths_here, axis=1)[:, :-1]

    def places_of(member_id):
        slots = lax.dynamic_index_in_dim(
            block_slot, group_id * seq_span + member_id, 0, keepdims=False
        )
        return block_places(slots, bounds)

    own_places, own_docs = places_of(my_member)

    def visible_of(member_id):
        key_places, key_docs = places_of(member_id)
        return (key_places[:, None, :] <= own_places[:, :, None]) & (
            key_docs[:, None, :] == own_docs[:, :, None]
        )

    def heads_view(rows):
        return rows.reshape(seq_batch, BLOCK, heads_here, HEAD)

    input_float = layer_in.astype(jnp.float32)
    first_norm, first_scaled, first_inverse = norm_rows(
        input_float, gain_attention, shift_attention
    )
    first_rows = lax.all_gather(first_norm.astype(jnp.bfloat16), "tp", axis=0, tiled=True)
    queries = (product(first_rows, query_weight) + query_bias).astype(jnp.bfloat16)
    keys_here = product(first_rows, key_weight).astype(jnp.bfloat16)
    fresh = (product(first_rows, value_weight) + value_bias).astype(jnp.bfloat16)
    values_here = jnp.concatenate([fresh, skip_values], axis=1)
    query_heads = heads_view(queries)
    sources = [(heads_view(keys_here), heads_view(values_here), visible_of(my_member))]
    held = jnp.stack([keys_here, values_here])[None]
    for level in level_order:
        held = jnp.concatenate([held, swap_blocks(held, level)], axis=0)
    for slot in range(1, seq_span):
        partner = 0
        for step in range(span_levels):
            partner = partner + ((slot >> step & 1) << level_order[step])
        sources.append(
            (
                heads_view(held[slot, 0]),
                heads_view(held[slot, 1]),
                visible_of(jnp.bitwise_xor(my_member, partner)),
            )
        )

    def scores_of(key_heads, seen_mask):
        raw = (
            jnp.einsum(
                "bqhe,bkhe->bhqk", query_heads, key_heads, preferred_element_type=jnp.float32
            )
            * score_scale
        )
        return jnp.where(seen_mask[:, None], raw, -jnp.inf)

    score_list = [scores_of(key_heads, seen_mask) for key_heads, value_heads, seen_mask in sources]
    row_max = reduce(jnp.maximum, [jnp.max(scores, axis=-1) for scores in score_list])
    row_total = reduce(
        jnp.add, [jnp.sum(jnp.exp(scores - row_max[..., None]), axis=-1) for scores in score_list]
    )
    log_total = row_max + jnp.log(row_total)
    attended = reduce(
        jnp.add,
        [
            jnp.einsum(
                "bhqk,bkhe->bqhe",
                jnp.exp(scores - log_total[..., None]).astype(jnp.bfloat16),
                source[1],
                preferred_element_type=jnp.float32,
            )
            for scores, source in zip(score_list, sources)
        ],
    )
    attended_rows = attended.reshape(rows_all, heads_here * HEAD).astype(jnp.bfloat16)
    middle = (
        input_float
        + lax.psum_scatter(
            product(attended_rows, out_weight).astype(jnp.bfloat16),
            "tp",
            scatter_dimension=0,
            tiled=True,
        ).astype(jnp.float32)
        + out_bias
    )
    second_norm, second_scaled, second_inverse = norm_rows(middle, gain_feed, shift_feed)
    second_rows = lax.all_gather(second_norm.astype(jnp.bfloat16), "tp", axis=0, tiled=True)
    hidden = product(second_rows, up_weight) + up_bias
    activated, gelu_back = jax.vjp(partial(jax.nn.gelu, approximate=True), hidden)
    activated_low = activated.astype(jnp.bfloat16)
    feed_out = lax.psum_scatter(
        product(activated_low, down_weight).astype(jnp.bfloat16),
        "tp",
        scatter_dimension=0,
        tiled=True,
    ).astype(jnp.float32)
    layer_out = (middle + feed_out + down_bias).astype(jnp.bfloat16)
    grad_output = out_grad.astype(jnp.float32)
    grad_down_bias = jnp.sum(grad_output, axis=0)
    grad_rows_all = lax.all_gather(out_grad, "tp", axis=0, tiled=True)
    grad_down_weight = product_lt(activated_low, grad_rows_all)
    grad_hidden = gelu_back(product_rt(grad_rows_all, down_weight))[0]
    grad_up_bias = jnp.sum(grad_hidden, axis=0)
    hidden_low = grad_hidden.astype(jnp.bfloat16)
    grad_up_weight = product_lt(second_rows, hidden_low)
    second_grad = lax.psum_scatter(
        product_rt(hidden_low, up_weight).astype(jnp.bfloat16),
        "tp",
        scatter_dimension=0,
        tiled=True,
    ).astype(jnp.float32)
    grad_gain_feed = jnp.sum(second_grad * second_scaled, axis=0)
    grad_shift_feed = jnp.sum(second_grad, axis=0)
    middle_grad = grad_output + norm_back(second_grad, second_scaled, second_inverse, gain_feed)
    grad_out_bias = jnp.sum(middle_grad, axis=0)
    middle_rows = lax.all_gather(middle_grad.astype(jnp.bfloat16), "tp", axis=0, tiled=True)
    grad_out_weight = product_lt(attended_rows, middle_rows)
    grad_heads = heads_view(product_rt(middle_rows, out_weight).astype(jnp.bfloat16))
    prob_list = []
    dprob_list = []
    for key_heads, value_heads, seen_mask in sources:
        prob_list.append(jnp.exp(scores_of(key_heads, seen_mask) - log_total[..., None]))
        dprob_list.append(
            jnp.einsum(
                "bqhe,bkhe->bhqk", grad_heads, value_heads, preferred_element_type=jnp.float32
            )
        )
    delta = reduce(
        jnp.add, [jnp.sum(probs * dprobs, axis=-1) for probs, dprobs in zip(prob_list, dprob_list)]
    )
    query_parts = []
    pair_grads = []
    for probs, dprobs, source in zip(prob_list, dprob_list, sources):
        dscores = (probs * (dprobs - delta[..., None])).astype(jnp.bfloat16)
        query_parts.append(
            jnp.einsum("bhqk,bkhe->bqhe", dscores, source[0], preferred_element_type=jnp.float32)
            * score_scale
        )
        key_part = (
            jnp.einsum("bhqk,bqhe->bkhe", dscores, query_heads, preferred_element_type=jnp.float32)
            * score_scale
        )
        value_part = jnp.einsum(
            "bhqk,bqhe->bkhe",
            probs.astype(jnp.bfloat16),
            grad_heads,
            preferred_element_type=jnp.float32,
        )
        pair_grads.append(jnp.stack([key_part, value_part]))
    held_grads = jnp.stack(pair_grads)
    for step in reversed(range(span_levels)):
        half = 1 << step
        held_grads = held_grads[:half] + swap_grads(held_grads[half:], level_order[step])
    pair_total = held_grads[0]
    query_grad = reduce(jnp.add, query_parts).reshape(rows_all, heads_here * HEAD)
    key_grad = pair_total[0].reshape(rows_all, heads_here * HEAD)
    value_grad = pair_total[1].reshape(rows_all, heads_here * HEAD)
    fresh_grad = value_grad[:, :fresh_cols]
    skip_grad = value_grad[:, fresh_cols:]
    grad_query_bias = jnp.sum(query_grad, axis=0)
    grad_value_bias = jnp.sum(fresh_grad, axis=0)
    query_low = query_grad.astype(jnp.bfloat16)
    key_low = key_grad.astype(jnp.bfloat16)
    fresh_low = fresh_grad.astype(jnp.bfloat16)
    grad_query_weight = product_lt(first_rows, query_low)
    grad_key_weight = product_lt(first_rows, key_low)
    grad_value_weight = product_lt(first_rows, fresh_low)
    first_terms = (
        product_rt(query_low, query_weight)
        + product_rt(key_low, key_weight)
        + product_rt(fresh_low, value_weight)
    )
    first_grad = lax.psum_scatter(
        first_terms.astype(jnp.bfloat16), "tp", scatter_dimension=0, tiled=True
    ).astype(jnp.float32)
    grad_gain_attention = jnp.sum(first_grad * first_scaled, axis=0)
    grad_shift_attention = jnp.sum(first_grad, axis=0)
    input_grad = middle_grad + norm_back(first_grad, first_scaled, first_inverse, gain_attention)
    (
        grad_query_weight,
        grad_query_bias,
        grad_key_weight,
        grad_value_weight,
        grad_value_bias,
        grad_out_weight,
        grad_up_weight,
        grad_up_bias,
        grad_down_weight,
    ) = lax.psum(
        (
            grad_query_weight,
            grad_query_bias,
            grad_key_weight,
            grad_value_weight,
            grad_value_bias,
            grad_out_weight,
            grad_up_weight,
            grad_up_bias,
            grad_down_weight,
        ),
        "seq",
    )
    (
        grad_gain_attention,
        grad_shift_attention,
        grad_gain_feed,
        grad_shift_feed,
        grad_out_bias,
        grad_down_bias,
    ) = lax.psum(
        (
            grad_gain_attention,
            grad_shift_attention,
            grad_gain_feed,
            grad_shift_feed,
            grad_out_bias,
            grad_down_bias,
        ),
        ("seq", "tp"),
    )
    return (
        layer_out,
        input_grad,
        skip_grad,
        grad_gain_attention,
        grad_shift_attention,
        grad_query_weight,
        grad_query_bias,
        grad_key_weight,
        grad_value_weight,
        grad_value_bias,
        grad_out_weight,
        grad_out_bias,
        grad_gain_feed,
        grad_shift_feed,
        grad_up_weight,
        grad_up_bias,
        grad_down_weight,
        grad_down_bias,
    )


def solution(mesh):
    return jax.shard_map(
        per_device,
        mesh=mesh,
        in_specs=(
            P(("seq", "tp"), None),
            P("seq", "tp"),
            P(),
            P(),
            P(),
            P(),
            P(None, "tp"),
            P("tp"),
            P(None, "tp"),
            P(None, "tp"),
            P("tp"),
            P("tp", None),
            P(),
            P(),
            P(),
            P(None, "tp"),
            P("tp"),
            P("tp", None),
            P(),
            P(("seq", "tp"), None),
        ),
        out_specs=(
            P(("seq", "tp"), None),
            P(("seq", "tp"), None),
            P("seq", "tp"),
            P(),
            P(),
            P(None, "tp"),
            P("tp"),
            P(None, "tp"),
            P(None, "tp"),
            P("tp"),
            P("tp", None),
            P(),
            P(),
            P(),
            P(None, "tp"),
            P("tp"),
            P("tp", None),
            P(),
        ),
        check_vma=False,
    )
```

profile of v0, /device:TPU:0, one launch (start us, length us, event | category | flops | bytes accessed | tf_op | source)
XLA Modules:
  0.0 1259.1 jit_solution(5588381925399778991)
XLA Ops:
  13.7 47.7 %all-gather.5.cloned.1.call-done = bf16[2048,768]{1,0:T(8,128)(2,1)} async-done(((bf16[1024,768]{1,0:T(8,128)(2,1)}), bf16[2048,768]{1,0:T(8,128)(2,1)}) %all-gather.5.cloned.1.call-update) | async-done | bytes 3145744 | tf_op jit(solution)/shard_map/all_gather | solution.py:129
  109.8 107.2 %collective-permute-done.1 = bf16[2,2,2048,384]{2,3,1,0:T(8,128)(2,1)} collective-permute-done((bf16[2,2,2048,384]{2,3,1,0:T(8,128)(2,1)}, bf16[2,2,2048,384]{2,3,1,0:T(8,128)(2,1)}, u32[]{:S(2)}, u32[]{:S(2)}) %collective-permute-start.1) | collective-permute-done | bytes 6291488 | tf_op jit(solution)/shard_map/ppermute | solution.py:24
  233.4 20.6 %exponential_reduce_fusion.2 = (f32[8,6,256]{2,1,0:T(8,128)S(1)}, f32[8,6,256]{2,1,0:T(8,128)S(1)}, f32[8,6,256]{2,1,0:T(8,128)S(1)}, f32[8,6,256]{2,1,0:T(8,128)S(1)}) fusion(f32[8,6,256,256]{2,3,1,0:T(8,128)} %get-tuple-element.86, f32[8,6,256]{2,1,0:T(8,128)S(1)} %maximum_maximum_fusion, pred[8,256,256]{1,2,0:T(8,128)(4,1)S(1)} %copy-done.24, ...), kind=kLoop, calls=%fused_computation.24 | loop fusion | flops 50282496 | bytes 52674560 | tf_op jit(solution)/shard_map/reduce_sum | solution.py:163
  254.1 9.3 fusion.51
  263.3 9.3 fusion.55
  272.6 9.2 fusion.59
  297.5 43.4 %reduce-scatter.5.cloned.1.call-done = bf16[1024,768]{1,0:T(8,128)(2,1)} async-done(((bf16[2048,768]{1,0:T(8,128)(2,1)}), bf16[1024,768]{1,0:T(8,128)(2,1)}) %reduce-scatter.5.cloned.1.call-update) | async-done | bytes 1572880 | tf_op jit(solution)/shard_map/reduce_scatter | solution.py:181
  347.3 44.5 %all-gather.7.cloned.1.call-done = bf16[2048,768]{1,0:T(8,128)(2,1)} async-done(((bf16[1024,768]{1,0:T(8,128)(2,1)}), bf16[2048,768]{1,0:T(8,128)(2,1)}) %all-gather.7.cloned.1.call-update) | async-done | bytes 3145744 | tf_op jit(solution)/shard_map/all_gather | solution.py:190
  391.8 13.3 %multiply_convert_fusion.4 = (bf16[2048,1536]{1,0:T(8,128)(2,1)}, f32[2048,1536]{1,0:T(8,128)}) fusion(f32[1536]{0:T(1024)S(1)} %copy-done.80, bf16[2048,768]{1,0:T(8,128)(2,1)} %all-gather.7.cloned.1.call-done, bf16[768,1536]{1,0:T(8,128)(2,1)S(1)} %copy-done), kind=kOutput, calls=%fused_computation.17 | convolution fusion | flops 4863295488 | bytes 24385536 | tf_op jit(solution)/shard_map/dot_general | solution.py:28
  405.1 33.1 %all-gather.9.cloned.1.call-done = bf16[2048,768]{1,0:T(8,128)(2,1)} async-done(((bf16[1024,768]{1,0:T(8,128)(2,1)}), bf16[2048,768]{1,0:T(8,128)(2,1)}) %all-gather.9.cloned.1.call-update) | async-done | bytes 3145744 | tf_op jit(solution)/shard_map/all_gather | solution.py:203
  438.2 17.5 %fusion.107 = (f32[1536]{0:T(1024)}, bf16[2048,1536]{1,0:T(8,128)(2,1)S(1)}) fusion(f32[2048,1536]{1,0:T(8,128)} %get-tuple-element.88, f32[1536]{0:T(1024)S(1)} %copy-done.80, bf16[2048,768]{1,0:T(8,128)(2,1)} %all-gather.9.cloned.1.call-done, bf16[1536,768]{1,0:T(8,128)(2,1)} %param.37), kind=kOutput, calls=%fused_computation.199 | convolution fusion | flops 4901042688 | bytes 24391680 | tf_op jit(solution)/shard_map/dot_general | solution.py:32
  466.4 9.6 convolution_convert_fusion.2
  476.1 32.2 %reduce-scatter.9.cloned.1.call-done = bf16[1024,768]{1,0:T(8,128)(2,1)} async-done(((bf16[2048,768]{1,0:T(8,128)(2,1)}), bf16[1024,768]{1,0:T(8,128)(2,1)}) %reduce-scatter.9.cloned.1.call-update) | async-done | bytes 1572880 | tf_op jit(solution)/shard_map/reduce_scatter | solution.py:209
  512.3 42.0 %reduce-scatter.7.cloned.1.call-done = bf16[1024,768]{1,0:T(8,128)(2,1)} async-done(((bf16[2048,768]{1,0:T(8,128)(2,1)}), bf16[1024,768]{1,0:T(8,128)(2,1)}) %reduce-scatter.7.cloned.1.call-update) | async-done | bytes 1572880 | tf_op jit(solution)/shard_map/reduce_scatter | solution.py:194
  563.0 45.0 %all-gather.11.cloned.1.call-done = bf16[2048,768]{1,0:T(8,128)(2,1)} async-done(((bf16[1024,768]{1,0:T(8,128)(2,1)}), bf16[2048,768]{1,0:T(8,128)(2,1)}) %all-gather.11.cloned.1.call-update) | async-done | bytes 3145744 | tf_op jit(solution)/shard_map/all_gather | solution.py:219
  624.2 9.0 fusion.42
  652.6 36.6 %multiply_reduce_fusion.2 = (f32[8,6,256]{2,1,0:T(8,128)S(1)}, f32[8,6,256]{2,1,0:T(8,128)S(1)}, f32[8,6,256]{2,1,0:T(8,128)S(1)}, f32[8,6,256]{2,1,0:T(8,128)S(1)}, f32[8,6,256,256]{2,3,1,0:T(8,128)}) fusion(f32[8,6,256,256]{2,3,1,0:T(8,128)} %get-tuple-element.86, f32[8,6,256]{2,1,0:T(8,128)S(1)} %log_add_fusion, pred[8,256,256]{1,2,0:T(8,128)(4,1)S(1)} %copy-done.25, ...), kind=kOutput, calls=%fused_computation.15 | convolution fusion | flops 465518592 | bytes 106151936 | tf_op jit(solution)/shard_map/bqhe,bkhe->bhqk/dot_general | solution.py:227
  689.2 42.7 %multiply_convert_fusion.1 = (bf16[8,6,256,256]{2,3,1,0:T(8,128)(2,1)}, bf16[8,6,256,256]{2,3,1,0:T(8,128)(2,1)}, bf16[8,6,256,256]{2,3,1,0:T(8,128)(2,1)}, bf16[8,6,256,256]{2,3,1,0:T(8,128)(2,1)}) fusion(f32[8,6,256,256]{2,3,1,0:T(8,128)} %fusion.49, f32[8,6,256,256]{2,3,1,0:T(8,128)} %get-tuple-element.82, f32[8,6,256]{2,1,0:T(8,128)S(1)} %add_add_fusion, ...), kind=kLoop, calls=%fused_computation.10 | loop fusion | flops 75497472 | bytes 128024576 | tf_op jit(solution)/shard_map/convert_element_type | solution.py:237
  782.4 104.5 %collective-permute-done.2 = bf16[2,2,8,256,6,64]{3,5,4,2,1,0:T(8,128)(2,1)} collective-permute-done((bf16[2,2,8,256,6,64]{3,5,4,2,1,0:T(8,128)(2,1)}, bf16[2,2,8,256,6,64]{3,5,4,2,1,0:T(8,128)(2,1)}, u32[]{:S(2)}, u32[]{:S(2)}) %collective-permute-start.2) | collective-permute-done | bytes 6291488 | tf_op jit(solution)/shard_map/ppermute | solution.py:24
  886.9 11.3 maximum_add_fusion
  938.2 10.0 fusion.37
  972.5 64.0 %all-reduce.1 = (f32[384]{0:T(512)}, f32[192]{0:T(256)}, f32[1536]{0:T(1024)}) all-reduce(f32[384]{0:T(512)S(1)} %reduce_sum.290, f32[192]{0:T(256)S(1)} %get-tuple-element.64, f32[1536]{0:T(1024)S(1)} %copy-done.70), channel_id=1, replica_groups=mesh['seq'=16,'tp'=2] {'seq'}, use_global_device_ids=true, to_apply=%region_35.36 | all-reduce | flops 2112 | bytes 16896 | tf_op jit(solution)/shard_map/psum | solution.py:292
  1039.5 39.5 %all-reduce = (f32[768]{0:T(1024)}, f32[768]{0:T(1024)}, f32[768]{0:T(1024)}, f32[768]{0:T(1024)}, f32[768]{0:T(1024)}, /*index=5*/f32[768]{0:T(1024)}) all-reduce(f32[768]{0:T(1024)S(1)} %get-tuple-element.20, f32[768]{0:T(1024)S(1)} %get-tuple-element.25, f32[768]{0:T(1024)S(1)} %copy-done.68, ...), channel_id=1, replica_groups=mesh['seq'=16,'tp'=2] {'seq','tp'}, use_global_device_ids=true, to_apply=%region_30.31 | all-reduce | flops 4608 | bytes 36864 | tf_op jit(solution)/shard_map/psum | solution.py:313
  1083.1 158.4 %all-reduce.5.cloned.1.call-done = (f32[768,384]{1,0:T(8,128)}, f32[768,384]{1,0:T(8,128)}, f32[768,192]{0,1:T(8,128)}, f32[384,768]{1,0:T(8,128)}, f32[768,1536]{1,0:T(8,128)}, /*index=5*/f32[1536,768]{1,0:T(8,128)}) async-done(((f32[768,384]{1,0:T(8,128)}, f32[768,384]{1,0:T(8,128)}, f32[768,192]{0,1:T(8,128)}, f32[384,768]{1,0:T(8,128)}, f32[768,1536]{1,0:T(8,128)}, /*index=5*/f32[1536,768]{1,0:T(8,128)}), ...) | async-done | bytes 13565968 | tf_op jit(solution)/shard_map/psum | solution.py:292
  (345 shorter events, 283.9 us)
Async XLA Ops:
  7.2 384.6 %copy-start = (bf16[768,1536]{1,0:T(8,128)(2,1)S(1)}, bf16[768,1536]{1,0:T(8,128)(2,1)}, u32[]{:S(2)}) copy-start(bf16[768,1536]{1,0:T(8,128)(2,1)} %param.35) | copy-start | bytes 7077892
  7.2 54.2 %all-gather.5.cloned.1.call-start = ((), (), s32[]{:S(2)}) async-start(), calls=%async_computation.4 | async-start | bytes 4718592 | tf_op jit(solution)/shard_map/all_gather | solution.py:129
  13.7 327.2 %reduce-scatter.5.cloned.1.call-start = ((), (), s32[]{:S(2)}) async-start(), calls=%async_computation.5 | async-start | bytes 4718592 | tf_op jit(solution)/shard_map/reduce_scatter | solution.py:181
  69.7 5.7 collective-permute-start
  79.1 137.9 %collective-permute-start.1 = (bf16[2,2,2048,384]{2,3,1,0:T(8,128)(2,1)}, bf16[2,2,2048,384]{2,3,1,0:T(8,128)(2,1)}, u32[]{:S(2)}, u32[]{:S(2)}) collective-permute-start(bf16[2,2,2048,384]{2,3,1,0:T(8,128)(2,1)} %pad_maximum_fusion), channel_id=1, source_target_pairs={{0,4},{4,0},{2,6},{6,2},{8,12},{12,8},{10,14},{14,10},{16,20},{20,... | collective-permute-start | bytes 18874376 | tf_op jit(solution)/shard_map/ppermute | solution.py:24
  96.0 134.4 %copy-start.8 = (bf16[48,8,8,256]{3,2,1,0:T(8,128)(2,1)}, bf16[48,8,8,256]{3,2,1,0:T(8,128)(2,1)S(1)}, u32[]{:S(2)}) copy-start(bf16[48,8,8,256]{3,2,1,0:T(8,128)(2,1)S(1)} %copy.217) | copy-start | bytes 4718596
  96.5 176.1 %copy-start.20 = (bf16[48,8,8,256]{3,2,1,0:T(8,128)(2,1)}, bf16[48,8,8,256]{3,2,1,0:T(8,128)(2,1)S(1)}, u32[]{:S(2)}) copy-start(bf16[48,8,8,256]{3,2,1,0:T(8,128)(2,1)S(1)} %copy.216) | copy-start | bytes 4718596
  103.3 160.1 %copy-start.28 = (bf16[48,8,8,256]{3,2,1,0:T(8,128)(2,1)}, bf16[48,8,8,256]{3,2,1,0:T(8,128)(2,1)S(1)}, u32[]{:S(2)}) copy-start(bf16[48,8,8,256]{3,2,1,0:T(8,128)(2,1)S(1)} %copy.222) | copy-start | bytes 4718596
  297.4 94.4 %all-gather.7.cloned.1.call-start = ((), (), s32[]{:S(2)}) async-start(), calls=%async_computation.6 | async-start | bytes 4718592 | tf_op jit(solution)/shard_map/all_gather | solution.py:190
  346.7 91.5 %all-gather.9.cloned.1.call-start = ((), (), s32[]{:S(2)}) async-start(), calls=%async_computation.8 | async-start | bytes 4718592 | tf_op jit(solution)/shard_map/all_gather | solution.py:203
  347.3 161.0 %reduce-scatter.9.cloned.1.call-start = ((), (), s32[]{:S(2)}) async-start(), calls=%async_computation.9 | async-start | bytes 4718592 | tf_op jit(solution)/shard_map/reduce_scatter | solution.py:209
  464.8 89.6 %reduce-scatter.7.cloned.1.call-start = ((), (), s32[]{:S(2)}) async-start(), calls=%async_computation.7 | async-start | bytes 4718592 | tf_op jit(solution)/shard_map/reduce_scatter | solution.py:194
  476.0 78.3 %copy-start.72 = (f32[768]{0:T(1024)S(1)}, f32[768]{0:T(1024)}, u32[]{:S(2)}) copy-start(f32[768]{0:T(1024)} %param.38) | copy-start | bytes 9220
  476.0 132.0 %all-gather.11.cloned.1.call-start = ((), (), s32[]{:S(2)}) async-start(), calls=%async_computation.10 | async-start | bytes 4718592 | tf_op jit(solution)/shard_map/all_gather | solution.py:219
  562.9 473.6 %reduce-scatter.11.cloned.1.call-start = ((), (), s32[]{:S(2)}) async-start(), calls=%async_computation.11 | async-start | bytes 4718592 | tf_op jit(solution)/shard_map/reduce_scatter | solution.py:276
  749.3 137.6 %collective-permute-start.2 = (bf16[2,2,8,256,6,64]{3,5,4,2,1,0:T(8,128)(2,1)}, bf16[2,2,8,256,6,64]{3,5,4,2,1,0:T(8,128)(2,1)}, u32[]{:S(2)}, u32[]{:S(2)}) collective-permute-start(bf16[2,2,8,256,6,64]{3,5,4,2,1,0:T(8,128)(2,1)} %pad_maximum_fusion.1), channel_id=1, source_target_pairs={{0,4},{4,0},{2,6},{6,2},{8,12},{12,8},{10,14},{14,10},{16,20},{20,... | collective-permute-start | bytes 18874376 | tf_op jit(solution)/shard_map/ppermute | solution.py:24
  779.5 123.8 %slice-start.8 = ((s8[6291456]{0:T(1024)(128)(4,1)}), s8[4194304]{0:T(1024)(128)(4,1)S(1)}, s32[]{:S(2)}) async-start(s8[6291456]{0:T(1024)(128)(4,1)} %bitcast.189), calls=%async_computation.21 | async-start | bytes 8388608
  779.5 124.9 %slice-start.12 = ((s8[6291456]{0:T(1024)(128)(4,1)}), s8[4194304]{0:T(1024)(128)(4,1)S(1)}, s32[]{:S(2)}) async-start(s8[6291456]{0:T(1024)(128)(4,1)} %bitcast.193), calls=%async_computation.25 | async-start | bytes 8388608
  782.4 120.9 %slice-start.9 = ((s8[6291456]{0:T(1024)(128)(4,1)}), s8[2097152]{0:T(1024)(128)(4,1)S(1)}, s32[]{:S(2)}) async-start(s8[6291456]{0:T(1024)(128)(4,1)} %bitcast.189), calls=%async_computation.22 | async-start | bytes 4194304
  782.4 122.0 %slice-start.13 = ((s8[6291456]{0:T(1024)(128)(4,1)}), s8[2097152]{0:T(1024)(128)(4,1)S(1)}, s32[]{:S(2)}) async-start(s8[6291456]{0:T(1024)(128)(4,1)} %bitcast.193), calls=%async_computation.26 | async-start | bytes 4194304
  903.3 15.1 %collective-permute-start.3 = (bf16[1,2,8,256,6,64]{3,5,4,2,1,0:T(8,128)(2,1)}, bf16[1,2,8,256,6,64]{3,5,4,2,1,0:T(8,128)(2,1)}, u32[]{:S(2)}, u32[]{:S(2)}) collective-permute-start(bf16[1,2,8,256,6,64]{3,5,4,2,1,0:T(8,128)(2,1)} %slice.79), channel_id=1, source_target_pairs={{0,2},{2,0},{4,6},{6,4},{8,10},{10,8},{12,14},{14,12},{16,18},{18,... | collective-permute-start | bytes 9437192 | tf_op jit(solution)/shard_map/ppermute | solution.py:24
  938.1 303.4 %all-reduce.5.cloned.1.call-start = ((), (), s32[]{:S(2)}) async-start(), calls=%async_computation.12 | async-start | bytes 27131904 | tf_op jit(solution)/shard_map/psum | solution.py:292
  969.1 70.3 %copy-start.68 = (f32[768]{0:T(1024)S(1)}, f32[768]{0:T(1024)}, u32[]{:S(2)}) copy-start(f32[768]{0:T(1024)} %get-tuple-element.57) | copy-start | bytes 9220
  969.1 70.3 %copy-start.69 = (f32[768]{0:T(1024)S(1)}, f32[768]{0:T(1024)}, u32[]{:S(2)}) copy-start(f32[768]{0:T(1024)} %get-tuple-element.68) | copy-start | bytes 9220
  (93 other events, 1316.2 us)
Sparse Core Ops, SparseCore 0:
  13.8 47.6 all-gather.4
  297.5 43.3 reduce-scatter.4
  346.8 44.9 all-gather.6
  393.3 44.9 all-gather.8
  464.9 43.3 reduce-scatter.8
  510.9 43.3 reduce-scatter.6
  563.0 44.9 all-gather.10
  938.2 43.3 reduce-scatter.10
  988.6 252.8 all-reduce.4
where the time goes:
time: 1260 us
  waiting for transfers between devices  664 us (53%)
  matrix products  269 us (21%)
  other arithmetic  145 us (12%)
  blocking collectives  104 us (8%)
  local copies, waits for them, and re-layouts  58.9 us (5%)
  between operations  15.3 us (1%)
    ppermute x4, waiting for transfers between devices, from_partner(): return lax.ppermute(block, axis, route)  217 us
    psum x1, waiting for transfers between devices, per_device(): lax.psum((grad_query_weight, grad_query_bias, grad_key_weight, grad_value...  158 us
    psum x1, blocking collectives, per_device(): lax.psum((grad_query_weight, grad_query_bias, grad_key_weight, grad_value...  64 us
    dot_general x4, matrix products, per_device(): jnp.einsum('bqhe,bkhe->bhqk', grad_heads, value_heads, preferred_element_...  56 us
    all_gather x1, waiting for transfers between devices, per_device(): lax.all_gather(first_norm.astype(jnp.bfloat16), 'tp', axis=0, tiled=True)  47.7 us
    all_gather x1, waiting for transfers between devices, per_device(): lax.all_gather(middle_grad.astype(jnp.bfloat16), 'tp', axis=0, tiled=True)  45 us
    all_gather x1, waiting for transfers between devices, per_device(): lax.all_gather(second_norm.astype(jnp.bfloat16), 'tp', axis=0, tiled=True)  44.5 us
    reduce_scatter x1, waiting for transfers between devices, per_device(): lax.psum_scatter(product(attended_rows, out_weight).astype(jnp.bfloat16),...  43.4 us
  transfers between devices with their start and end apart: 13, of which 11 were waited for; matrix products, arithmetic and copies ran while one was open for 11% of the time, Pallas kernels for 0%

commit v1 on v0

v1 whole, which is shorter than its diff:
```python
from functools import partial

import jax
import jax.numpy as jnp
from jax import lax
from jax.experimental import pallas as pl
from jax.experimental.pallas import tpu as pltpu
from jax.sharding import PartitionSpec as P

HEAD = 64
SEQ_LEN = 1024
BLOCK = 256
LONGEST = 512
SPAN = SEQ_LEN // BLOCK
REACH = -(-LONGEST // BLOCK) + 1
PAIR = 2 * HEAD
EPSILON = 1e-05
MASKED = -1e30
GELU_A = 0.7978845608028654
GELU_B = 0.044715
SCALE = HEAD ** (-0.5)
VMEM = 56 * 1024 * 1024

F32 = jnp.float32
BF16 = jnp.bfloat16


def nn(left, right):
    return lax.dot_general(left, right, (((1,), (0,)), ((), ())), preferred_element_type=F32)


def nt(left, right):
    return lax.dot_general(left, right, (((1,), (1,)), ((), ())), preferred_element_type=F32)


def tn(left, right):
    return lax.dot_general(left, right, (((0,), (0,)), ((), ())), preferred_element_type=F32)


def normed(rows):
    centred = rows - jnp.mean(rows, axis=-1, keepdims=True)
    inverse = lax.rsqrt(jnp.mean(centred * centred, axis=-1, keepdims=True) + EPSILON)
    return centred * inverse, inverse


def norm_back(grad_out, scaled, inverse, gain):
    grad_scaled = grad_out * gain
    first_mean = jnp.mean(grad_scaled, axis=-1, keepdims=True)
    second_mean = jnp.mean(grad_scaled * scaled, axis=-1, keepdims=True)
    return inverse * (grad_scaled - first_mean - scaled * second_mean)


def full(shape):
    return pl.BlockSpec(shape, lambda *_: (0,) * len(shape), pipeline_mode=pl.Buffered(1))


def placed(columns):
    return pl.BlockSpec((None, BLOCK, columns), lambda p, src, *_: (src[p], 0, 0))


def in_order(columns):
    return pl.BlockSpec((BLOCK, columns), lambda p, *_: (p, 0))


def by_block(columns):
    return pl.BlockSpec((None, BLOCK, columns), lambda p, *_: (p, 0, 0))


def shape_of(shape, dtype):
    return jax.ShapeDtypeStruct(shape, dtype)


def call(kernel, scalars, grid, ins, outs, out_shapes, scratch=(), flops=0, name=None):
    return pl.pallas_call(
        kernel,
        grid_spec=pltpu.PrefetchScalarGridSpec(
            num_scalar_prefetch=scalars,
            grid=grid,
            in_specs=ins,
            out_specs=outs,
            scratch_shapes=scratch,
        ),
        out_shape=out_shapes,
        compiler_params=pltpu.CompilerParams(
            dimension_semantics=("arbitrary",) * len(grid), vmem_limit_bytes=VMEM
        ),
        cost_estimate=pl.CostEstimate(flops=flops, bytes_accessed=flops // 400, transcendentals=0),
        name=name,
    )


def project_kernel(
    src, x_ref, skip_ref, own_ref, other_ref, bias_ref, gain_ref, shift_ref,
    norm_ref, q_ref, k_ref, v_ref,
):
    half = own_ref.shape[1] * 2 // 5
    fresh = half // 2
    scaled, _ = normed(x_ref[...].astype(F32))
    rows = (scaled * gain_ref[...] + shift_ref[...]).astype(BF16)
    norm_ref[...] = rows
    parts = []
    for side, weight in enumerate((own_ref, other_ref)):
        made = (nn(rows, weight[...]) + bias_ref[side:side + 1, :]).astype(BF16)
        columns = slice(side * half, (side + 1) * half)
        q_ref[:, columns] = made[:, :half]
        k_ref[:, columns] = made[:, half:2 * half]
        parts.append(made[:, 2 * half:])
        parts.append(skip_ref[:, side * fresh:(side + 1) * fresh])
    v_ref[...] = jnp.concatenate(parts, axis=1)


def doc_start(position, bounds, bound_count):
    start = jnp.zeros_like(position)
    for index in range(bound_count):
        start = jnp.where(position >= bounds[index], bounds[index], start)
    return start


def attend_kernel(
    bound_count, src, bounds, x_ref, q_ref, k_ref, v_ref, own_ref, other_ref, bias_ref,
    gain_ref, shift_ref, att_ref, lse_ref, middle_ref, norm_ref, att_s, lse_s,
):
    p = pl.program_id(0)
    width = q_ref.shape[1]
    half = width // 2
    first = doc_start(p * BLOCK, bounds, bound_count)
    needed = p - first // BLOCK + 1
    lane = lax.broadcasted_iota(jnp.int32, (1, PAIR), 1)
    low = lane < HEAD
    picks = [jnp.where(low, SCALE, 0.0).astype(BF16), jnp.where(low, 0.0, SCALE).astype(BF16)]

    def run(count):
        span = count * BLOCK
        base = pl.multiple_of((p - count + 1) * BLOCK, BLOCK)
        row = p * BLOCK + lax.broadcasted_iota(jnp.int32, (BLOCK, 1), 0)
        start = doc_start(row, bounds, bound_count)
        column = base + lax.broadcasted_iota(jnp.int32, (1, span), 1)
        seen = (column <= row) & (column >= start)
        bias = jnp.where(seen, 0.0, MASKED)
        head_lane = lax.broadcasted_iota(jnp.int32, (1, 128), 1)

        @pl.loop(0, width // PAIR)
        def _(pair):
            lanes = pl.ds(pl.multiple_of(pair * PAIR, PAIR), PAIR)
            queries = q_ref[:, lanes]
            keys = k_ref[pl.ds(base, span), lanes]
            values = v_ref[pl.ds(base, span), lanes]
            outs = []
            for side in range(2):
                scores = nt(queries * picks[side], keys) + bias
                top = jnp.max(scores, axis=1, keepdims=True)
                probs = jnp.exp(scores - top)
                total = jnp.sum(probs, axis=1, keepdims=True)
                outs.append(nn(probs.astype(BF16), values) / total)
                lse_s[...] = jnp.where(
                    head_lane == 2 * pair + side, top + jnp.log(total), lse_s[...]
                )
            att_s[:, lanes] = jnp.where(low, outs[0], outs[1]).astype(BF16)

    for count in range(1, REACH + 1):
        pl.when(needed == count)(partial(run, count))

    lse_ref[...] = lse_s[...].T[:lse_ref.shape[0], :]
    attended = att_s[...]
    att_ref[...] = attended
    middle = (
        x_ref[...].astype(F32)
        + (nn(attended[:, :half], own_ref[...]) + nn(attended[:, half:], other_ref[...]))
        + bias_ref[...]
    )
    middle_ref[...] = middle
    scaled, _ = normed(middle)
    norm_ref[...] = (scaled * gain_ref[...] + shift_ref[...]).astype(BF16)


def feed_kernel(
    first_call, core, *refs
):
    if first_call:
        (norm_ref, grad_ref, up_ref, down_ref, bias_ref,
         out_ref, back_ref, ku_ref, su_ref, kd_ref, sd_ref, gb_ref) = refs
    else:
        (norm_ref, grad_ref, ua_ref, ub_ref, da_ref, db_ref, bias_ref, out_in, back_in,
         out_ref, back_ref, ku_ref, su_ref, kd_ref, sd_ref, gb_ref) = refs
    j = pl.program_id(0)
    near = j < pl.num_programs(0) // 2

    @pl.when(j == 0)
    def _():
        if first_call:
            out_ref[...] = jnp.zeros_like(out_ref)
            back_ref[...] = jnp.zeros_like(back_ref)
        else:
            out_ref[...] = out_in[...]
            back_ref[...] = back_in[...]

    if first_call:
        up = up_ref[...]
        down = down_ref[...]
    else:
        up = jnp.where(near, ua_ref[...], ub_ref[...])
        down = jnp.where(near, da_ref[...], db_ref[...])
    rows = norm_ref[...]
    grads = grad_ref[...]
    hidden = nn(rows, up) + bias_ref[...]
    square = hidden * hidden
    curve = jnp.tanh(GELU_A * hidden * (1.0 + GELU_B * square))
    plus = 0.5 * (1.0 + curve)
    active = (hidden * plus).astype(BF16)
    slope = plus + (hidden * plus) * (1.0 - curve) * (GELU_A + 3.0 * GELU_A * GELU_B * square)
    hidden_grad = nt(grads, down) * slope
    gb_ref[...] = jnp.sum(hidden_grad, axis=0, keepdims=True)
    hidden_low = hidden_grad.astype(BF16)
    out_ref[...] += nn(active, down)
    back_ref[...] += nt(hidden_low, up)
    down_grad = tn(active, grads).astype(BF16)
    up_grad = tn(rows, hidden_low).astype(BF16)

    @pl.when(near)
    def _():
        ku_ref[...] = up_grad
        kd_ref[...] = down_grad

    @pl.when(jnp.logical_not(near))
    def _():
        su_ref[...] = up_grad
        sd_ref[...] = down_grad


def feed(first_call, core, rows, grads, weights, bias, carried, chunk):
    tokens, width = rows.shape
    units = bias.shape[1]
    steps = units // chunk
    part = steps // 2
    turn = lambda j, core: lax.rem(j + core[0] * part, steps)
    near = lambda j: jnp.minimum(j, part - 1)
    far = lambda j: jnp.maximum(j - part, 0)
    up_near = pl.BlockSpec((width, chunk), lambda j, core: (0, near(j)))
    up_far = pl.BlockSpec((width, chunk), lambda j, core: (0, far(j)))
    down_near = pl.BlockSpec((chunk, width), lambda j, core: (near(j), 0))
    down_far = pl.BlockSpec((chunk, width), lambda j, core: (far(j), 0))
    if first_call:
        weight_specs = [
            pl.BlockSpec((width, chunk), lambda j, core: (0, turn(j, core))),
            pl.BlockSpec((chunk, width), lambda j, core: (turn(j, core), 0)),
        ]
    else:
        weight_specs = [up_near, up_far, down_near, down_far]
    bias_spec = pl.BlockSpec((1, chunk), lambda j, core: (0, turn(j, core)))
    total = full((tokens, width))
    return call(
        partial(feed_kernel, first_call),
        1,
        (steps,),
        [total, total] + weight_specs + [bias_spec] + [total] * len(carried),
        [total, total, up_near, up_far, down_near, down_far, bias_spec],
        [
            shape_of((tokens, width), F32),
            shape_of((tokens, width), F32),
            shape_of((width, units // 2), BF16),
            shape_of((width, units // 2), BF16),
            shape_of((units // 2, width), BF16),
            shape_of((units // 2, width), BF16),
            shape_of((1, units), F32),
        ],
        flops=12 * tokens * width * units,
        name="feed_own" if first_call else "feed_other",
    )(core, rows, grads, *weights, bias, *carried)


def residual_kernel(
    core, out_ref, back_ref, grad_ref, middle_ref, att_ref, own_ref, other_ref, gain_ref,
    down_bias_ref, layer_ref, mg_ref, ga_ref, keep_ref, send_ref, small_ref, acc_s,
):
    p = pl.program_id(0)
    half = own_ref.shape[0]
    middle = middle_ref[...]
    layer_ref[...] = (middle + out_ref[...] + down_bias_ref[...]).astype(BF16)
    scaled, inverse = normed(middle)
    second = back_ref[...]
    out_grad = grad_ref[...].astype(F32)
    middle_grad = out_grad + norm_back(second, scaled, inverse, gain_ref[...])
    mg_ref[...] = middle_grad
    low = middle_grad.astype(BF16)
    ga_ref[:, :half] = nt(low, own_ref[...]).astype(BF16)
    ga_ref[:, half:] = nt(low, other_ref[...]).astype(BF16)
    weight_grad = tn(att_ref[...], low)
    sums = jnp.concatenate(
        [
            jnp.sum(value, axis=0, keepdims=True)
            for value in (second * scaled, second, middle_grad, out_grad)
        ],
        axis=0,
    )

    @pl.when(p == 0)
    def _():
        acc_s[...] = weight_grad
        small_ref[...] = sums

    @pl.when(p > 0)
    def _():
        acc_s[...] += weight_grad
        small_ref[...] += sums

    @pl.when(p == pl.num_programs(0) - 1)
    def _():
        rows = half // 2
        near = pl.multiple_of(core[0] * rows, 32)
        far = pl.multiple_of(rows - core[0] * rows, 32)
        for side in range(2):
            keep_ref[side] = acc_s[pl.ds(side * half + near, rows), :].astype(BF16)
            send_ref[side] = acc_s[pl.ds(side * half + far, rows), :].astype(BF16)


def attend_back_kernel(
    bound_count, src, bounds, q_ref, k_ref, v_ref, att_ref, ga_ref, lse_ref,
    own_ref, other_ref, skip_ref, dq_s, dk_s, dv_s, delta_s,
):
    p = pl.program_id(0)
    width = q_ref.shape[1]
    half = width // 2
    fresh = half // 2
    place = src[p]
    first = doc_start(p * BLOCK, bounds, bound_count)
    needed = p - first // BLOCK + 1
    low = lax.broadcasted_iota(jnp.int32, (1, PAIR), 1) < HEAD
    picks = [jnp.where(low, SCALE, 0.0).astype(BF16), jnp.where(low, 0.0, SCALE).astype(BF16)]
    ones = [jnp.where(low, 1.0, 0.0).astype(BF16), jnp.where(low, 0.0, 1.0).astype(BF16)]

    @pl.when(p == 0)
    def _():
        dk_s[...] = jnp.zeros_like(dk_s)
        dv_s[...] = jnp.zeros_like(dv_s)

    product = ga_ref[...].astype(F32) * att_ref[...].astype(F32)
    high = product.astype(BF16)
    rest = (product - high.astype(F32)).astype(BF16)
    owner = lax.broadcasted_iota(jnp.int32, (delta_s.shape[0], width), 1) // HEAD
    which = lax.broadcasted_iota(jnp.int32, (delta_s.shape[0], width), 0)
    gather = (owner == which).astype(F32).astype(BF16)
    delta_s[...] = nt(gather, high) + nt(gather, rest)

    def run(count):
        span = count * BLOCK
        base = pl.multiple_of((p - count + 1) * BLOCK, BLOCK)
        row = p * BLOCK + lax.broadcasted_iota(jnp.int32, (1, BLOCK), 1)
        start = doc_start(row, bounds, bound_count)
        column = base + lax.broadcasted_iota(jnp.int32, (span, 1), 0)
        seen = (column <= row) & (column >= start)
        bias = jnp.where(seen, 0.0, MASKED)

        @pl.loop(0, width // PAIR)
        def _(pair):
            lanes = pl.ds(pl.multiple_of(pair * PAIR, PAIR), PAIR)
            queries = q_ref[:, lanes]
            grads = ga_ref[:, lanes]
            keys = k_ref[pl.ds(base, span), lanes]
            values = v_ref[pl.ds(base, span), lanes]
            query_parts = []
            for side in range(2):
                head = 2 * pair + side
                picked = queries * picks[side]
                chosen = grads * ones[side]
                scores = nt(keys, picked) + bias
                probs = jnp.exp(scores - lse_ref[pl.ds(head, 1), :])
                dprobs = nt(values, chosen)
                dscores = (probs * (dprobs - delta_s[pl.ds(head, 1), :])).astype(BF16)
                value_part = nn(probs.astype(BF16), chosen)
                key_part = nn(dscores, picked)
                query_parts.append(tn(dscores, keys))
                if side == 0:
                    value_sum, key_sum = value_part, key_part
                else:
                    value_sum, key_sum = value_sum + value_part, key_sum + key_part
            dv_s[pl.ds(base, span), lanes] += value_sum
            dk_s[pl.ds(base, span), lanes] += key_sum
            dq_s[:, lanes] = (
                jnp.where(low, query_parts[0], query_parts[1]) * SCALE
            ).astype(BF16)

    for count in range(1, REACH + 1):
        pl.when(needed == count)(partial(run, count))

    own_ref[place, :, :half] = dq_s[:, :half]
    other_ref[place, :, :half] = dq_s[:, half:]

    @pl.when(p == pl.num_programs(0) - 1)
    def _():
        for block in range(SPAN):
            rows = slice(block * BLOCK, (block + 1) * BLOCK)
            to = src[block]
            value_grad = dv_s[rows, :]
            own_ref[to, :, half:2 * half] = dk_s[rows, :half].astype(BF16)
            other_ref[to, :, half:2 * half] = dk_s[rows, half:].astype(BF16)
            own_ref[to, :, 2 * half:] = value_grad[:, :fresh].astype(BF16)
            other_ref[to, :, 2 * half:] = value_grad[:, half:half + fresh].astype(BF16)
            skip_ref[to] = jnp.concatenate(
                [value_grad[:, fresh:half], value_grad[:, half + fresh:]], axis=1
            ).astype(BF16)


def weight_kernel(core, norm_ref, own_ref, other_ref, keep_ref, send_ref, sums_ref, made_s):
    rows = norm_ref[...]
    half = made_s.shape[0] // 2
    near = pl.multiple_of(core[0] * half, 128)
    far = pl.multiple_of(half - core[0] * half, 128)
    for side, grads_ref in enumerate((own_ref, other_ref)):
        grads = grads_ref[...]
        made_s[...] = tn(rows, grads)
        keep_ref[side] = made_s[pl.ds(near, half), :].astype(BF16)
        send_ref[side] = made_s[pl.ds(far, half), :].astype(BF16)
        sums_ref[side:side + 1, :] = jnp.sum(grads.astype(F32), axis=0, keepdims=True)


def input_kernel(
    own_ref, other_ref, w_own_ref, w_other_ref, x_ref, mg_ref, gain_ref, grad_ref, small_ref
):
    p = pl.program_id(0)
    first = nt(own_ref[...], w_own_ref[...]) + nt(other_ref[...], w_other_ref[...])
    scaled, inverse = normed(x_ref[...].astype(F32))
    grad_ref[...] = (mg_ref[...] + norm_back(first, scaled, inverse, gain_ref[...])).astype(BF16)
    sums = jnp.concatenate(
        [jnp.sum(value, axis=0, keepdims=True) for value in (first * scaled, first)], axis=0
    )

    @pl.when(p == 0)
    def _():
        small_ref[...] = sums

    @pl.when(p > 0)
    def _():
        small_ref[...] += sums


def per_device(
    sizes,
    layer_in,
    skip_values,
    block_slot,
    doc_lengths,
    gain_attention,
    shift_attention,
    query_weight,
    query_bias,
    key_weight,
    value_weight,
    value_bias,
    out_weight,
    out_bias,
    gain_feed,
    shift_feed,
    up_weight,
    up_bias,
    down_weight,
    down_bias,
    out_grad,
):
    seq_count, tp_count = sizes
    width = layer_in.shape[1]
    half = query_weight.shape[1]
    fresh = value_weight.shape[1]
    units = up_weight.shape[1]
    tokens = layer_in.shape[0]
    batch = skip_values.shape[0] // BLOCK
    seq_index = lax.axis_index("seq")
    tp_index = lax.axis_index("tp")
    member = seq_index % SPAN
    group = seq_index // SPAN
    core = seq_index % 2
    core_scalar = core.reshape(1).astype(jnp.int32)
    members = [[g * SPAN + m for m in range(SPAN)] for g in range(seq_count // SPAN)]
    same_core = [list(range(c, seq_count, 2)) for c in range(2)]
    pieces = seq_count // 2
    local_seq = tp_index * (batch // tp_count) + member

    def swap_core(value):
        return lax.ppermute(value, "seq", [(i, i ^ 1) for i in range(seq_count)])

    def swap_tp(value):
        return lax.ppermute(value, "tp", [(i, i ^ 1) for i in range(tp_count)])

    def to_seqs(value):
        return lax.all_to_all(value, "seq", 0, 0, tiled=True, axis_index_groups=members)

    def in_core_order(mine, theirs, axis):
        return jnp.where(
            core == 0,
            jnp.concatenate([mine, theirs], axis=axis),
            jnp.concatenate([theirs, mine], axis=axis),
        )

    slots = lax.dynamic_slice(block_slot, (group * SPAN, local_seq), (SPAN, 1))[:, 0]
    source = jnp.argsort(slots).astype(jnp.int32)
    lengths = lax.dynamic_index_in_dim(doc_lengths, group * batch + local_seq, 0, keepdims=False)
    bounds = jnp.cumsum(lengths)[:-1].astype(jnp.int32)
    bound_count = bounds.shape[0]

    qkv_own = jnp.concatenate([query_weight, key_weight, value_weight], axis=1)
    qkv_sent = lax.dynamic_slice_in_dim(qkv_own, core * (width // 2), width // 2, 0)
    qkv_near = swap_tp(qkv_sent)
    blocks_in = to_seqs(layer_in.reshape(SPAN, BLOCK, width))
    row_bias = lambda value: value.reshape(1, -1)
    bias_own = jnp.concatenate(
        [query_bias, jnp.zeros((half,), F32), value_bias, up_bias]
    ).reshape(1, -1)
    bias_other = swap_tp(bias_own)
    skip_split = skip_values.reshape(tp_count, batch // tp_count, BLOCK, fresh)
    skip_mine = lax.dynamic_index_in_dim(skip_split, tp_index, 0, keepdims=False)
    skip_theirs = lax.dynamic_index_in_dim(skip_split, 1 - tp_index, 0, keepdims=False)
    skip_theirs = swap_tp(skip_theirs)
    skip_blocks = to_seqs(jnp.concatenate([skip_mine, skip_theirs], axis=2))
    qkv_far = swap_core(qkv_near)
    qkv_other = in_core_order(qkv_near, qkv_far, 0)

    out_near = swap_tp(lax.dynamic_slice_in_dim(out_weight, core * (half // 2), half // 2, 0))
    out_other = in_core_order(out_near, swap_core(out_near), 0)
    up_near = swap_tp(lax.dynamic_slice_in_dim(up_weight, core * (units // 2), units // 2, 1))
    down_near = swap_tp(lax.dynamic_slice_in_dim(down_weight, core * (units // 2), units // 2, 0))
    up_far = swap_core(up_near)
    down_far = swap_core(down_near)
    grad_blocks = to_seqs(out_grad.reshape(SPAN, BLOCK, width))

    gain_one, shift_one = row_bias(gain_attention), row_bias(shift_attention)
    gain_two, shift_two = row_bias(gain_feed), row_bias(shift_feed)
    columns = qkv_own.shape[1]
    qkv_bias = jnp.concatenate([bias_own[:, :columns], bias_other[:, :columns]], axis=0)
    own_shape = (SPAN, BLOCK, width)

    norm_one, queries, keys, values = call(
        project_kernel,
        1,
        (SPAN,),
        [
            placed(width), placed(2 * fresh), full((width, columns)), full((width, columns)),
            full((2, columns)), full((1, width)), full((1, width)),
        ],
        [placed(width), in_order(width), in_order(width), in_order(width)],
        [shape_of(own_shape, BF16)] + [shape_of((tokens, width), BF16)] * 3,
        flops=4 * tokens * width * columns,
        name="project",
    )(source, blocks_in, skip_blocks, qkv_own, qkv_other, qkv_bias, gain_one, shift_one)

    heads = width // HEAD
    head_rows = -(-heads // 8) * 8
    lse_spec = pl.BlockSpec((head_rows, BLOCK), lambda p, *_: (0, p))
    attended, log_total, middle, norm_two = call(
        partial(attend_kernel, bound_count),
        2,
        (SPAN,),
        [
            placed(width), in_order(width), full((tokens, width)), full((tokens, width)),
            full((half, width)), full((half, width)), full((1, width)), full((1, width)),
            full((1, width)),
        ],
        [placed(width), lse_spec, placed(width), placed(width)],
        [
            shape_of(own_shape, BF16), shape_of((head_rows, tokens), F32),
            shape_of(own_shape, F32), shape_of(own_shape, BF16),
        ],
        scratch=[pltpu.VMEM((BLOCK, width), BF16), pltpu.VMEM((BLOCK, 128), F32)],
        flops=8 * tokens * BLOCK * width * 2,
        name="attend",
    )(
        source, bounds, blocks_in, queries, keys, values, out_weight, out_other,
        row_bias(out_bias), gain_two, shift_two,
    )

    rows_two = norm_two.reshape(tokens, width)
    grad_rows = grad_blocks.reshape(tokens, width)
    chunk = 256
    own = feed(
        True, core_scalar, rows_two, grad_rows, (up_weight, down_weight),
        bias_own[:, columns:], (), chunk,
    )
    other = feed(
        False, core_scalar, rows_two, grad_rows, (up_near, up_far, down_near, down_far),
        bias_other[:, columns:], own[:2], chunk,
    )
    feed_out, second_grad = other[:2]

    def reduced(own_keep, own_send, other_keep, other_send):
        mine = own_keep.astype(F32) + swap_core(own_send).astype(F32)
        given = (other_keep.astype(F32) + swap_core(other_send).astype(F32)).astype(BF16)
        return (mine + swap_tp(given).astype(F32)).astype(BF16)

    def across(value):
        rows = value.shape[0]
        split = value.reshape(pieces, rows // pieces, value.shape[1])
        parts = lax.all_to_all(split, "seq", 0, 0, tiled=True, axis_index_groups=same_core)
        piece = jnp.sum(parts.astype(F32), axis=0, keepdims=True).astype(BF16)
        spread = jnp.broadcast_to(piece, split.shape)
        whole = lax.all_to_all(spread, "seq", 0, 0, tiled=True, axis_index_groups=same_core)
        return whole.reshape(value.shape)

    def finished(value, axis):
        return in_core_order(value, swap_core(value), axis).astype(F32)

    grad_up_weight = finished(across(reduced(own[2], own[3], other[2], other[3])), 1)
    grad_down_weight = finished(across(reduced(own[4], own[5], other[4], other[5])), 0)

    layer_blocks, middle_grad, att_grad, out_keep, out_send, small_two = call(
        residual_kernel,
        1,
        (SPAN,),
        [
            in_order(width), in_order(width), in_order(width), by_block(width), by_block(width),
            full((half, width)), full((half, width)), full((1, width)), full((1, width)),
        ],
        [
            by_block(width), by_block(width), by_block(width),
            full((2, half // 2, width)), full((2, half // 2, width)), full((4, width)),
        ],
        [
            shape_of(own_shape, BF16), shape_of(own_shape, F32), shape_of(own_shape, BF16),
            shape_of((2, half // 2, width), BF16), shape_of((2, half // 2, width), BF16),
            shape_of((4, width), F32),
        ],
        scratch=[pltpu.VMEM((width, width), F32)],
        flops=4 * tokens * width * width,
        name="residual",
    )(
        core_scalar, feed_out, second_grad, grad_rows, middle, attended, out_weight, out_other,
        gain_two, row_bias(down_bias),
    )
    layer_out = to_seqs(layer_blocks).reshape(tokens, width)

    grads_own, grads_other, grads_skip = call(
        partial(attend_back_kernel, bound_count),
        2,
        (SPAN,),
        [
            in_order(width), full((tokens, width)), full((tokens, width)), placed(width),
            placed(width), lse_spec,
        ],
        [
            full((SPAN, BLOCK, columns)), full((SPAN, BLOCK, columns)),
            full((SPAN, BLOCK, 2 * fresh)),
        ],
        [
            shape_of((SPAN, BLOCK, columns), BF16), shape_of((SPAN, BLOCK, columns), BF16),
            shape_of((SPAN, BLOCK, 2 * fresh), BF16),
        ],
        scratch=[
            pltpu.VMEM((BLOCK, width), BF16), pltpu.VMEM((tokens, width), F32),
            pltpu.VMEM((tokens, width), F32), pltpu.VMEM((head_rows, BLOCK), F32),
        ],
        flops=20 * tokens * BLOCK * width * 2,
        name="attend_back",
    )(source, bounds, queries, keys, values, attended, att_grad, log_total)

    qkv_keep, qkv_send, qkv_sums = call(
        weight_kernel,
        1,
        (1,),
        [full((tokens, width)), full((tokens, columns)), full((tokens, columns))],
        [
            full((2, width // 2, columns)), full((2, width // 2, columns)), full((2, columns)),
        ],
        [
            shape_of((2, width // 2, columns), BF16), shape_of((2, width // 2, columns), BF16),
            shape_of((2, columns), F32),
        ],
        scratch=[pltpu.VMEM((width, columns), F32)],
        flops=4 * tokens * width * columns,
        name="weights",
    )(
        core_scalar, norm_one.reshape(tokens, width), grads_own.reshape(tokens, columns),
        grads_other.reshape(tokens, columns),
    )

    input_blocks, small_one = call(
        input_kernel,
        0,
        (SPAN,),
        [
            by_block(columns), by_block(columns), full((width, columns)), full((width, columns)),
            by_block(width), by_block(width), full((1, width)),
        ],
        [by_block(width), full((2, width))],
        [shape_of(own_shape, BF16), shape_of((2, width), F32)],
        flops=4 * tokens * width * columns,
        name="input",
    )(grads_own, grads_other, qkv_own, qkv_other, blocks_in, middle_grad, gain_one)
    input_grad = to_seqs(input_blocks).reshape(tokens, width).astype(F32)

    skip_back = to_seqs(grads_skip)
    skip_other = swap_tp(skip_back[:, :, fresh:])
    skip_own = skip_back[:, :, :fresh]
    skip_grad = jnp.where(
        tp_index == 0,
        jnp.concatenate([skip_own, skip_other], axis=0),
        jnp.concatenate([skip_other, skip_own], axis=0),
    ).reshape(batch * BLOCK, fresh).astype(F32)

    def reduced_pair(keep, send):
        both = keep.astype(F32) + swap_core(send).astype(F32)
        return (both[0] + swap_tp(both[1].astype(BF16)).astype(F32)).astype(BF16)

    grad_out_weight = finished(across(reduced_pair(out_keep, out_send)), 0)
    grad_qkv = finished(across(reduced_pair(qkv_keep, qkv_send)), 0)

    shared = jnp.concatenate([small_one.reshape(-1), small_two.reshape(-1)])
    split_own = jnp.concatenate([qkv_sums[0], own[6].reshape(-1)])
    split_other = jnp.concatenate([qkv_sums[1], other[6].reshape(-1)])
    vectors = jnp.concatenate([shared, split_own]) + swap_tp(
        jnp.concatenate([shared, split_other])
    )
    distance = 1
    while distance < seq_count:
        vectors = vectors + lax.ppermute(
            vectors, "seq", [(i, i ^ distance) for i in range(seq_count)]
        )
        distance *= 2
    shared = vectors[:6 * width].reshape(6, width)
    split = vectors[6 * width:]

    return (
        layer_out,
        input_grad,
        skip_grad,
        shared[0],
        shared[1],
        grad_qkv[:, :half],
        split[:half],
        grad_qkv[:, half:2 * half],
        grad_qkv[:, 2 * half:],
        split[2 * half:columns],
        grad_out_weight,
        shared[4],
        shared[2],
        shared[3],
        grad_up_weight,
        split[columns:],
        grad_down_weight,
        shared[5],
    )


def solution(mesh):
    return jax.shard_map(
        partial(per_device, (mesh.shape["seq"], mesh.shape["tp"])),
        mesh=mesh,
        in_specs=(
            P(("seq", "tp"), None),
            P("seq", "tp"),
            P(),
            P(),
            P(),
            P(),
            P(None, "tp"),
            P("tp"),
            P(None, "tp"),
            P(None, "tp"),
            P("tp"),
            P("tp", None),
            P(),
            P(),
            P(),
            P(None, "tp"),
            P("tp"),
            P("tp", None),
            P(),
            P(("seq", "tp"), None),
        ),
        out_specs=(
            P(("seq", "tp"), None),
            P(("seq", "tp"), None),
            P("seq", "tp"),
            P(),
            P(),
            P(None, "tp"),
            P("tp"),
            P(None, "tp"),
            P(None, "tp"),
            P("tp"),
            P("tp", None),
            P(),
            P(),
            P(),
            P(None, "tp"),
            P("tp"),
            P("tp", None),
            P(),
        ),
        check_vma=False,
    )
```

time: 1260 us -> 602 us (0.48)
  waiting for transfers between devices: 664 us -> 258 us
  matrix products: 269 us -> 0 us
  Pallas kernels: 0 us -> 148 us
  blocking collectives: 104 us -> 0 us
  other arithmetic: 145 us -> 42.5 us
  starting transfers between devices: 3.3 us -> 96 us
  between operations: 15.3 us -> 1.56 us
    dot_general x42 -> x0, matrix products: 269 us -> none  [the longest x4 56 us: per_device(): jnp.einsum('bqhe,bkhe->bhqk', grad_heads, value_heads, preferred_element_...]
    all_gather x4 -> x0, waiting for transfers between devices: 170 us -> none  [the longest x1 47.7 us: per_device(): lax.all_gather(first_norm.astype(jnp.bfloat16), 'tp', axis=0, tiled=True)]
    psum x1 -> x0, waiting for transfers between devices: 158 us -> none  [per_device(): lax.psum((grad_query_weight, grad_query_bias, grad_key_weight, grad_value...]
    pallas_call x0 -> x8, Pallas kernels: none -> 148 us  [the longest x2 53.1 us: feed(): call(partial(feed_kernel, first_call), 1, (steps,), [total, total] + weig...]
    reduce_scatter x4 -> x0, waiting for transfers between devices: 118 us -> none  [the longest x1 43.4 us: per_device(): lax.psum_scatter(product(attended_rows, out_weight).astype(jnp.bfloat16),...]
    all_to_all x0 -> x14, waiting for transfers between devices: none -> 112 us  [the longest x4 48.1 us: across(): lax.all_to_all(spread, 'seq', 0, 0, tiled=True, axis_index_groups=same_core)]
    psum x2 -> x0, blocking collectives: 104 us -> none  [the longest x1 64 us: per_device(): lax.psum((grad_query_weight, grad_query_bias, grad_key_weight, grad_value...]
    ppermute x4 -> x30, waiting for transfers between devices: 217 us -> 146 us  [the longest x12 139 us: swap_tp(): return lax.ppermute(value, 'tp', [(i, i ^ 1) for i in range(tp_count)])]
  transfers between devices with their start and end apart: 13 -> 44, of which waited for: 11 -> 21; matrix products, arithmetic and copies ran while one was open for 11% -> 13% of each run, Pallas kernels for 0% -> 18%
where the time goes in v1:
time: 602 us; the launch traced here: 597 us
  waiting for transfers between devices  258 us (43%)
  Pallas kernels  148 us (25%)
  starting transfers between devices  96 us (16%)
  local copies, waits for them, and re-layouts  50.8 us (8%)
  other arithmetic  42.5 us (7%)
    ppermute x12, waiting for transfers between devices, swap_tp(): return lax.ppermute(value, 'tp', [(i, i ^ 1) for i in range(tp_count)])  139 us
    pallas_call x2, Pallas kernels, feed(): call(partial(feed_kernel, first_call), 1, (steps,), [total, total] + weig...  53.1 us
    all_to_all x4, waiting for transfers between devices, across(): lax.all_to_all(spread, 'seq', 0, 0, tiled=True, axis_index_groups=same_core)  48.1 us
    all_to_all x6, waiting for transfers between devices, to_seqs(): lax.all_to_all(value, 'seq', 0, 0, tiled=True, axis_index_groups=members)  34.2 us
    pallas_call x1, Pallas kernels, per_device(): call(partial(attend_back_kernel, bound_count), 2, (SPAN,), [in_order(widt...  31.5 us
    all_to_all x4, waiting for transfers between devices, across(): lax.all_to_all(split, 'seq', 0, 0, tiled=True, axis_index_groups=same_core)  29.3 us
    pallas_call x1, Pallas kernels, per_device(): call(partial(attend_kernel, bound_count), 2, (SPAN,), [placed(width), in_...  25.7 us
    all_to_all x6, starting transfers between devices, to_seqs(): lax.all_to_all(value, 'seq', 0, 0, tiled=True, axis_index_groups=members)  23.4 us
  transfers between devices with their start and end apart: 44, of which 21 were waited for; matrix products, arithmetic and copies ran while one was open for 13% of the time, Pallas kernels for 18%

profile of v1, /device:TPU:0, one launch (start us, length us, event | category | flops | bytes accessed | tf_op | source)
XLA Modules:
  0.0 597.1 jit_solution(18073469673847470811)
XLA Ops:
  5.2 11.9 %collective-permute-done = bf16[4,256,192]{2,1,0:T(8,128)(2,1)S(1)} collective-permute-done((bf16[4,256,192]{2,1,0:T(8,128)(2,1)S(1)}, bf16[4,256,192]{2,1,0:T(8,128)(2,1)S(1)}, u32[]{:S(2)}, u32[]{:S(2)}) %collective-permute-start) | collective-permute-done | bytes 393248 | tf_op jit(solution)/shard_map/ppermute | solution.py:481
  22.0 11.4 %all-to-all-done.1.skip_ref = bf16[4,256,384]{2,1,0:T(8,128)(2,1)S(1)} async-done(((bf16[4,256,384]{2,1,0:T(8,128)(2,1)}), bf16[4,256,384]{2,1,0:T(8,128)(2,1)S(1)}, u32[]{:S(2)}, u32[]{:S(2)}) %all-to-all-start.1) | async-done | bytes 786464 | tf_op jit(solution)/shard_map/all_to_all | solution.py:484
  50.5 11.8 %collective-permute-done.1 = bf16[384,960]{0,1:T(8,128)(2,1)} collective-permute-done((bf16[384,960]{0,1:T(8,128)(2,1)}, bf16[384,960]{0,1:T(8,128)(2,1)}, u32[]{:S(2)}, u32[]{:S(2)}) %collective-permute-start.1) | collective-permute-done | bytes 737312 | tf_op jit(solution)/shard_map/ppermute | solution.py:481
  64.6 54.2 %collective-permute-done.4 = bf16[192,768]{1,0:T(8,128)(2,1)S(1)} collective-permute-done((bf16[192,768]{1,0:T(8,128)(2,1)S(1)}, bf16[192,768]{1,0:T(8,128)(2,1)S(1)}, u32[]{:S(2)}, u32[]{:S(2)}) %collective-permute-start.4) | collective-permute-done | bytes 294944 | tf_op jit(solution)/shard_map/ppermute | solution.py:481
  138.2 9.2 %project.1 = (bf16[4,256,768]{2,1,0:T(8,128)(2,1)}, bf16[1024,768]{1,0:T(8,128)(2,1)}, bf16[1024,768]{1,0:T(8,128)(2,1)}, bf16[1024,768]{1,0:T(8,128)(2,1)}) custom-call(s32[4]{0:T(128)} %get-tuple-element.55.src, bf16[4,256,768]{2,1,0:T(8,128)(2,1)} %copy-done.4, bf16[4,256,384]{2,1,0:T(8,128)(2,1)} %copy-done.12, bf16[768,960]{1,0:T(8,128)(2,1)} %copy-done.2, ...), custom_call_target="tpu_custom_call" | custom-call | flops 3019898880 | bytes 7549747 | tf_op jit(solution)/shard_map/project/pallas_call | solution.py:530
  147.4 25.7 %attend.1 = (bf16[4,256,768]{2,1,0:T(8,128)(2,1)}, f32[16,1024]{1,0:T(8,128)}, f32[4,256,768]{2,1,0:T(8,128)}, bf16[4,256,768]{2,1,0:T(8,128)(2,1)}) custom-call(s32[4]{0:T(128)} %get-tuple-element.55.src, s32[3]{0:T(128)} %slice_bitcast_fusion.2.bounds, bf16[4,256,768]{2,1,0:T(8,128)(2,1)} %copy-done.4, bf16[1024,768]{1,0:T(8,128)(2,1)} %get-tuple-element.56.q_ref, ...), custom_call_target="tpu_custom_call" | custom-call | flops 3221225472 | bytes 8053063 | tf_op jit(solution)/shard_map/attend/pallas_call | solution.py:547
  174.2 25.4 %feed_own.1 = (f32[1024,768]{1,0:T(8,128)}, f32[1024,768]{1,0:T(8,128)}, bf16[768,768]{1,0:T(8,128)(2,1)}, bf16[768,768]{1,0:T(8,128)(2,1)}, bf16[768,768]{1,0:T...) custom-call(s32[1]{0:T(128)} %bitcast.core, bf16[1024,768]{1,0:T(8,128)(2,1)} %bitcast.68, ...), custom_call_target="tpu_custom_call" | custom-call | flops 14495514624 | bytes 36238784 | tf_op jit(solution)/shard_map/feed_own/pallas_call | solution.py:251
  199.7 27.6 %feed_other.1 = (f32[1024,768]{1,0:T(8,128)}, f32[1024,768]{1,0:T(8,128)}, bf16[768,768]{1,0:T(8,128)(2,1)}, bf16[768,768]{1,0:T(8,128)(2,1)}, bf16[768,768]{1,0...) custom-call(s32[1]{0:T(128)} %bitcast.core, bf16[1024,768]{1,0:T(8,128)(2,1)} %bitcast.69, ...), custom_call_target="tpu_custom_call" | custom-call | flops 14495514624 | bytes 36238784 | tf_op jit(solution)/shard_map/feed_other/pallas_call | solution.py:251
  227.3 11.6 %residual.1 = (bf16[4,256,768]{2,1,0:T(8,128)(2,1)}, f32[4,256,768]{2,1,0:T(8,128)}, bf16[4,256,768]{2,1,0:T(8,128)(2,1)}, bf16[2,192,768]{2,1,0:T(8,128)(2,1)},...) custom-call(s32[1]{0:T(128)} %bitcast.core, f32[1024,768]{1,0:T(8,128)} %get-tuple-element.62.out_ref, ...), custom_call_target="tpu_custom_call" | custom-call | flops 2415919104 | bytes 6039797 | tf_op jit(solution)/shard_map/residual/pallas_call | solution.py:602
  241.4 31.5 %attend_back.1 = (bf16[4,256,960]{2,1,0:T(8,128)(2,1)}, bf16[4,256,960]{2,1,0:T(8,128)(2,1)}, bf16[4,256,384]{2,1,0:T(8,128)(2,1)}) custom-call(s32[4]{0:T(128)} %get-tuple-element.55.src, s32[3]{0:T(128)} %slice_bitcast_fusion.2.bounds, bf16[1024,768]{1,0:T(8,128)(2,1)} %get-tuple-element.56.q_ref, bf16[1024,768]{1,0:T(8,128)(2,1)} %get-tuple-element.57.k_ref, ...), custom_call_target="tpu_custom_call" | custom-call | flops 8053063680 | bytes 20132660 | tf_op jit(solution)/shard_map/attend_back/pallas_call | solution.py:628
  272.9 8.0 %weights.1 = (bf16[2,384,960]{2,1,0:T(8,128)(2,1)}, bf16[2,384,960]{2,1,0:T(8,128)(2,1)}, f32[2,960]{1,0:T(2,128)}) custom-call(s32[1]{0:T(128)} %bitcast.core, bf16[1024,768]{1,0:T(8,128)(2,1)} %bitcast.67, bf16[1024,960]{1,0:T(8,128)(2,1)} %bitcast.59, bf16[1024,960]{1,0:T(8,128)(2,1)} %bitcast.60), custom_call_target="tpu_custom_call" | custom-call | flops 3019898880 | bytes 7549747 | tf_op jit(solution)/shard_map/weights/pallas_call | solution.py:652
  291.2 7.9 %collective-permute-done.20 = bf16[192,768]{1,0:T(8,128)(2,1)S(1)} collective-permute-done((bf16[192,768]{1,0:T(8,128)(2,1)S(1)}, bf16[192,768]{1,0:T(8,128)(2,1)S(1)}, u32[]{:S(2)}, u32[]{:S(2)}) %collective-permute-start.20) | collective-permute-done | bytes 294944 | tf_op jit(solution)/shard_map/ppermute | solution.py:481
  306.3 9.3 %input.1 = (bf16[4,256,768]{2,1,0:T(8,128)(2,1)}, f32[2,768]{1,0:T(2,128)}) custom-call(bf16[4,256,960]{2,1,0:T(8,128)(2,1)} %get-tuple-element.69.own_ref, bf16[4,256,960]{2,1,0:T(8,128)(2,1)} %get-tuple-element.70.other_ref, bf16[768,960]{1,0:T(8,128)(2,1)} %copy-done.2, bf16[768,960]{1,0:T(8,128)(2,1)} %maximum_select_fusion.2.other_ref.w_other_ref, ...), custom_call_target="tpu_custom_call" | custom-call | flops 3019898880 | bytes 7549747 | tf_op jit(solution)/shard_map/input/pallas_call | solution.py:672
  330.5 9.8 %all-to-all-done.4 = bf16[4,256,768]{2,1,0:T(8,128)(2,1)} async-done(((bf16[4,256,768]{2,1,0:T(8,128)(2,1)}), bf16[4,256,768]{2,1,0:T(8,128)(2,1)}, u32[]{:S(2)}, u32[]{:S(2)}) %all-to-all-start.4) | async-done | bytes 1572896 | tf_op jit(solution)/shard_map/all_to_all | solution.py:484
  355.4 5.6 all-to-all-start.6
  361.1 15.4 %collective-permute-done.28 = bf16[768,768]{1,0:T(8,128)(2,1)} collective-permute-done((bf16[768,768]{1,0:T(8,128)(2,1)}, bf16[768,768]{1,0:T(8,128)(2,1)}, u32[]{:S(2)}, u32[]{:S(2)}) %collective-permute-start.28) | collective-permute-done | bytes 1179680 | tf_op jit(solution)/shard_map/ppermute | solution.py:481
  388.7 26.9 %collective-permute-done.24 = bf16[768,768]{1,0:T(8,128)(2,1)S(1)} collective-permute-done((bf16[768,768]{1,0:T(8,128)(2,1)S(1)}, bf16[768,768]{1,0:T(8,128)(2,1)S(1)}, u32[]{:S(2)}, u32[]{:S(2)}) %collective-permute-start.24) | collective-permute-done | bytes 1179680 | tf_op jit(solution)/shard_map/ppermute | solution.py:481
  417.1 6.0 %all-to-all-start.10 = ((bf16[8,96,768]{2,1,0:T(8,128)(2,1)}), bf16[8,96,768]{2,1,0:T(8,128)(2,1)S(1)}, u32[]{:S(2)}, u32[]{:S(2)}) async-start(bf16[8,96,768]{2,1,0:T(8,128)(2,1)} %bitcast.56), calls=%async_computation.10 | async-start | bytes 2359296 | tf_op jit(solution)/shard_map/all_to_all | solution.py:590
  423.2 28.3 %all-to-all-done.10 = bf16[8,96,768]{2,1,0:T(8,128)(2,1)S(1)} async-done(((bf16[8,96,768]{2,1,0:T(8,128)(2,1)}), bf16[8,96,768]{2,1,0:T(8,128)(2,1)S(1)}, u32[]{:S(2)}, u32[]{:S(2)}) %all-to-all-start.10) | async-done | bytes 1179680 | tf_op jit(solution)/shard_map/all_to_all | solution.py:590
  456.9 19.5 %all-to-all-done.7 = bf16[8,48,960]{2,1,0:T(8,128)(2,1)S(1)} async-done(((bf16[8,48,960]{2,1,0:T(8,128)(2,1)}), bf16[8,48,960]{2,1,0:T(8,128)(2,1)S(1)}, u32[]{:S(2)}, u32[]{:S(2)}) %all-to-all-start.7) | async-done | bytes 737312 | tf_op jit(solution)/shard_map/all_to_all | solution.py:593
  483.1 28.1 %all-to-all-done.13 = bf16[8,96,768]{2,1,0:T(8,128)(2,1)} async-done(((bf16[8,96,768]{2,1,0:T(8,128)(2,1)}), bf16[8,96,768]{2,1,0:T(8,128)(2,1)}, u32[]{:S(2)}, u32[]{:S(2)}) %all-to-all-start.13) | async-done | bytes 1179680 | tf_op jit(solution)/shard_map/all_to_all | solution.py:593
  519.5 11.1 %collective-permute-done.11 = f32[7104]{0:T(1024)S(1)} collective-permute-done((f32[7104]{0:T(1024)S(1)}, f32[7104]{0:T(1024)S(1)}, u32[]{:S(2)}, u32[]{:S(2)}) %collective-permute-start.11) | collective-permute-done | bytes 28448 | tf_op jit(solution)/shard_map/ppermute | solution.py:481
  561.0 11.7 %all-to-all-done.3 = bf16[4,256,768]{2,1,0:T(8,128)(2,1)} async-done(((bf16[4,256,768]{2,1,0:T(8,128)(2,1)}), bf16[4,256,768]{2,1,0:T(8,128)(2,1)}, u32[]{:S(2)}, u32[]{:S(2)}) %all-to-all-start.3) | async-done | bytes 1572896 | tf_op jit(solution)/shard_map/all_to_all | solution.py:484
  588.7 5.5 fusion
  (221 shorter events, 182.0 us)
Async XLA Ops:
  34.3 84.4 %all-to-all-start = ((bf16[4,256,768]{2,1,0:T(8,128)(2,1)}), bf16[4,256,768]{2,1,0:T(8,128)(2,1)S(1)}, u32[]{:S(2)}, u32[]{:S(2)}) async-start(bf16[4,256,768]{2,1,0:T(8,128)(2,1)} %bitcast.3), calls=%async_computation | async-start | bytes 3145728 | tf_op jit(solution)/shard_map/all_to_all | solution.py:484
  47.0 87.3 %collective-permute-start.6 = (bf16[768,768]{1,0:T(8,128)(2,1)}, bf16[768,768]{1,0:T(8,128)(2,1)}, u32[]{:S(2)}, u32[]{:S(2)}) collective-permute-start(bf16[768,768]{1,0:T(8,128)(2,1)} %constant_dynamic-slice_fusion.1), channel_id=1, source_target_pairs={{0,1},{1,0},{2,3},{3,2},{4,5},{5,4},{6,7},{7,6},{8,9},{9,8},{10,11... | collective-permute-start | bytes 3538952 | tf_op jit(solution)/shard_map/ppermute | solution.py:481
  48.4 86.5 %collective-permute-start.8 = (bf16[768,768]{1,0:T(8,128)(2,1)}, bf16[768,768]{1,0:T(8,128)(2,1)}, u32[]{:S(2)}, u32[]{:S(2)}) collective-permute-start(bf16[768,768]{1,0:T(8,128)(2,1)} %constant_dynamic-slice_fusion), channel_id=1, source_target_pairs={{0,1},{1,0},{2,3},{3,2},{4,5},{5,4},{6,7},{7,6},{8,9},{9,8},{10,11... | collective-permute-start | bytes 3538952 | tf_op jit(solution)/shard_map/ppermute | solution.py:481
  50.2 68.6 %collective-permute-start.4 = (bf16[192,768]{1,0:T(8,128)(2,1)S(1)}, bf16[192,768]{1,0:T(8,128)(2,1)S(1)}, u32[]{:S(2)}, u32[]{:S(2)}) collective-permute-start(bf16[192,768]{1,0:T(8,128)(2,1)S(1)} %constant_dynamic-slice_fusion.2), channel_id=1, source_target_pairs={{0,1},{1,0},{2,3},{3,2},{4,5},{5,4},{6,7},{7,6},{8,9},{9,8},{10,11... | collective-permute-start | bytes 884744 | tf_op jit(solution)/shard_map/ppermute | solution.py:481
  62.3 72.7 %collective-permute-start.2 = (bf16[384,960]{0,1:T(8,128)(2,1)}, bf16[384,960]{0,1:T(8,128)(2,1)}, u32[]{:S(2)}, u32[]{:S(2)}) collective-permute-start(bf16[384,960]{0,1:T(8,128)(2,1)} %collective-permute-done.1), channel_id=1, source_target_pairs={{0,2},{2,0},{4,6},{6,4},{8,10},{10,8},{12,14},{14,12},{16,18},{18,... | collective-permute-start | bytes 2211848 | tf_op jit(solution)/shard_map/ppermute | solution.py:478
  62.4 67.1 %collective-permute-start.3 = (f32[1,2496]{1,0:T(1,128)S(1)}, f32[1,2496]{1,0:T(1,128)S(1)}, u32[]{:S(2)}, u32[]{:S(2)}) collective-permute-start(f32[1,2496]{1,0:T(1,128)S(1)} %reshape.174), channel_id=1, source_target_pairs={{0,1},{1,0},{2,3},{3,2},{4,5},{5,4},{6,7},{7,6},{8,9},{9,8},{10,11... | collective-permute-start | bytes 29960 | tf_op jit(solution)/shard_map/ppermute | solution.py:481
  119.9 53.1 %all-to-all-start.2 = ((bf16[4,256,768]{2,1,0:T(8,128)(2,1)}), bf16[4,256,768]{2,1,0:T(8,128)(2,1)S(1)}, u32[]{:S(2)}, u32[]{:S(2)}) async-start(bf16[4,256,768]{2,1,0:T(8,128)(2,1)} %bitcast.61), calls=%async_computation.2 | async-start | bytes 3145728 | tf_op jit(solution)/shard_map/all_to_all | solution.py:484
  134.3 65.3 %collective-permute-start.7 = (bf16[768,768]{1,0:T(8,128)(2,1)}, bf16[768,768]{1,0:T(8,128)(2,1)}, u32[]{:S(2)}, u32[]{:S(2)}) collective-permute-start(bf16[768,768]{1,0:T(8,128)(2,1)} %collective-permute-done.6.refs_2_), channel_id=1, source_target_pairs={{0,2},{2,0},{4,6},{6,4},{8,10},{10,8},{12,14},{14,12},{16,18},{18,... | collective-permute-start | bytes 3538952 | tf_op jit(solution)/shard_map/ppermute | solution.py:478
  134.9 64.8 %collective-permute-start.9 = (bf16[768,768]{1,0:T(8,128)(2,1)}, bf16[768,768]{1,0:T(8,128)(2,1)}, u32[]{:S(2)}, u32[]{:S(2)}) collective-permute-start(bf16[768,768]{1,0:T(8,128)(2,1)} %collective-permute-done.8.refs_4_), channel_id=1, source_target_pairs={{0,2},{2,0},{4,6},{6,4},{8,10},{10,8},{12,14},{14,12},{16,18},{18,... | collective-permute-start | bytes 3538952 | tf_op jit(solution)/shard_map/ppermute | solution.py:478
  239.0 50.6 %collective-permute-start.19 = (bf16[2,192,768]{2,1,0:T(8,128)(2,1)}, bf16[2,192,768]{2,1,0:T(8,128)(2,1)S(1)}, u32[]{:S(2)}, u32[]{:S(2)}) collective-permute-start(bf16[2,192,768]{2,1,0:T(8,128)(2,1)} %get-tuple-element.83), channel_id=1, source_target_pairs={{0,2},{2,0},{4,6},{6,4},{8,10},{10,8},{12,14},{14,12},{16,18},{18,... | collective-permute-start | bytes 1769480 | tf_op jit(solution)/shard_map/ppermute | solution.py:478
  282.9 37.7 %collective-permute-start.16 = (bf16[2,384,960]{1,2,0:T(8,128)(2,1)S(1)}, bf16[2,384,960]{1,2,0:T(8,128)(2,1)}, u32[]{:S(2)}, u32[]{:S(2)}) collective-permute-start(bf16[2,384,960]{1,2,0:T(8,128)(2,1)S(1)} %copy.51), channel_id=1, source_target_pairs={{0,2},{2,0},{4,6},{6,4},{8,10},{10,8},{12,14},{14,12},{16,18},{18,... | collective-permute-start | bytes 4423688 | tf_op jit(solution)/shard_map/ppermute | solution.py:478
  315.8 24.5 %all-to-all-start.4 = ((bf16[4,256,768]{2,1,0:T(8,128)(2,1)}), bf16[4,256,768]{2,1,0:T(8,128)(2,1)}, u32[]{:S(2)}, u32[]{:S(2)}) async-start(bf16[4,256,768]{2,1,0:T(8,128)(2,1)} %get-tuple-element.72), calls=%async_computation.4 | async-start | bytes 3145728 | tf_op jit(solution)/shard_map/all_to_all | solution.py:484
  320.1 25.8 %collective-permute-start.27 = (bf16[768,768]{1,0:T(8,128)(2,1)}, bf16[768,768]{1,0:T(8,128)(2,1)}, u32[]{:S(2)}, u32[]{:S(2)}) collective-permute-start(bf16[768,768]{1,0:T(8,128)(2,1)} %get-tuple-element.91), channel_id=1, source_target_pairs={{0,2},{2,0},{4,6},{6,4},{8,10},{10,8},{12,14},{14,12},{16,18},{18,... | collective-permute-start | bytes 3538952 | tf_op jit(solution)/shard_map/ppermute | solution.py:478
  330.4 30.7 %collective-permute-start.26 = (bf16[768,768]{1,0:T(8,128)(2,1)}, bf16[768,768]{1,0:T(8,128)(2,1)}, u32[]{:S(2)}, u32[]{:S(2)}) collective-permute-start(bf16[768,768]{1,0:T(8,128)(2,1)} %get-tuple-element.89), channel_id=1, source_target_pairs={{0,2},{2,0},{4,6},{6,4},{8,10},{10,8},{12,14},{14,12},{16,18},{18,... | collective-permute-start | bytes 3538952 | tf_op jit(solution)/shard_map/ppermute | solution.py:478
  348.9 27.6 %collective-permute-start.28 = (bf16[768,768]{1,0:T(8,128)(2,1)}, bf16[768,768]{1,0:T(8,128)(2,1)}, u32[]{:S(2)}, u32[]{:S(2)}) collective-permute-start(bf16[768,768]{1,0:T(8,128)(2,1)} %add_convert_fusion.1), channel_id=1, source_target_pairs={{0,1},{1,0},{2,3},{3,2},{4,5},{5,4},{6,7},{7,6},{8,9},{9,8},{10,11... | collective-permute-start | bytes 3538952 | tf_op jit(solution)/shard_map/ppermute | solution.py:481
  355.4 24.9 %all-to-all-start.6 = ((bf16[8,48,960]{2,1,0:T(8,128)(2,1)}), bf16[8,48,960]{2,1,0:T(8,128)(2,1)S(1)}, u32[]{:S(2)}, u32[]{:S(2)}) async-start(bf16[8,48,960]{2,1,0:T(8,128)(2,1)} %bitcast.58), calls=%async_computation.6 | async-start | bytes 1572864 | tf_op jit(solution)/shard_map/all_to_all | solution.py:590
  380.3 36.7 %all-to-all-start.12 = ((bf16[8,96,768]{2,1,0:T(8,128)(2,1)}), bf16[8,96,768]{2,1,0:T(8,128)(2,1)S(1)}, u32[]{:S(2)}, u32[]{:S(2)}) async-start(bf16[8,96,768]{2,1,0:T(8,128)(2,1)} %bitcast.28), calls=%async_computation.12 | async-start | bytes 2359296 | tf_op jit(solution)/shard_map/all_to_all | solution.py:590
  387.1 28.4 %collective-permute-start.24 = (bf16[768,768]{1,0:T(8,128)(2,1)S(1)}, bf16[768,768]{1,0:T(8,128)(2,1)S(1)}, u32[]{:S(2)}, u32[]{:S(2)}) collective-permute-start(bf16[768,768]{1,0:T(8,128)(2,1)S(1)} %add_convert_fusion.3), channel_id=1, source_target_pairs={{0,1},{1,0},{2,3},{3,2},{4,5},{5,4},{6,7},{7,6},{8,9},{9,8},{10,11... | collective-permute-start | bytes 3538952 | tf_op jit(solution)/shard_map/ppermute | solution.py:481
  417.1 34.4 %all-to-all-start.10 = ((bf16[8,96,768]{2,1,0:T(8,128)(2,1)}), bf16[8,96,768]{2,1,0:T(8,128)(2,1)S(1)}, u32[]{:S(2)}, u32[]{:S(2)}) async-start(bf16[8,96,768]{2,1,0:T(8,128)(2,1)} %bitcast.56), calls=%async_computation.10 | async-start | bytes 2359296 | tf_op jit(solution)/shard_map/all_to_all | solution.py:590
  478.6 32.6 %all-to-all-start.13 = ((bf16[8,96,768]{2,1,0:T(8,128)(2,1)}), bf16[8,96,768]{2,1,0:T(8,128)(2,1)}, u32[]{:S(2)}, u32[]{:S(2)}) async-start(bf16[8,96,768]{2,1,0:T(8,128)(2,1)} %broadcast_in_dim.14), calls=%async_computation.13 | async-start | bytes 2359296 | tf_op jit(solution)/shard_map/all_to_all | solution.py:593
  512.3 36.0 %all-to-all-start.11 = ((bf16[8,96,768]{2,1,0:T(8,128)(2,1)}), bf16[8,96,768]{2,1,0:T(8,128)(2,1)}, u32[]{:S(2)}, u32[]{:S(2)}) async-start(bf16[8,96,768]{2,1,0:T(8,128)(2,1)} %broadcast_in_dim.13), calls=%async_computation.11 | async-start | bytes 2359296 | tf_op jit(solution)/shard_map/all_to_all | solution.py:593
  517.1 36.1 %collective-permute-start.10 = (bf16[4,256,192]{2,1,0:T(8,128)(2,1)S(1)}, bf16[4,256,192]{2,1,0:T(8,128)(2,1)S(1)}, u32[]{:S(2)}, u32[]{:S(2)}) collective-permute-start(bf16[4,256,192]{2,1,0:T(8,128)(2,1)S(1)} %get-tuple-element.133), channel_id=1, source_target_pairs={{0,1},{1,0},{2,3},{3,2},{4,5},{5,4},{6,7},{7,6},{8,9},{9,8},{10,11... | collective-permute-start | bytes 1179656 | tf_op jit(solution)/shard_map/ppermute | solution.py:481
  555.2 28.2 %collective-permute-start.29 = (bf16[768,768]{1,0:T(8,128)(2,1)}, bf16[768,768]{1,0:T(8,128)(2,1)}, u32[]{:S(2)}, u32[]{:S(2)}) collective-permute-start(bf16[768,768]{1,0:T(8,128)(2,1)} %bitcast.29), channel_id=1, source_target_pairs={{0,2},{2,0},{4,6},{6,4},{8,10},{10,8},{12,14},{14,12},{16,18},{18,... | collective-permute-start | bytes 3538952 | tf_op jit(solution)/shard_map/ppermute | solution.py:478
  557.6 31.0 %collective-permute-start.25 = (bf16[768,768]{1,0:T(8,128)(2,1)}, bf16[768,768]{1,0:T(8,128)(2,1)}, u32[]{:S(2)}, u32[]{:S(2)}) collective-permute-start(bf16[768,768]{1,0:T(8,128)(2,1)} %bitcast.27), channel_id=1, source_target_pairs={{0,2},{2,0},{4,6},{6,4},{8,10},{10,8},{12,14},{14,12},{16,18},{18,... | collective-permute-start | bytes 3538952 | tf_op jit(solution)/shard_map/ppermute | solution.py:478
  (51 other events, 735.3 us)

commit v2 on v1

v2 whole, which is shorter than its diff:
```python
from functools import partial

import jax
import jax.numpy as jnp
from jax import lax
from jax.experimental import pallas as pl
from jax.experimental.pallas import tpu as pltpu
from jax.sharding import PartitionSpec as P

HEAD = 64
SEQ_LEN = 1024
BLOCK = 256
LONGEST = 512
SPAN = SEQ_LEN // BLOCK
REACH = -(-LONGEST // BLOCK) + 1
PAIR = 2 * HEAD
EPSILON = 1e-05
MASKED = -1e30
GELU_A = 0.7978845608028654
GELU_B = 0.044715
SCALE = HEAD ** (-0.5)
DOCS = 4
PARTS = 4
CORE, LINK, OUTER, MEMBER = 0, 1, 2, 3
BOUND = MEMBER + SPAN
PEAK = 1.15e9
VMEM = 56 * 1024 * 1024

F32 = jnp.float32
BF16 = jnp.bfloat16


def nn(left, right):
    return lax.dot_general(left, right, (((1,), (0,)), ((), ())), preferred_element_type=F32)


def nt(left, right):
    return lax.dot_general(left, right, (((1,), (1,)), ((), ())), preferred_element_type=F32)


def tn(left, right):
    return lax.dot_general(left, right, (((0,), (0,)), ((), ())), preferred_element_type=F32)


def vector(ref):
    return ref[...].reshape(1, -1)


def normed(rows):
    centred = rows - jnp.mean(rows, axis=-1, keepdims=True)
    inverse = lax.rsqrt(jnp.mean(centred * centred, axis=-1, keepdims=True) + EPSILON)
    return centred * inverse, inverse


def norm_back(grad_out, scaled, inverse, gain):
    grad_scaled = grad_out * gain
    first_mean = jnp.mean(grad_scaled, axis=-1, keepdims=True)
    second_mean = jnp.mean(grad_scaled * scaled, axis=-1, keepdims=True)
    return inverse * (grad_scaled - first_mean - scaled * second_mean)


def full(shape):
    return pl.BlockSpec(shape, lambda *_: (0,) * len(shape), pipeline_mode=pl.Buffered(1))


def member_at(p, ids):
    return ids[MEMBER + p]


def doc_bounds(ids):
    return [ids[BOUND + index] for index in range(DOCS - 1)]


def placed(columns, rows=BLOCK, column=0):
    return pl.BlockSpec(
        (None, rows, columns), lambda p, ids: (member_at(p, ids), 0, column)
    )


def in_rows(columns):
    return pl.BlockSpec((BLOCK, columns), lambda p, *_: (p, 0))


def by_block(columns):
    return pl.BlockSpec((None, BLOCK, columns), lambda p, *_: (p, 0, 0))


def shape_of(shape, dtype):
    return jax.ShapeDtypeStruct(shape, dtype)


def call(kernel, scalars, grid, ins, outs, out_shapes, scratch=(), micros=1, name=None,
         aliases=None):
    return pl.pallas_call(
        kernel,
        grid_spec=pltpu.PrefetchScalarGridSpec(
            num_scalar_prefetch=scalars,
            grid=grid,
            in_specs=ins,
            out_specs=outs,
            scratch_shapes=scratch,
        ),
        out_shape=out_shapes,
        compiler_params=pltpu.CompilerParams(
            dimension_semantics=("arbitrary",) * len(grid), vmem_limit_bytes=VMEM
        ),
        cost_estimate=pl.CostEstimate(
            flops=int(micros * PEAK), bytes_accessed=int(micros * PEAK) // 1000, transcendentals=0
        ),
        input_output_aliases=aliases or {},
        name=name,
    )


def project_kernel(
    ids, x_ref, own_ref, near_ref, far_ref, bias_ref, gain_ref, shift_ref,
    norm_ref, q_ref, k_ref, fresh_ref, other_ref, out_ref,
):
    half = q_ref.shape[1] // 2
    fresh = half // 2
    split = other_ref.shape[0] // 2

    @pl.when(pl.program_id(0) == 0)
    def _():
        first = ids[CORE] == 0
        near, far = near_ref[...], far_ref[...]
        low, high = jnp.where(first, near, far), jnp.where(first, far, near)
        other_ref[:split, :] = low[:split]
        other_ref[split:, :] = high[:split]
        out_ref[:half // 2, :] = low[split:]
        out_ref[half // 2:, :] = high[split:]

    scaled, _ = normed(x_ref[...].astype(F32))
    rows = (scaled * vector(gain_ref) + vector(shift_ref)).astype(BF16)
    norm_ref[...] = rows
    for side, weight in enumerate((own_ref, other_ref)):
        made = nn(rows, weight[:2 * half, :])
        value = nt(rows, weight[2 * half:, :])
        columns = slice(side * half, (side + 1) * half)
        q_ref[:, columns] = (made[:, :half] + bias_ref[side:side + 1, :half]).astype(BF16)
        k_ref[:, columns] = made[:, half:].astype(BF16)
        fresh_ref[side] = (value + bias_ref[side:side + 1, half:half + fresh]).astype(BF16)


def doc_start(position, bounds):
    start = jnp.zeros_like(position)
    for bound in bounds:
        start = jnp.where(position >= bound, bound, start)
    return start


def attend_kernel(
    ids, x_ref, q_ref, k_ref, fresh_ref, skip_ref, own_ref, other_ref,
    bias_ref, gain_ref, shift_ref, v_ref, att_ref, lse_ref, middle_ref, norm_ref, att_s, lse_s,
):
    p = pl.program_id(0)
    bounds = doc_bounds(ids)
    skipped = skip_ref[...].T
    part = skipped.shape[1] // 2
    v_ref[pl.ds(pl.multiple_of(p * BLOCK, BLOCK), BLOCK), :] = jnp.concatenate(
        [fresh_ref[0], skipped[:, :part], fresh_ref[1], skipped[:, part:]], axis=1
    )
    width = q_ref.shape[1]
    half = width // 2
    first = doc_start(p * BLOCK, bounds)
    needed = p - first // BLOCK + 1
    lane = lax.broadcasted_iota(jnp.int32, (1, PAIR), 1)
    low = lane < HEAD
    picks = [jnp.where(low, SCALE, 0.0).astype(BF16), jnp.where(low, 0.0, SCALE).astype(BF16)]

    def run(count):
        span = count * BLOCK
        base = pl.multiple_of((p - count + 1) * BLOCK, BLOCK)
        row = p * BLOCK + lax.broadcasted_iota(jnp.int32, (BLOCK, 1), 0)
        start = doc_start(row, bounds)
        column = base + lax.broadcasted_iota(jnp.int32, (1, span), 1)
        seen = (column <= row) & (column >= start)
        bias = jnp.where(seen, 0.0, MASKED)
        head_lane = lax.broadcasted_iota(jnp.int32, (1, 128), 1)

        @pl.loop(0, width // PAIR)
        def _(pair):
            lanes = pl.ds(pl.multiple_of(pair * PAIR, PAIR), PAIR)
            queries = q_ref[:, lanes]
            keys = k_ref[pl.ds(base, span), lanes]
            values = v_ref[pl.ds(base, span), lanes]
            outs = []
            for side in range(2):
                scores = nt(queries * picks[side], keys) + bias
                top = jnp.max(scores, axis=1, keepdims=True)
                probs = jnp.exp(scores - top)
                total = jnp.sum(probs, axis=1, keepdims=True)
                outs.append(nn(probs.astype(BF16), values) / total)
                lse_s[...] = jnp.where(
                    head_lane == 2 * pair + side, top + jnp.log(total), lse_s[...]
                )
            att_s[:, lanes] = jnp.where(low, outs[0], outs[1]).astype(BF16)

    for count in range(1, REACH + 1):
        pl.when(needed == count)(partial(run, count))

    lse_ref[...] = lse_s[...].T[:lse_ref.shape[0], :]
    attended = att_s[...]
    att_ref[...] = attended
    middle = (
        x_ref[...].astype(F32)
        + nn(attended[:, :half], own_ref[...])
        + nn(attended[:, half:], other_ref[...])
        + vector(bias_ref)
    )
    middle_ref[...] = middle
    scaled, _ = normed(middle)
    norm_ref[...] = (scaled * vector(gain_ref) + vector(shift_ref)).astype(BF16)


def feed_kernel(fetched, has_sums, has_grads, ids, *refs):
    norm_ref, grad_ref = refs[:2]
    if fetched:
        mine_ref, theirs_ref, down_ref, bias_ref = refs[2:6]
        refs = refs[6:]
        first = ids[OUTER] % 2 == 0
        mine, theirs = mine_ref[...], theirs_ref[...]
        up = jnp.concatenate(
            [jnp.where(first, mine, theirs), jnp.where(first, theirs, mine)], axis=0
        )
        down = down_ref[...]
    else:
        weight_ref, bias_ref = refs[2:4]
        refs = refs[4:]
        up = weight_ref[:weight_ref.shape[0] // 2, :]
        down = weight_ref[weight_ref.shape[0] // 2:, :]
    units = up.shape[0]
    if has_sums:
        out_in, back_in = refs[:2]
        refs = refs[2:]
    if has_grads:
        made_in = refs[0]
        refs = refs[1:]
    out_ref, back_ref, gb_ref = refs[:3]
    made_refs = refs[3:]
    rows = norm_ref[...]
    grads = grad_ref[...]
    hidden = nt(rows, up) + bias_ref[...]
    square = hidden * hidden
    curve = jnp.tanh(hidden * (GELU_A + GELU_A * GELU_B * square))
    plus = 0.5 + 0.5 * curve
    value = hidden * plus
    active = value.astype(BF16)
    slope = plus + value * (1.0 - curve) * (GELU_A + 3.0 * GELU_A * GELU_B * square)
    hidden_grad = nt(grads, down) * slope
    gb_ref[...] = jnp.sum(hidden_grad, axis=0, keepdims=True)
    hidden_low = hidden_grad.astype(BF16)
    out = nn(active, down)
    back = nn(hidden_low, up)
    if has_sums:
        out = out + out_in[...].astype(F32)
        back = back + back_in[...].astype(F32)
    out_ref[...] = out.astype(BF16)
    back_ref[...] = back.astype(BF16)
    for piece, left, right in (
        (slice(0, units), hidden_low, rows), (slice(units, 2 * units), active, grads)
    ):
        made = tn(left, right)
        if has_grads:
            made = made + made_in[piece, :].astype(F32)
        made = made.astype(BF16)
        count = made_refs[0].shape[0]
        for row in range(piece.start, piece.stop, count):
            part = made_refs[row // count]
            if count > units:
                part[piece, :] = made
            else:
                part[...] = made[row - piece.start:row - piece.start + count]


def feed(ids, rows, grads, weights, bias, sums=(), made=(), parts=1):
    tokens, width = rows.shape
    units = bias.shape[1]
    total = full((tokens, width))
    return call(
        partial(feed_kernel, len(weights) > 1, len(sums) > 0, len(made) > 0),
        1,
        (1,),
        [total, total] + [full(weight.shape) for weight in weights] + [full((1, units))]
        + [total] * len(sums) + [full((2 * units, width))] * len(made),
        [total, total, full((1, units))] + [full((2 * units // parts, width))] * parts,
        [
            shape_of((tokens, width), BF16), shape_of((tokens, width), BF16),
            shape_of((1, units), F32),
        ] + [shape_of((2 * units // parts, width), BF16)] * parts,
        micros=14,
        name="feed",
    )(ids, rows, grads, *weights, bias, *sums, *made)


def residual_kernel(
    ids, out_a, out_b, back_a, back_b, grad_ref, middle_ref, att_ref, own_ref, other_ref,
    gain_ref, down_bias_ref, layer_ref, mg_ref, ga_ref, keep_ref, send_ref, small_ref, acc_s,
):
    p = pl.program_id(0)
    half = own_ref.shape[0]
    middle = middle_ref[...]
    summed = lambda refs: sum(ref[...].astype(F32) for ref in refs)
    layer_ref[...] = (middle + summed((out_a, out_b)) + vector(down_bias_ref)).astype(BF16)
    scaled, inverse = normed(middle)
    second = summed((back_a, back_b))
    out_grad = grad_ref[...].astype(F32)
    middle_grad = out_grad + norm_back(second, scaled, inverse, vector(gain_ref))
    mg_ref[...] = middle_grad
    low = middle_grad.astype(BF16)
    ga_ref[:, :half] = nt(low, own_ref[...]).astype(BF16)
    ga_ref[:, half:] = nt(low, other_ref[...]).astype(BF16)
    weight_grad = tn(att_ref[...], low)
    sums = jnp.concatenate(
        [
            jnp.sum(value, axis=0, keepdims=True)
            for value in (second * scaled, second, middle_grad, out_grad)
        ],
        axis=0,
    )

    @pl.when(p == 0)
    def _():
        acc_s[...] = weight_grad
        small_ref[...] = sums

    @pl.when(p > 0)
    def _():
        acc_s[...] += weight_grad
        small_ref[...] += sums

    @pl.when(p == pl.num_programs(0) - 1)
    def _():
        rows = half // 2
        near = pl.multiple_of(ids[CORE] * rows, 32)
        far = pl.multiple_of(rows - ids[CORE] * rows, 32)
        for side in range(2):
            keep_ref[side] = acc_s[pl.ds(side * half + near, rows), :].astype(BF16)
            send_ref[side] = acc_s[pl.ds(side * half + far, rows), :].astype(BF16)


def attend_back_kernel(
    head_base, ids, q_ref, k_ref, v_ref, att_ref, ga_ref, lse_ref,
    made_ref, skip_ref, dq_s, dk_s, dv_s, delta_s,
):
    p = pl.program_id(0)
    width = q_ref.shape[1]
    fresh = width // 2
    bounds = doc_bounds(ids)
    place = member_at(p, ids)
    first = doc_start(p * BLOCK, bounds)
    needed = p - first // BLOCK + 1
    low = lax.broadcasted_iota(jnp.int32, (1, PAIR), 1) < HEAD
    picks = [jnp.where(low, SCALE, 0.0).astype(BF16), jnp.where(low, 0.0, SCALE).astype(BF16)]
    ones = [jnp.where(low, 1.0, 0.0).astype(BF16), jnp.where(low, 0.0, 1.0).astype(BF16)]

    @pl.when(p == 0)
    def _():
        dk_s[...] = jnp.zeros_like(dk_s)
        dv_s[...] = jnp.zeros_like(dv_s)

    product = ga_ref[...].astype(F32) * att_ref[...].astype(F32)
    high = product.astype(BF16)
    rest = (product - high.astype(F32)).astype(BF16)
    owner = lax.broadcasted_iota(jnp.int32, (delta_s.shape[0], width), 1) // HEAD
    which = lax.broadcasted_iota(jnp.int32, (delta_s.shape[0], width), 0)
    gather = (owner == which).astype(F32).astype(BF16)
    delta_s[...] = nt(gather, high) + nt(gather, rest)

    def run(count):
        span = count * BLOCK
        base = pl.multiple_of((p - count + 1) * BLOCK, BLOCK)
        row = p * BLOCK + lax.broadcasted_iota(jnp.int32, (1, BLOCK), 1)
        start = doc_start(row, bounds)
        column = base + lax.broadcasted_iota(jnp.int32, (span, 1), 0)
        seen = (column <= row) & (column >= start)
        bias = jnp.where(seen, 0.0, MASKED)

        @pl.loop(0, width // PAIR)
        def _(pair):
            lanes = pl.ds(pl.multiple_of(pair * PAIR, PAIR), PAIR)
            queries = q_ref[:, lanes]
            grads = ga_ref[:, lanes]
            keys = k_ref[pl.ds(base, span), lanes]
            values = v_ref[pl.ds(base, span), lanes]
            query_parts = []
            for side in range(2):
                head = 2 * pair + side
                picked = queries * picks[side]
                chosen = grads * ones[side]
                scores = nt(keys, picked) + bias
                probs = jnp.exp(scores - lse_ref[pl.ds(head_base + head, 1), :])
                dprobs = nt(values, chosen)
                dscores = (probs * (dprobs - delta_s[pl.ds(head, 1), :])).astype(BF16)
                value_part = nn(probs.astype(BF16), chosen)
                key_part = nn(dscores, picked)
                query_parts.append(tn(dscores, keys))
                if side == 0:
                    value_sum, key_sum = value_part, key_part
                else:
                    value_sum, key_sum = value_sum + value_part, key_sum + key_part
            dv_s[pl.ds(base, span), lanes] += value_sum
            dk_s[pl.ds(base, span), lanes] += key_sum
            dq_s[:, lanes] = (
                jnp.where(low, query_parts[0], query_parts[1]) * SCALE
            ).astype(BF16)

    for count in range(1, REACH + 1):
        pl.when(needed == count)(partial(run, count))

    made_ref[place, :, :width] = dq_s[...]

    @pl.when(p == pl.num_programs(0) - 1)
    def _():
        for block in range(SPAN):
            rows = slice(block * BLOCK, (block + 1) * BLOCK)
            to = member_at(block, ids)
            made_ref[to, :, width:2 * width] = dk_s[rows, :].astype(BF16)
            value_grad = dv_s[rows, :]
            made_ref[to, :, 2 * width:] = value_grad[:, :fresh].astype(BF16)
            skip_ref[to] = value_grad.T[fresh:, :].astype(BF16)


def weight_kernel(ids, norm_ref, made_ref, keep_ref, send_ref, sums_ref, made_s):
    rows = norm_ref[...]
    grads = made_ref[...]
    width = rows.shape[1]
    made_s[:width, :] = tn(rows, grads[:, :width])
    made_s[width:, :] = tn(grads[:, width:], rows)
    half = made_s.shape[0] // 2
    near = pl.multiple_of(ids[CORE] * half, 32)
    far = pl.multiple_of(half - ids[CORE] * half, 32)
    for target, start in ((keep_ref, near), (send_ref, far)):
        target[:half, :] = made_s[pl.ds(start, half), :].astype(BF16)
        target[half:, :] = jnp.zeros((target.shape[0] - half, width), BF16)
    sums_ref[...] = jnp.sum(grads.astype(F32), axis=0, keepdims=True)


def input_kernel(
    own_ref, other_ref, w_own_ref, w_other_ref, x_ref, mg_ref, gain_ref, grad_ref, small_ref
):
    p = pl.program_id(0)
    first = None
    for made_ref, weight in ((own_ref, w_own_ref), (other_ref, w_other_ref)):
        width = weight.shape[1]
        part = nt(made_ref[:, :width], weight[:width, :]) + nn(made_ref[:, width:], weight[width:, :])
        first = part if first is None else first + part
    scaled, inverse = normed(x_ref[...].astype(F32))
    grad_ref[...] = (mg_ref[...] + norm_back(first, scaled, inverse, vector(gain_ref))).astype(BF16)
    sums = jnp.concatenate(
        [jnp.sum(value, axis=0, keepdims=True) for value in (first * scaled, first)], axis=0
    )

    @pl.when(p == 0)
    def _():
        small_ref[...] = sums

    @pl.when(p > 0)
    def _():
        small_ref[...] += sums


def fold_kernel(groups, starts, ids, *refs):
    sources = sum(len(group) for group in groups)
    outs = refs[sources:-1]
    total_s = refs[-1]
    row = 0
    place = 0
    for group in groups:
        total = None
        for index in group:
            ref = refs[place]
            place += 1
            value = (ref[...] if index is None else ref[index]).astype(F32)
            total = value if total is None else total + value
        total_s[row:row + total.shape[0], :] = total
        row += total.shape[0]
    for out, start in zip(outs, starts):
        at = start(ids)
        if not isinstance(at, int):
            at = pl.multiple_of(at, 8)
        out[...] = total_s[pl.ds(at, out.shape[0]), :].astype(BF16)


def fold(ids, groups, starts, count):
    arrays = [entry[0] for group in groups for entry in group]
    indices = tuple(tuple(entry[1] for entry in group) for group in groups)
    width = arrays[0].shape[-1]
    rows = sum(group[0][0].shape[-2] for group in groups)
    return call(
        partial(fold_kernel, indices, starts),
        1,
        (1,),
        [full(array.shape) for array in arrays],
        [full((count, width)) for _ in starts],
        [shape_of((count, width), BF16) for _ in starts],
        scratch=[pltpu.VMEM((rows, width), F32)],
        micros=3.5,
        name="fold",
    )(ids, *arrays)


def join_kernel(ends, ids, *refs):
    for ref, end in zip(refs[:-1], ends):
        rows = ref.shape[0]
        refs[-1][pl.ds(pl.multiple_of(end(ids) * rows, 8), rows), :] = ref[...]


def join(ids, pieces, ends):
    rows, width = pieces[0].shape
    spec = full((rows, width))
    return call(
        partial(join_kernel, ends),
        1,
        (1,),
        [spec] * len(pieces),
        [full((rows * len(pieces), width))],
        [shape_of((rows * len(pieces), width), BF16)],
        micros=2.5,
        name="join",
    )(ids, *pieces)[0]


def both_halves(ids, bit, mine, theirs):
    first = ids[bit] == 0
    return jnp.where(first, mine, theirs), jnp.where(first, theirs, mine)


def place_feed_kernel(ids, mine_ref, theirs_ref, up_ref, down_ref, out_ref):
    units = down_ref.shape[0]
    here = pl.program_id(0) == ids[CORE]
    whole = jnp.where(here, mine_ref[...], theirs_ref[...]).astype(F32)
    up_ref[...] = whole[:units].T
    down_ref[...] = whole[units:2 * units]
    out_ref[...] = whole[2 * units:]


def place_feed(ids, mine, theirs, units):
    rows, width = mine.shape
    size = units // 2
    out_rows = rows - 2 * size
    return call(
        place_feed_kernel,
        1,
        (2,),
        [full((rows, width))] * 2,
        [
            pl.BlockSpec((width, size), lambda h, ids: (0, h)),
            pl.BlockSpec((size, width), lambda h, ids: (h, 0)),
            pl.BlockSpec((out_rows, width), lambda h, ids: (h, 0)),
        ],
        [
            shape_of((width, units), F32), shape_of((units, width), F32),
            shape_of((2 * out_rows, width), F32),
        ],
        micros=8,
        name="place_feed",
    )(ids, mine, theirs)


def place_qkv_kernel(ids, mine, mine_far, theirs, theirs_far, q_ref, k_ref, v_ref):
    half = q_ref.shape[1]
    split = (q_ref.shape[0] + v_ref.shape[0]) // 2
    near = jnp.concatenate(both_halves(ids, LINK, mine[...], mine_far[...]), axis=0)
    far = jnp.concatenate(both_halves(ids, LINK, theirs[...], theirs_far[...]), axis=0)
    low, high = [value[:split].astype(F32) for value in both_halves(ids, CORE, near, far)]
    rest = q_ref.shape[0] - split
    for ref, columns in ((q_ref, slice(0, half)), (k_ref, slice(half, 2 * half))):
        ref[:split, :] = low[:, columns]
        ref[split:, :] = high[:rest, columns]
    v_ref[...] = high[rest:]


def place_qkv(ids, pieces, half, fresh):
    rows, width = pieces[0].shape
    return call(
        place_qkv_kernel,
        1,
        (1,),
        [full((rows, width))] * 4,
        [full((width, half)), full((width, half)), full((fresh, width))],
        [shape_of((width, half), F32), shape_of((width, half), F32), shape_of((fresh, width), F32)],
        micros=4,
        name="place_qkv",
    )(ids, *pieces)


def tie(value, *others):
    return lax.optimization_barrier((value,) + others)[0]


def per_device(
    sizes,
    layer_in,
    skip_values,
    block_slot,
    doc_lengths,
    gain_attention,
    shift_attention,
    query_weight,
    query_bias,
    key_weight,
    value_weight,
    value_bias,
    out_weight,
    out_bias,
    gain_feed,
    shift_feed,
    up_weight,
    up_bias,
    down_weight,
    down_bias,
    out_grad,
):
    seq_count, tp_count = sizes
    width = layer_in.shape[1]
    half = query_weight.shape[1]
    fresh = value_weight.shape[1]
    units = up_weight.shape[1]
    tokens = layer_in.shape[0]
    batch = skip_values.shape[0] // BLOCK
    heads = width // HEAD
    head_rows = -(-heads // 8) * 8
    packed = 2 * half + fresh
    side = units // 2
    seq_index = lax.axis_index("seq")
    tp_index = lax.axis_index("tp")
    member = seq_index % SPAN
    group = seq_index // SPAN
    core = seq_index % 2
    pair_bit = seq_index // 2 % 2
    members = [[g * SPAN + m for m in range(SPAN)] for g in range(seq_count // SPAN)]
    alike = [list(range(m, seq_count, SPAN)) for m in range(SPAN)]
    same_core = [list(range(c, seq_count, 2)) for c in range(2)]
    pieces = seq_count // SPAN
    local_seq = tp_index * (batch // tp_count) + member

    def swap_seq(value, distance):
        return lax.ppermute(value, "seq", [(i, i ^ distance) for i in range(seq_count)])

    def swap_core(value):
        return swap_seq(value, 1)

    def swap_tp(value):
        return lax.ppermute(value, "tp", [(i, i ^ 1) for i in range(tp_count)])

    def to_seqs(value):
        return lax.all_to_all(value, "seq", 0, 0, tiled=True, axis_index_groups=members)

    def either(bit, first, second):
        return jnp.where(bit == 0, first, second)

    def in_order(bit, mine, theirs):
        return either(
            bit, jnp.concatenate([mine, theirs], 0), jnp.concatenate([theirs, mine], 0)
        )

    def rows_of(value, start, count):
        return lax.dynamic_slice_in_dim(value, start, count, 0)

    def row(value):
        return value.reshape(1, -1)

    local_seq = tp_index * (batch // tp_count) + member
    slots = lax.dynamic_slice(block_slot, (group * SPAN, local_seq), (SPAN, 1))
    holders = jnp.sum(
        jnp.where(
            slots == lax.broadcasted_iota(jnp.int32, (SPAN, SPAN), 1),
            lax.broadcasted_iota(jnp.int32, (SPAN, SPAN), 0), 0,
        ),
        axis=0,
    )
    lengths = lax.dynamic_slice(doc_lengths, (group * batch + local_seq, 0), (1, DOCS))
    ends = jnp.sum(
        jnp.where(
            lax.broadcasted_iota(jnp.int32, (DOCS, DOCS), 0)
            <= lax.broadcasted_iota(jnp.int32, (DOCS, DOCS), 1),
            lengths.reshape(DOCS, 1), 0,
        ),
        axis=0,
    )
    ids = jnp.concatenate(
        [jnp.stack([core, pair_bit, group]).astype(jnp.int32), holders, ends[:DOCS - 1]]
    ).astype(jnp.int32)

    qkv_own = jnp.concatenate(
        [jnp.concatenate([query_weight, key_weight], axis=1), value_weight.T], axis=0
    )
    early_sent = jnp.concatenate(
        [
            rows_of(qkv_own, core * (packed // 2), packed // 2),
            rows_of(out_weight, core * (half // 2), half // 2),
        ],
        0,
    )
    early_near = swap_tp(early_sent)
    layer_in, skip_values = lax.optimization_barrier((layer_in, skip_values, early_sent))[:2]
    blocks_in = to_seqs(layer_in.reshape(SPAN, BLOCK, width))
    skip_split = skip_values.T.reshape(fresh, batch, BLOCK).transpose(1, 0, 2)
    skip_split = skip_split.reshape(tp_count, batch // tp_count, fresh, BLOCK)
    skip_mine = lax.dynamic_index_in_dim(skip_split, tp_index, 0, keepdims=False)
    skip_theirs = swap_tp(lax.dynamic_index_in_dim(skip_split, 1 - tp_index, 0, keepdims=False))
    up_bias_half = rows_of(up_bias, core * side, side)
    bias_own = jnp.concatenate([query_bias, value_bias, up_bias_half])
    bias_other = swap_tp(bias_own)
    feed_own = jnp.concatenate(
        [lax.dynamic_slice_in_dim(up_weight, core * side, side, 1).T,
         rows_of(down_weight, core * side, side)], 0,
    )
    feed_own, ids = lax.optimization_barrier((feed_own, ids))
    early_near, skip_theirs, bias_other = lax.optimization_barrier(
        (early_near, skip_theirs, bias_other, feed_own)
    )[:3]
    early_far = swap_core(early_near)
    up_part = rows_of(feed_own, group % 2 * (side // 2), side // 2)
    up_near = swap_tp(tie(up_part, early_near))
    down_sent = tie(feed_own[side:], early_near)

    qkv_bias = jnp.stack([bias_own[:half + fresh], bias_other[:half + fresh]])
    own_shape = (SPAN, BLOCK, width)
    flat = (tokens, width)

    norm_one, queries, keys, fresh_values, qkv_other, out_other = call(
        project_kernel,
        1,
        (SPAN,),
        [
            placed(width), full((packed, width)), full((packed // 2 + half // 2, width)),
            full((packed // 2 + half // 2, width)), full((2, half + fresh)), full((width,)), full((width,)),
        ],
        [
            placed(width), in_rows(width), in_rows(width),
            pl.BlockSpec((2, BLOCK, fresh), lambda p, *_: (0, p, 0)), full((packed, width)),
            full((half, width)),
        ],
        [
            shape_of(own_shape, BF16), shape_of(flat, BF16), shape_of(flat, BF16),
            shape_of((2, tokens, fresh), BF16), shape_of((packed, width), BF16),
            shape_of((half, width), BF16),
        ],
        micros=9,
        name="project",
    )(ids, blocks_in, qkv_own, early_near, early_far, qkv_bias, gain_attention, shift_attention)

    skip_blocks = to_seqs(
        tie(jnp.concatenate([skip_mine, skip_theirs], axis=1), blocks_in)
    )
    grad_blocks = to_seqs(tie(out_grad.reshape(SPAN, BLOCK, width), skip_blocks))
    up_near = tie(up_near, queries)
    up_far = swap_seq(up_near, SPAN)
    down_other = swap_tp(down_sent)
    lse_spec = pl.BlockSpec((head_rows, BLOCK), lambda p, *_: (0, p))
    values, attended, log_total, middle, norm_two = call(
        attend_kernel,
        1,
        (SPAN,),
        [
            placed(width), in_rows(width), full(flat),
            pl.BlockSpec((2, BLOCK, fresh), lambda p, *_: (0, p, 0)), placed(BLOCK, 2 * fresh),
            full((half, width)), full((half, width)), full((width,)), full((width,)),
            full((width,)),
        ],
        [full(flat), placed(width), lse_spec, placed(width), placed(width)],
        [
            shape_of(flat, BF16), shape_of(own_shape, BF16), shape_of((head_rows, tokens), F32),
            shape_of(own_shape, F32), shape_of(own_shape, BF16),
        ],
        scratch=[pltpu.VMEM((BLOCK, width), BF16), pltpu.VMEM((BLOCK, 128), F32)],
        micros=27,
        name="attend",
    )(
        ids, blocks_in, queries, keys, fresh_values, skip_blocks, out_weight, out_other,
        out_bias, gain_feed, shift_feed,
    )
    rows_mine = norm_two.reshape(flat)
    grads_mine = grad_blocks.reshape(flat)

    rows_theirs = swap_core(rows_mine)
    grads_theirs = swap_core(grads_mine)
    feed_other = (up_near, up_far, down_other)
    bias_here = row(up_bias_half)
    bias_there = row(bias_other[half + fresh:])
    out_mine, back_mine, bias_one, made_other = feed(
        ids, rows_mine, grads_mine, feed_other, bias_there
    )
    rows_theirs = tie(rows_theirs, out_mine)
    out_theirs, back_theirs, bias_two, *made_other = feed(
        ids, rows_theirs, grads_theirs, feed_other, bias_there, (), (made_other,), PARTS
    )
    cross_feed = [swap_tp(made_other[0])]
    out_theirs, back_theirs, bias_three, made_own = feed(
        ids, rows_theirs, grads_theirs, (feed_own,), tie(bias_here, made_other[0]),
        (out_theirs, back_theirs),
    )
    out_given = swap_core(out_theirs)
    back_given = swap_core(back_theirs)
    cross_feed.append(swap_tp(tie(made_other[1], cross_feed[0], out_theirs)))
    out_mine, back_mine, bias_four, *made_own = feed(
        ids, rows_mine, grads_mine, (feed_own,), tie(bias_here, cross_feed[0]),
        (out_mine, back_mine), (made_own,), PARTS,
    )
    cross_feed.append(swap_tp(tie(made_other[2], cross_feed[1], out_mine)))

    def begin(groups, rows):
        kept, sent = fold(
            ids, groups,
            [lambda ids: ids[LINK] * (rows // 2), lambda ids: (1 - ids[LINK]) * (rows // 2)],
            rows // 2,
        )
        return kept, swap_seq(sent, 2)

    def inner(kept, given):
        rows = kept.shape[0] // pieces
        groups = [[(kept, None), (given, None)]]
        if pieces > 4:
            whole, = fold(ids, groups, [lambda ids: 0], kept.shape[0])
            whole = whole.reshape(pieces, rows, width)
            return [lax.all_to_all(whole, "seq", 0, 0, tiled=True, axis_index_groups=alike)]
        cut = fold(
            ids, groups,
            [lambda ids, k=k: (ids[OUTER] ^ k) * rows for k in range(pieces)], rows,
        )
        return [cut[0]] + [swap_seq(cut[k], SPAN * k) for k in range(1, pieces)]

    def outer(parts):
        if pieces > 4:
            piece = jnp.sum(parts[0].astype(F32), axis=0, keepdims=True).astype(BF16)
            spread = jnp.broadcast_to(piece, parts[0].shape)
            return [lax.all_to_all(spread, "seq", 0, 0, tiled=True, axis_index_groups=alike)]
        piece, = fold(
            ids, [[(part, None) for part in parts]], [lambda ids: 0], parts[0].shape[0]
        )
        return [piece] + [swap_seq(piece, SPAN * k) for k in range(1, pieces)]

    def joined(spread):
        if pieces > 4:
            return spread[0].reshape(-1, width)
        return join(ids, spread, [lambda ids, k=k: ids[OUTER] ^ k for k in range(pieces)])

    layer_blocks, middle_grad, att_grad, out_keep, out_send, small_two = call(
        residual_kernel,
        1,
        (SPAN,),
        [in_rows(width)] * 5
        + [
            by_block(width), by_block(width), full((half, width)), full((half, width)),
            full((width,)), full((width,)),
        ],
        [
            by_block(width), by_block(width), by_block(width),
            full((2, half // 2, width)), full((2, half // 2, width)), full((4, width)),
        ],
        [
            shape_of(own_shape, BF16), shape_of(own_shape, F32), shape_of(own_shape, BF16),
            shape_of((2, half // 2, width), BF16), shape_of((2, half // 2, width), BF16),
            shape_of((4, width), F32),
        ],
        scratch=[pltpu.VMEM((width, width), F32)],
        micros=12.5,
        name="residual",
    )(
        ids, tie(out_mine, cross_feed[1]), out_given, back_mine, back_given, grads_mine, middle, attended, out_weight,
        out_other, gain_feed, down_bias,
    )
    sent_given = swap_core(out_send)
    out_total = (out_keep.astype(F32) + sent_given.astype(F32)).astype(BF16)
    out_total = tie(out_total, cross_feed[2])
    cross_feed.append(swap_tp(tie(made_other[3], cross_feed[2])))
    cross_out = swap_tp(out_total[1])

    def attend_back(which, query_rows):
        return call(
            partial(attend_back_kernel, which * (heads // 2)),
            1,
            (SPAN,),
            [
                pl.BlockSpec((BLOCK, half), lambda p, *_: (p, which)),
                pl.BlockSpec((tokens, half), lambda p, *_: (0, which)),
                pl.BlockSpec((tokens, half), lambda p, *_: (0, which)),
                placed(half, column=which), placed(half, column=which), lse_spec,
            ],
            [full((SPAN, BLOCK, packed)), full((SPAN, fresh, BLOCK))],
            [shape_of((SPAN, BLOCK, packed), BF16), shape_of((SPAN, fresh, BLOCK), BF16)],
            scratch=[
                pltpu.VMEM((BLOCK, half), BF16), pltpu.VMEM((tokens, half), F32),
                pltpu.VMEM((tokens, half), F32), pltpu.VMEM((8, BLOCK), F32),
            ],
            micros=17.5,
            name="attend_back",
        )(
            ids, query_rows, keys, values, attended, att_grad,
            log_total,
        )

    qkv_rows = -(-packed // 128) * 64

    def weights(made):
        return call(
            weight_kernel,
            1,
            (1,),
            [full(flat), full((tokens, packed))],
            [full((qkv_rows, width)), full((qkv_rows, width)), full((1, packed))],
            [
                shape_of((qkv_rows, width), BF16), shape_of((qkv_rows, width), BF16),
                shape_of((1, packed), F32),
            ],
            scratch=[pltpu.VMEM((packed, width), F32)],
            micros=6,
            name="weights",
        )(ids, norm_one.reshape(flat), made.reshape(tokens, packed))

    layer_out = to_seqs(tie(layer_blocks, out_total)).reshape(flat)
    grads_other, skip_other = attend_back(1, tie(queries, out_total))
    cross_feed[3], cross_out = lax.optimization_barrier(
        (cross_feed[3], cross_out, grads_other)
    )[:2]
    ready_feed, = fold(
        ids,
        [[(mine, None), (theirs, None)] for mine, theirs in zip(made_own, cross_feed)]
        + [[(out_total, 0), (cross_out, None)]],
        [lambda ids: 0],
        2 * side + half // 2,
    )
    total_feed = lax.psum(ready_feed, "seq", axis_index_groups=same_core)
    keep_other, send_other, sums_other = weights(tie(grads_other, ready_feed, layer_out))
    given_other = swap_core(send_other)
    skip_theirs = swap_tp(skip_other)
    total_other, = fold(
        ids, [[(keep_other, None), (given_other, None)]], [lambda ids: 0], qkv_rows
    )
    cross_other = swap_tp(total_other)
    grads_own, skip_own = attend_back(0, tie(queries, total_other))
    keep_own, send_own, sums_own = weights(tie(grads_own, cross_other))
    given_own = swap_core(send_own)

    input_blocks, small_one = call(
        input_kernel,
        0,
        (SPAN,),
        [
            by_block(packed), by_block(packed), full((packed, width)), full((packed, width)),
            by_block(width), by_block(width), full((width,)),
        ],
        [by_block(width), full((2, width))],
        [shape_of(own_shape, BF16), shape_of((2, width), F32)],
        micros=9,
        name="input",
    )(
        tie(grads_own, keep_own), grads_other, qkv_own, qkv_other, blocks_in, middle_grad,
        gain_attention,
    )
    given_own, skip_theirs = lax.optimization_barrier((given_own, skip_theirs, input_blocks))[:2]
    kept_qkv, given_y_qkv = begin(
        [[(keep_own, None), (given_own, None), (cross_other, None)]], qkv_rows
    )
    input_blocks = tie(input_blocks, kept_qkv)
    input_back = to_seqs(input_blocks)
    shared = jnp.concatenate([small_one.reshape(-1), small_two.reshape(-1)])
    widened = lambda value: jnp.where(
        lax.broadcasted_iota(jnp.int32, (2, 1), 0) == core, value, 0.0
    ).reshape(-1)
    split_own = jnp.concatenate([sums_own.reshape(-1), widened(bias_three + bias_four)])
    split_other = jnp.concatenate([sums_other.reshape(-1), widened(bias_one + bias_two)])
    vector_own = jnp.concatenate([shared, split_own])
    vector_other = jnp.concatenate([shared, split_other])

    distances = [1 << bit for bit in range(seq_count.bit_length() - 1)]
    crossed = swap_tp(tie(vector_other, kept_qkv))

    def step(values, vectors, given):
        values = list(values)
        held = lax.optimization_barrier(tuple(values) + (vectors, given))
        return list(held[:-2]), held[-2] + held[-1]

    (given_y_qkv,), vectors = step([given_y_qkv], vector_own, crossed)
    parts_qkv = inner(kept_qkv, given_y_qkv)
    given = swap_seq(vectors, distances[0])
    parts_qkv, vectors = step(parts_qkv, vectors, given)
    spread_qkv = outer(parts_qkv)
    given = swap_seq(vectors, distances[1])
    spread_qkv, vectors = step(spread_qkv, vectors, given)
    whole_qkv = joined(spread_qkv)
    far_qkv = swap_seq(whole_qkv, 2)
    near_theirs = swap_core(whole_qkv)
    given = swap_seq(vectors, distances[2])
    (far_qkv,), vectors = step([far_qkv], vectors, given)
    far_theirs = swap_core(far_qkv)
    for distance in distances[3:]:
        vectors = vectors + swap_seq(vectors, distance)
    pieces_qkv = (whole_qkv, far_qkv, near_theirs, far_theirs)
    grad_query, grad_key, grad_value = place_qkv(ids, pieces_qkv, half, fresh)
    shared = vectors[:6 * width].reshape(6, width)
    split = vectors[6 * width:]

    input_back, skip_theirs = lax.optimization_barrier((input_back, skip_theirs))
    input_grad = input_back.reshape(flat).astype(F32)
    skip_back = to_seqs(jnp.concatenate([skip_own, skip_theirs], axis=1))
    skip_halves = skip_back.reshape(SPAN, 2, fresh, BLOCK).transpose(1, 0, 2, 3)
    skip_halves = either(tp_index, skip_halves, skip_halves[::-1])
    skip_grad = skip_halves.reshape(batch, fresh, BLOCK).transpose(1, 0, 2)
    skip_grad = skip_grad.reshape(fresh, batch * BLOCK).astype(F32).T

    total_feed = tie(total_feed, *pieces_qkv, skip_back)
    grad_up_weight, grad_down_weight, grad_out_weight = place_feed(
        ids, total_feed, swap_core(total_feed), units
    )

    return (
        layer_out,
        input_grad,
        skip_grad,
        shared[0],
        shared[1],
        grad_query,
        split[:half],
        grad_key,
        grad_value.T,
        split[2 * half:packed],
        grad_out_weight,
        shared[4],
        shared[2],
        shared[3],
        grad_up_weight,
        split[packed:],
        grad_down_weight,
        shared[5],
    )


def solution(mesh):
    return jax.shard_map(
        partial(per_device, (mesh.shape["seq"], mesh.shape["tp"])),
        mesh=mesh,
        in_specs=(
            P(("seq", "tp"), None),
            P("seq", "tp"),
            P(),
            P(),
            P(),
            P(),
            P(None, "tp"),
            P("tp"),
            P(None, "tp"),
            P(None, "tp"),
            P("tp"),
            P("tp", None),
            P(),
            P(),
            P(),
            P(None, "tp"),
            P("tp"),
            P("tp", None),
            P(),
            P(("seq", "tp"), None),
        ),
        out_specs=(
            P(("seq", "tp"), None),
            P(("seq", "tp"), None),
            P("seq", "tp"),
            P(),
            P(),
            P(None, "tp"),
            P("tp"),
            P(None, "tp"),
            P(None, "tp"),
            P("tp"),
            P("tp", None),
            P(),
            P(),
            P(),
            P(None, "tp"),
            P("tp"),
            P("tp", None),
            P(),
        ),
        check_vma=False,
    )
```

time: 602 us -> 387 us (0.64)
  waiting for transfers between devices: 258 us -> 72 us
  Pallas kernels: 148 us -> 189 us
  starting transfers between devices: 96 us -> 63.4 us
  other arithmetic: 42.5 us -> 13.2 us
  local copies, waits for them, and re-layouts: 50.8 us -> 28.2 us
  between operations: 1.56 us -> 15 us
    ppermute x12 -> x13, waiting for transfers between devices: 139 us -> 19.8 us  [swap_tp(): return lax.ppermute(value, 'tp', [(i, i ^ 1) for i in range(tp_count)])]
    all_to_all x8 -> x0, waiting for transfers between devices: 77.4 us -> none  [the longest x4 48.1 us: across(): lax.all_to_all(spread, 'seq', 0, 0, tiled=True, axis_index_groups=same_core)]
    pallas_call x8 -> x20, Pallas kernels: 148 us -> 189 us  [the longest x4 53.4 us: feed(): call(partial(feed_kernel, len(weights) > 1, len(sums) > 0, len(made) > 0)...]
    all_to_all x8 -> x0, starting transfers between devices: 39.1 us -> none  [the longest x4 21.8 us: across(): lax.all_to_all(split, 'seq', 0, 0, tiled=True, axis_index_groups=same_core)]
    convert_element_type x12 -> x2, other arithmetic: 30.1 us -> 3.23 us  [the longest x1 2 us: per_device(): input_grad = input_back.reshape(flat).astype(F32)]
    all_to_all x6, waiting for transfers between devices: 34.2 us -> 7.51 us  [to_seqs(): lax.all_to_all(value, 'seq', 0, 0, tiled=True, axis_index_groups=members)]
    ppermute x18 -> x24, waiting for transfers between devices: 7.22 us -> 31.8 us  [swap_seq(): lax.ppermute(value, 'seq', [(i, i ^ distance) for i in range(seq_count)])]
    psum x0 -> x1, waiting for transfers between devices: none -> 13 us  [per_device(): total_feed = lax.psum(ready_feed, 'seq', axis_index_groups=same_core)]
  transfers between devices with their start and end apart: 44 -> 44, of which waited for: 21 -> 16; matrix products, arithmetic and copies ran while one was open for 13% -> 7% of each run, Pallas kernels for 18% -> 43%
where the time goes in v2:
time: 387 us; the launch traced here: 381 us
  Pallas kernels  189 us (49%)
  waiting for transfers between devices  72 us (19%)
  starting transfers between devices  63.4 us (16%)
  local copies, waits for them, and re-layouts  28.2 us (7%)
  between operations  15 us (4%)
  other arithmetic  13.2 us (3%)
    pallas_call x4, Pallas kernels, feed(): call(partial(feed_kernel, len(weights) > 1, len(sums) > 0, len(made) > 0)...  53.4 us
    pallas_call x2, Pallas kernels, attend_back(): call(partial(attend_back_kernel, which * (heads // 2)), 1, (SPAN,), [pl.B...  35.2 us
    ppermute x24, waiting for transfers between devices, swap_seq(): lax.ppermute(value, 'seq', [(i, i ^ distance) for i in range(seq_count)])  31.8 us
    pallas_call x1, Pallas kernels, per_device(): call(attend_kernel, 1, (SPAN,), [placed(width), in_rows(width), full(flat...  26.6 us
    all_to_all x6, starting transfers between devices, to_seqs(): lax.all_to_all(value, 'seq', 0, 0, tiled=True, axis_index_groups=members)  23.7 us
    ppermute x13, starting transfers between devices, swap_tp(): return lax.ppermute(value, 'tp', [(i, i ^ 1) for i in range(tp_count)])  20.7 us
    ppermute x13, waiting for transfers between devices, swap_tp(): return lax.ppermute(value, 'tp', [(i, i ^ 1) for i in range(tp_count)])  19.8 us
    ppermute x24, starting transfers between devices, swap_seq(): lax.ppermute(value, 'seq', [(i, i ^ distance) for i in range(seq_count)])  19 us
  transfers between devices with their start and end apart: 44, of which 16 were waited for; matrix products, arithmetic and copies ran while one was open for 7% of the time, Pallas kernels for 43%

profile of v2, /device:TPU:0, one launch (start us, length us, event | category | flops | bytes accessed | tf_op | source)
XLA Modules:
  0.0 381.3 jit_solution(7126807344296231897)
XLA Ops:
  14.8 4.5 %all-to-all-start = ((bf16[4,256,768]{2,1,0:T(8,128)(2,1)}), bf16[4,256,768]{2,1,0:T(8,128)(2,1)}, u32[]{:S(2)}, u32[]{:S(2)}) async-start(bf16[4,256,768]{2,1,0:T(8,128)(2,1)} %bitcast.6), calls=%async_computation | async-start | bytes 3145728 | tf_op jit(solution)/shard_map/all_to_all | solution.py:648
  28.5 9.6 %collective-permute-done.2 = f32[1344]{0:T(1024)} collective-permute-done((f32[1344]{0:T(1024)}, f32[1344]{0:T(1024)}, u32[]{:S(2)}, u32[]{:S(2)}) %collective-permute-start.2) | collective-permute-done | bytes 5408 | tf_op jit(solution)/shard_map/ppermute | solution.py:645
  38.2 7.6 %collective-permute-done.1 = bf16[4,192,256]{2,1,0:T(8,128)(2,1)} collective-permute-done((bf16[4,192,256]{2,1,0:T(8,128)(2,1)}, bf16[4,192,256]{2,1,0:T(8,128)(2,1)}, u32[]{:S(2)}, u32[]{:S(2)}) %collective-permute-start.1) | collective-permute-done | bytes 393248 | tf_op jit(solution)/shard_map/ppermute | solution.py:645
  56.4 7.5 %all-to-all-done.1.skip_ref = bf16[4,384,256]{2,1,0:T(8,128)(2,1)} async-done(((bf16[4,384,256]{2,1,0:T(8,128)(2,1)}), bf16[4,384,256]{2,1,0:T(8,128)(2,1)}, u32[]{:S(2)}, u32[]{:S(2)}) %all-to-all-start.1) | async-done | bytes 786464 | tf_op jit(solution)/shard_map/all_to_all | solution.py:648
  67.4 9.7 %project.1 = (bf16[4,256,768]{2,1,0:T(8,128)(2,1)}, bf16[1024,768]{1,0:T(8,128)(2,1)}, bf16[1024,768]{1,0:T(8,128)(2,1)}, bf16[2,1024,192]{2,1,0:T(8,128)(2,1)},...) custom-call(s32[10]{0:T(128)} %concatenate.37.ids, bf16[4,256,768]{2,1,0:T(8,128)(2,1)} %all-to-all-done.x_ref, ...), custom_call_target="tpu_custom_call" | custom-call | flops 10350000128 | bytes 10350000 | tf_op jit(solution)/shard_map/project/pallas_call | solution.py:723
  79.0 26.6 %attend.1 = (bf16[1024,768]{1,0:T(8,128)(2,1)}, bf16[4,256,768]{2,1,0:T(8,128)(2,1)}, f32[16,1024]{1,0:T(8,128)}, f32[4,256,768]{2,1,0:T(8,128)}, bf16[4,256,768]{2,1,0:T(8,128)(2,1)}) custom-call(s32[10]{0:T(128)} %concatenate.37.ids, bf16[4,256,768]{2,1,0:T(8,128)(2,1)} %all-to-all-done.x_ref, bf16[1024,768]{1,0:T(8,128)(2,1)} %get-tuple-element.194.q_ref, ...), custom_call_target="tpu_custom_call" | custom-call | flops 31050000384 | bytes 31050000 | tf_op jit(solution)/shard_map/attend/pallas_call | solution.py:753
  108.3 12.5 %feed.4 = (bf16[1024,768]{1,0:T(8,128)(2,1)}, bf16[1024,768]{1,0:T(8,128)(2,1)}, f32[1,768]{1,0:T(1,128)}, bf16[1536,768]{1,0:T(8,128)(2,1)}) custom-call(s32[10]{0:T(128)} %concatenate.37.ids, bf16[1024,768]{1,0:T(8,128)(2,1)} %bitcast.64, bf16[1024,768]{1,0:T(8,128)(2,1)} %bitcast.54, bf16[384,768]{1,0:T(8,128)(2,1)} %copy-done.32, ...), custom_call_target="tpu_custom_call" | custom-call | flops 16099999744 | bytes 16100000 | tf_op jit(solution)/shard_map/feed/pallas_call | solution.py:280
  122.0 13.2 %feed.5 = (bf16[1024,768]{1,0:T(8,128)(2,1)}, bf16[1024,768]{1,0:T(8,128)(2,1)}, f32[1,768]{1,0:T(1,128)}, bf16[384,768]{1,0:T(8,128)(2,1)}, bf16[384,768]{1,0:T...) custom-call(s32[10]{0:T(128)} %concatenate.37.ids, bf16[1024,768]{1,0:T(8,128)(2,1)} %collective-permute-done.4.refs_0_, ...), custom_call_target="tpu_custom_call" | custom-call | flops 16099999744 | bytes 16100000 | tf_op jit(solution)/shard_map/feed/pallas_call | solution.py:280
  138.6 13.6 %feed.6 = (bf16[1024,768]{1,0:T(8,128)(2,1)}, bf16[1024,768]{1,0:T(8,128)(2,1)}, f32[1,768]{1,0:T(1,128)}, bf16[1536,768]{1,0:T(8,128)(2,1)}) custom-call(s32[10]{0:T(128)} %concatenate.37.ids, bf16[1024,768]{1,0:T(8,128)(2,1)} %collective-permute-done.4.refs_0_, bf16[1024,768]{1,0:T(8,128)(2,1)} %copy-done.26, bf16[1536,768]{1,0:T(8,128)(2,1)} %copy-done.2, ...), custom_call_target="tpu_custom_call" | custom-call | flops 16099999744 | bytes 16100000 | tf_op jit(solution)/shard_map/feed/pallas_call | solution.py:280
  154.2 14.0 %feed.7 = (bf16[1024,768]{1,0:T(8,128)(2,1)}, bf16[1024,768]{1,0:T(8,128)(2,1)}, f32[1,768]{1,0:T(1,128)}, bf16[384,768]{1,0:T(8,128)(2,1)}, bf16[384,768]{1,0:T...) custom-call(s32[10]{0:T(128)} %concatenate.37.ids, bf16[1024,768]{1,0:T(8,128)(2,1)} %bitcast.65, ...), custom_call_target="tpu_custom_call" | custom-call | flops 16099999744 | bytes 16100000 | tf_op jit(solution)/shard_map/feed/pallas_call | solution.py:280
  170.6 12.9 %residual.1 = (bf16[4,256,768]{2,1,0:T(8,128)(2,1)}, f32[4,256,768]{2,1,0:T(8,128)}, bf16[4,256,768]{2,1,0:T(8,128)(2,1)}, bf16[2,192,768]{2,1,0:T(8,128)(2,1)},...) custom-call(s32[10]{0:T(128)} %concatenate.37.ids, bf16[1024,768]{1,0:T(8,128)(2,1)} %get-tuple-element.165.out_a, ...), custom_call_target="tpu_custom_call" | custom-call | flops 14375000064 | bytes 14375000 | tf_op jit(solution)/shard_map/residual/pallas_call | solution.py:840
  192.9 17.6 %attend_back.2 = (bf16[4,256,960]{2,1,0:T(8,128)(2,1)}, bf16[4,192,256]{2,1,0:T(8,128)(2,1)}) custom-call(s32[10]{0:T(128)} %concatenate.37.ids, bf16[1024,768]{1,0:T(8,128)(2,1)} %get-tuple-element.194.q_ref, bf16[1024,768]{1,0:T(8,128)(2,1)} %get-tuple-element.141.k_ref, bf16[1024,768]{1,0:T(8,128)(2,1)} %get-tuple-element.179.v_ref, ...), custom_call_target="tpu_custom_call" | custom-call | flops 20124999680 | bytes 20125000 | tf_op jit(solution)/shard_map/attend_back/pallas_call | solution.py:872
  211.2 5.3 %fold.5 = bf16[1728,768]{1,0:T(8,128)(2,1)} custom-call(s32[10]{0:T(128)} %concatenate.37.ids, bf16[384,768]{1,0:T(8,128)(2,1)} %get-tuple-element.183.refs_0_, bf16[384,768]{1,0:T(8,128)(2,1)} %copy-done.31, bf16[384,768]{1,0:T(8,128)(2,1)} %get-tuple-element.184.refs_2_, bf16[384,768]{1,0:T(8,128)(2,1)} %copy-done.33, ...), custom_call_target="tpu_custom_call" | custom-call | flops 4024999936 | bytes 4025000 | tf_op jit(solution)/shard_map/fold/pallas_call | solution.py:490
  216.6 5.8 %weights.2 = (bf16[512,768]{1,0:T(8,128)(2,1)}, bf16[512,768]{1,0:T(8,128)(2,1)}, f32[1,960]{1,0:T(1,128)}) custom-call(s32[10]{0:T(128)} %concatenate.37.ids, bf16[1024,768]{1,0:T(8,128)(2,1)} %bitcast.68, bf16[1024,960]{1,0:T(8,128)(2,1)} %bitcast.66), custom_call_target="tpu_custom_call" | custom-call | flops 6899999744 | bytes 6900000 | tf_op jit(solution)/shard_map/weights/pallas_call | solution.py:898
  231.1 17.7 %attend_back.3 = (bf16[4,256,960]{2,1,0:T(8,128)(2,1)}, bf16[4,192,256]{2,1,0:T(8,128)(2,1)}) custom-call(s32[10]{0:T(128)} %concatenate.37.ids, bf16[1024,768]{1,0:T(8,128)(2,1)} %get-tuple-element.194.q_ref, bf16[1024,768]{1,0:T(8,128)(2,1)} %get-tuple-element.141.k_ref, bf16[1024,768]{1,0:T(8,128)(2,1)} %get-tuple-element.179.v_ref, ...), custom_call_target="tpu_custom_call" | custom-call | flops 20124999680 | bytes 20125000 | tf_op jit(solution)/shard_map/attend_back/pallas_call | solution.py:872
  251.3 5.7 %weights.3 = (bf16[512,768]{1,0:T(8,128)(2,1)}, bf16[512,768]{1,0:T(8,128)(2,1)}, f32[1,960]{1,0:T(1,128)}) custom-call(s32[10]{0:T(128)} %concatenate.37.ids, bf16[1024,768]{1,0:T(8,128)(2,1)} %bitcast.69, bf16[1024,960]{1,0:T(8,128)(2,1)} %bitcast.67), custom_call_target="tpu_custom_call" | custom-call | flops 6899999744 | bytes 6900000 | tf_op jit(solution)/shard_map/weights/pallas_call | solution.py:898
  257.0 9.1 %input.1 = (bf16[4,256,768]{2,1,0:T(8,128)(2,1)}, f32[2,768]{1,0:T(2,128)}) custom-call(bf16[4,256,960]{2,1,0:T(8,128)(2,1)} %get-tuple-element.198.own_ref, bf16[4,256,960]{2,1,0:T(8,128)(2,1)} %get-tuple-element.191.other_ref, bf16[960,768]{1,0:T(8,128)(2,1)} %copy-done.3, bf16[960,768]{1,0:T(8,128)(2,1)} %get-tuple-element.199.w_other_ref, ...), custom_call_target="tpu_custom_call" | custom-call | flops 10350000128 | bytes 10350000 | tf_op jit(solution)/shard_map/input/pallas_call | solution.py:937
  279.7 4.4 %collective-permute-done.21.refs_1_ = bf16[256,768]{1,0:T(8,128)(2,1)} collective-permute-done((bf16[256,768]{1,0:T(8,128)(2,1)}, bf16[256,768]{1,0:T(8,128)(2,1)}, u32[]{:S(2)}, u32[]{:S(2)}) %collective-permute-start.21) | collective-permute-done | bytes 393248 | tf_op jit(solution)/shard_map/ppermute | solution.py:639
  294.8 6.9 %collective-permute-done.24.refs_2_ = bf16[64,768]{1,0:T(8,128)(2,1)S(1)} collective-permute-done((bf16[64,768]{1,0:T(8,128)(2,1)}, bf16[64,768]{1,0:T(8,128)(2,1)S(1)}, u32[]{:S(2)}, u32[]{:S(2)}) %collective-permute-start.24) | collective-permute-done | bytes 98336 | tf_op jit(solution)/shard_map/ppermute | solution.py:639
  321.9 4.3 %all-to-all-start.5 = ((bf16[4,384,256]{2,1,0:T(8,128)(2,1)}), bf16[4,384,256]{2,1,0:T(8,128)(2,1)}, u32[]{:S(2)}, u32[]{:S(2)}) async-start(bf16[4,384,256]{2,1,0:T(8,128)(2,1)} %pad_maximum_fusion.4), calls=%async_computation.5 | async-start | bytes 1572864 | tf_op jit(solution)/shard_map/all_to_all | solution.py:648
  327.7 4.6 %collective-permute-done.32 = f32[7104]{0:T(1024)S(1)} collective-permute-done((f32[7104]{0:T(1024)S(1)}, f32[7104]{0:T(1024)S(1)}, u32[]{:S(2)}, u32[]{:S(2)}) %collective-permute-start.32) | collective-permute-done | bytes 28448 | tf_op jit(solution)/shard_map/ppermute | solution.py:639
  336.4 13.0 %all-reduce.2.cloned.1.call-done.mine_ref = bf16[1728,768]{1,0:T(8,128)(2,1)} async-done(((bf16[1728,768]{1,0:T(8,128)(2,1)}), bf16[1728,768]{1,0:T(8,128)(2,1)}) %all-reduce.2.cloned.1.call-update) | async-done | bytes 2654224 | tf_op jit(solution)/shard_map/psum | solution.py:925
  350.2 4.2 %collective-permute-done.33 = f32[7104]{0:T(1024)S(1)} collective-permute-done((f32[7104]{0:T(1024)S(1)}, f32[7104]{0:T(1024)S(1)}, u32[]{:S(2)}, u32[]{:S(2)}) %collective-permute-start.33) | collective-permute-done | bytes 28448 | tf_op jit(solution)/shard_map/ppermute | solution.py:639
  365.5 7.6 %place_feed.1 = (f32[768,1536]{1,0:T(8,128)}, f32[1536,768]{1,0:T(8,128)}, f32[384,768]{1,0:T(8,128)}) custom-call(s32[10]{0:T(128)} %concatenate.37.ids, bf16[1728,768]{1,0:T(8,128)(2,1)} %all-reduce.2.cloned.1.call-done.mine_ref, bf16[1728,768]{1,0:T(8,128)(2,1)} %collective-permute-done.36.theirs_ref), custom_call_target="tpu_custom_call" | custom-call | flops 9200000000 | bytes 9200000 | tf_op jit(solution)/shard_map/place_feed/pallas_call | solution.py:542
  (230 shorter events, 128.3 us)
Async XLA Ops:
  11.1 34.7 %collective-permute-start = (bf16[672,768]{1,0:T(8,128)(2,1)}, bf16[672,768]{1,0:T(8,128)(2,1)}, u32[]{:S(2)}, u32[]{:S(2)}) collective-permute-start(bf16[672,768]{1,0:T(8,128)(2,1)} %pad_maximum_fusion.2), channel_id=1, source_target_pairs={{0,1},{1,0},{2,3},{3,2},{4,5},{5,4},{6,7},{7,6},{8,9},{9,8},{10,11... | collective-permute-start | bytes 3096584 | tf_op jit(solution)/shard_map/ppermute | solution.py:645
  14.8 23.4 %collective-permute-start.2 = (f32[1344]{0:T(1024)}, f32[1344]{0:T(1024)}, u32[]{:S(2)}, u32[]{:S(2)}) collective-permute-start(f32[1344]{0:T(1024)} %concatenate.41), channel_id=1, source_target_pairs={{0,1},{1,0},{2,3},{3,2},{4,5},{5,4},{6,7},{7,6},{8,9},{9,8},{10,11... | collective-permute-start | bytes 16136 | tf_op jit(solution)/shard_map/ppermute | solution.py:645
  14.8 33.0 %all-to-all-start = ((bf16[4,256,768]{2,1,0:T(8,128)(2,1)}), bf16[4,256,768]{2,1,0:T(8,128)(2,1)}, u32[]{:S(2)}, u32[]{:S(2)}) async-start(bf16[4,256,768]{2,1,0:T(8,128)(2,1)} %bitcast.6), calls=%async_computation | async-start | bytes 3145728 | tf_op jit(solution)/shard_map/all_to_all | solution.py:648
  20.6 25.2 %collective-permute-start.1 = (bf16[4,192,256]{2,1,0:T(8,128)(2,1)}, bf16[4,192,256]{2,1,0:T(8,128)(2,1)}, u32[]{:S(2)}, u32[]{:S(2)}) collective-permute-start(bf16[4,192,256]{2,1,0:T(8,128)(2,1)} %get-tuple-element.251), channel_id=1, source_target_pairs={{0,1},{1,0},{2,3},{3,2},{4,5},{5,4},{6,7},{7,6},{8,9},{9,8},{10,11... | collective-permute-start | bytes 1179656 | tf_op jit(solution)/shard_map/ppermute | solution.py:645
  45.8 21.7 %collective-permute-start.3 = (bf16[672,768]{1,0:T(8,128)(2,1)}, bf16[672,768]{1,0:T(8,128)(2,1)}, u32[]{:S(2)}, u32[]{:S(2)}) collective-permute-start(bf16[672,768]{1,0:T(8,128)(2,1)} %collective-permute-done.near_ref), channel_id=1, source_target_pairs={{0,2},{2,0},{4,6},{6,4},{8,10},{10,8},{12,14},{14,12},{16,18},{18,... | collective-permute-start | bytes 3096584 | tf_op jit(solution)/shard_map/ppermute | solution.py:639
  47.8 16.0 %all-to-all-start.1 = ((bf16[4,384,256]{2,1,0:T(8,128)(2,1)}), bf16[4,384,256]{2,1,0:T(8,128)(2,1)}, u32[]{:S(2)}, u32[]{:S(2)}) async-start(bf16[4,384,256]{2,1,0:T(8,128)(2,1)} %pad_maximum_fusion.3), calls=%async_computation.1 | async-start | bytes 1572864 | tf_op jit(solution)/shard_map/all_to_all | solution.py:648
  53.7 23.4 %collective-permute-start.5 = (bf16[384,768]{1,0:T(8,128)(2,1)}, bf16[384,768]{1,0:T(8,128)(2,1)S(1)}, u32[]{:S(2)}, u32[]{:S(2)}) collective-permute-start(bf16[384,768]{1,0:T(8,128)(2,1)} %constant_dynamic-slice_fusion), channel_id=1, source_target_pairs={{0,1},{1,0},{2,3},{3,2},{4,5},{5,4},{6,7},{7,6},{8,9},{9,8},{10,11... | collective-permute-start | bytes 1769480 | tf_op jit(solution)/shard_map/ppermute | solution.py:645
  55.5 52.8 %collective-permute-start.7 = (bf16[768,768]{1,0:T(8,128)(2,1)S(1)}, bf16[768,768]{1,0:T(8,128)(2,1)}, u32[]{:S(2)}, u32[]{:S(2)}) collective-permute-start(bf16[768,768]{1,0:T(8,128)(2,1)S(1)} %slice.63), channel_id=1, source_target_pairs={{0,1},{1,0},{2,3},{3,2},{4,5},{5,4},{6,7},{7,6},{8,9},{9,8},{10,11... | collective-permute-start | bytes 3538952 | tf_op jit(solution)/shard_map/ppermute | solution.py:645
  63.9 41.9 %all-to-all-start.2 = ((bf16[4,256,768]{2,1,0:T(8,128)(2,1)}), bf16[4,256,768]{2,1,0:T(8,128)(2,1)S(1)}, u32[]{:S(2)}, u32[]{:S(2)}) async-start(bf16[4,256,768]{2,1,0:T(8,128)(2,1)} %bitcast.52), calls=%async_computation.2 | async-start | bytes 3145728 | tf_op jit(solution)/shard_map/all_to_all | solution.py:648
  77.1 31.1 %collective-permute-start.6 = (bf16[384,768]{1,0:T(8,128)(2,1)S(1)}, bf16[384,768]{1,0:T(8,128)(2,1)}, u32[]{:S(2)}, u32[]{:S(2)}) collective-permute-start(bf16[384,768]{1,0:T(8,128)(2,1)S(1)} %collective-permute-done.5.refs_2_), channel_id=1, source_target_pairs={{0,8},{2,10},{4,12},{6,14},{8,0},{10,2},{12,4},{14,6},{16,24},{18,... | collective-permute-start | bytes 1769480 | tf_op jit(solution)/shard_map/ppermute | solution.py:639
  135.2 17.6 %collective-permute-start.9 = (bf16[384,768]{1,0:T(8,128)(2,1)}, bf16[384,768]{1,0:T(8,128)(2,1)S(1)}, u32[]{:S(2)}, u32[]{:S(2)}) collective-permute-start(bf16[384,768]{1,0:T(8,128)(2,1)} %get-tuple-element.154), channel_id=1, source_target_pairs={{0,1},{1,0},{2,3},{3,2},{4,5},{5,4},{6,7},{7,6},{8,9},{9,8},{10,11... | collective-permute-start | bytes 1769480 | tf_op jit(solution)/shard_map/ppermute | solution.py:645
  152.2 16.7 %collective-permute-start.12 = (bf16[1024,768]{1,0:T(8,128)(2,1)}, bf16[1024,768]{1,0:T(8,128)(2,1)S(1)}, u32[]{:S(2)}, u32[]{:S(2)}) collective-permute-start(bf16[1024,768]{1,0:T(8,128)(2,1)} %get-tuple-element.167), channel_id=1, source_target_pairs={{0,2},{2,0},{4,6},{6,4},{8,10},{10,8},{12,14},{14,12},{16,18},{18,... | collective-permute-start | bytes 4718600 | tf_op jit(solution)/shard_map/ppermute | solution.py:639
  152.2 16.7 %collective-permute-start.11 = (bf16[1024,768]{1,0:T(8,128)(2,1)}, bf16[1024,768]{1,0:T(8,128)(2,1)S(1)}, u32[]{:S(2)}, u32[]{:S(2)}) collective-permute-start(bf16[1024,768]{1,0:T(8,128)(2,1)} %get-tuple-element.163), channel_id=1, source_target_pairs={{0,2},{2,0},{4,6},{6,4},{8,10},{10,8},{12,14},{14,12},{16,18},{18,... | collective-permute-start | bytes 4718600 | tf_op jit(solution)/shard_map/ppermute | solution.py:639
  183.6 26.9 %collective-permute-start.15 = (bf16[384,768]{1,0:T(8,128)(2,1)S(1)}, bf16[384,768]{1,0:T(8,128)(2,1)}, u32[]{:S(2)}, u32[]{:S(2)}) collective-permute-start(bf16[384,768]{1,0:T(8,128)(2,1)S(1)} %copy-done.30), channel_id=1, source_target_pairs={{0,1},{1,0},{2,3},{3,2},{4,5},{5,4},{6,7},{7,6},{8,9},{9,8},{10,11... | collective-permute-start | bytes 1769480 | tf_op jit(solution)/shard_map/ppermute | solution.py:645
  187.8 28.7 %all-to-all-start.3 = ((bf16[4,256,768]{2,1,0:T(8,128)(2,1)}), bf16[4,256,768]{2,1,0:T(8,128)(2,1)S(1)}, u32[]{:S(2)}, u32[]{:S(2)}) async-start(bf16[4,256,768]{2,1,0:T(8,128)(2,1)} %get-tuple-element.176), calls=%async_computation.3 | async-start | bytes 3145728 | tf_op jit(solution)/shard_map/all_to_all | solution.py:648
  191.4 158.0 %all-reduce.2.cloned.1.call-start = ((), (), s32[]{:S(2)}) async-start(), calls=%async_computation.6 | async-start | bytes 5308416 | tf_op jit(solution)/shard_map/psum | solution.py:925
  191.4 19.1 %collective-permute-start.16 = (bf16[192,768]{1,0:T(8,128)(2,1)S(1)}, bf16[192,768]{1,0:T(8,128)(2,1)S(1)}, u32[]{:S(2)}, u32[]{:S(2)}) collective-permute-start(bf16[192,768]{1,0:T(8,128)(2,1)S(1)} %slice_bitcast_fusion), channel_id=1, source_target_pairs={{0,1},{1,0},{2,3},{3,2},{4,5},{5,4},{6,7},{7,6},{8,9},{9,8},{10,11... | collective-permute-start | bytes 884744 | tf_op jit(solution)/shard_map/ppermute | solution.py:645
  222.5 43.6 %collective-permute-start.20 = (bf16[4,192,256]{2,1,0:T(8,128)(2,1)S(1)}, bf16[4,192,256]{2,1,0:T(8,128)(2,1)S(1)}, u32[]{:S(2)}, u32[]{:S(2)}) collective-permute-start(bf16[4,192,256]{2,1,0:T(8,128)(2,1)S(1)} %copy-done.37), channel_id=1, source_target_pairs={{0,1},{1,0},{2,3},{3,2},{4,5},{5,4},{6,7},{7,6},{8,9},{9,8},{10,11... | collective-permute-start | bytes 1179656 | tf_op jit(solution)/shard_map/ppermute | solution.py:645
  228.9 22.4 %collective-permute-start.18 = (bf16[512,768]{1,0:T(8,128)(2,1)}, bf16[512,768]{1,0:T(8,128)(2,1)S(1)}, u32[]{:S(2)}, u32[]{:S(2)}) collective-permute-start(bf16[512,768]{1,0:T(8,128)(2,1)} %fold.6), channel_id=1, source_target_pairs={{0,1},{1,0},{2,3},{3,2},{4,5},{5,4},{6,7},{7,6},{8,9},{9,8},{10,11... | collective-permute-start | bytes 2359304 | tf_op jit(solution)/shard_map/ppermute | solution.py:645
  276.1 43.9 %all-to-all-start.4 = ((bf16[4,256,768]{2,1,0:T(8,128)(2,1)}), bf16[4,256,768]{2,1,0:T(8,128)(2,1)S(1)}, u32[]{:S(2)}, u32[]{:S(2)}) async-start(bf16[4,256,768]{2,1,0:T(8,128)(2,1)} %get-tuple-element.206), calls=%async_computation.4 | async-start | bytes 3145728 | tf_op jit(solution)/shard_map/all_to_all | solution.py:648
  319.6 16.8 %collective-permute-start.31 = (bf16[256,768]{1,0:T(8,128)(2,1)}, bf16[256,768]{1,0:T(8,128)(2,1)}, u32[]{:S(2)}, u32[]{:S(2)}) collective-permute-start(bf16[256,768]{1,0:T(8,128)(2,1)} %join.1.mine), channel_id=1, source_target_pairs={{0,4},{2,6},{4,0},{6,2},{8,12},{10,14},{12,8},{14,10},{16,20},{18,... | collective-permute-start | bytes 1179656 | tf_op jit(solution)/shard_map/ppermute | solution.py:639
  321.9 27.5 %all-to-all-start.5 = ((bf16[4,384,256]{2,1,0:T(8,128)(2,1)}), bf16[4,384,256]{2,1,0:T(8,128)(2,1)}, u32[]{:S(2)}, u32[]{:S(2)}) async-start(bf16[4,384,256]{2,1,0:T(8,128)(2,1)} %pad_maximum_fusion.4), calls=%async_computation.5 | async-start | bytes 1572864 | tf_op jit(solution)/shard_map/all_to_all | solution.py:648
  327.5 21.9 %collective-permute-start.34 = (bf16[256,768]{1,0:T(8,128)(2,1)}, bf16[256,768]{1,0:T(8,128)(2,1)}, u32[]{:S(2)}, u32[]{:S(2)}) collective-permute-start(bf16[256,768]{1,0:T(8,128)(2,1)} %join.1.mine), channel_id=1, source_target_pairs={{0,2},{2,0},{4,6},{6,4},{8,10},{10,8},{12,14},{14,12},{16,18},{18,... | collective-permute-start | bytes 1179656 | tf_op jit(solution)/shard_map/ppermute | solution.py:639
  349.4 16.1 %collective-permute-start.36 = (bf16[1728,768]{1,0:T(8,128)(2,1)}, bf16[1728,768]{1,0:T(8,128)(2,1)}, u32[]{:S(2)}, u32[]{:S(2)}) collective-permute-start(bf16[1728,768]{1,0:T(8,128)(2,1)} %all-reduce.2.cloned.1.call-done.mine_ref), channel_id=1, source_target_pairs={{0,2},{2,0},{4,6},{6,4},{8,10},{10,8},{12,14},{14,12},{16,18},{18,... | collective-permute-start | bytes 7962632 | tf_op jit(solution)/shard_map/ppermute | solution.py:639
  (65 other events, 462.3 us)
Sparse Core Ops, SparseCore 0:
  224.9 124.4 all-reduce.1

commit v3 on v2

--- a/solution.py
+++ b/solution.py
@@ -21,7 +21,7 @@
 SCALE = HEAD ** (-0.5)
 DOCS = 4
 PARTS = 4
-CORE, LINK, OUTER, MEMBER = 0, 1, 2, 3
+CORE, MINE, OUTER, TP, MEMBER = 0, 1, 2, 3, 4
 BOUND = MEMBER + SPAN
 PEAK = 1.15e9
 VMEM = 56 * 1024 * 1024
@@ -142,6 +142,18 @@
         fresh_ref[side] = (value + bias_ref[side:side + 1, half:half + fresh]).astype(BF16)
 
 
+def unpacked(value):
+    return jnp.concatenate(
+        [value[:, start:start + BLOCK] for start in range(0, value.shape[1], BLOCK)], axis=0
+    ).T
+
+
+def packed_rows(value):
+    return jnp.concatenate(
+        [value[start:start + HEAD] for start in range(0, value.shape[0], HEAD)], axis=1
+    )
+
+
 def doc_start(position, bounds):
     start = jnp.zeros_like(position)
     for bound in bounds:
@@ -150,15 +162,14 @@
 
 
 def attend_kernel(
-    ids, x_ref, q_ref, k_ref, fresh_ref, skip_ref, own_ref, other_ref,
+    ids, x_ref, q_ref, k_ref, fresh_ref, skip_own_ref, skip_other_ref, own_ref, other_ref,
     bias_ref, gain_ref, shift_ref, v_ref, att_ref, lse_ref, middle_ref, norm_ref, att_s, lse_s,
 ):
     p = pl.program_id(0)
     bounds = doc_bounds(ids)
-    skipped = skip_ref[...].T
-    part = skipped.shape[1] // 2
+    skip_own, skip_other = unpacked(skip_own_ref[...]), unpacked(skip_other_ref[...])
     v_ref[pl.ds(pl.multiple_of(p * BLOCK, BLOCK), BLOCK), :] = jnp.concatenate(
-        [fresh_ref[0], skipped[:, :part], fresh_ref[1], skipped[:, part:]], axis=1
+        [fresh_ref[0], skip_own, fresh_ref[1], skip_other], axis=1
     )
     width = q_ref.shape[1]
     half = width // 2
@@ -178,7 +189,7 @@
         bias = jnp.where(seen, 0.0, MASKED)
         head_lane = lax.broadcasted_iota(jnp.int32, (1, 128), 1)
 
-        @pl.loop(0, width // PAIR)
+        @pl.loop(0, width // PAIR, unroll=3)
         def _(pair):
             lanes = pl.ds(pl.multiple_of(pair * PAIR, PAIR), PAIR)
             queries = q_ref[:, lanes]
@@ -213,7 +224,7 @@
     norm_ref[...] = (scaled * vector(gain_ref) + vector(shift_ref)).astype(BF16)
 
 
-def feed_kernel(fetched, has_sums, has_grads, ids, *refs):
+def feed_kernel(fetched, has_sums, has_grads, swapped, ids, *refs):
     norm_ref, grad_ref = refs[:2]
     if fetched:
         mine_ref, theirs_ref, down_ref, bias_ref = refs[2:6]
@@ -269,16 +280,21 @@
             part = made_refs[row // count]
             if count > units:
                 part[piece, :] = made
+            elif swapped and piece.start > 0:
+                near = made[row - piece.start:row - piece.start + count]
+                far = made[units - count - row + piece.start:units - row + piece.start]
+                part[...] = jnp.where(ids[OUTER] % 2 == 0, near, far)
             else:
                 part[...] = made[row - piece.start:row - piece.start + count]
 
 
-def feed(ids, rows, grads, weights, bias, sums=(), made=(), parts=1):
+def feed(ids, rows, grads, weights, bias, sums=(), made=(), parts=1,
+         swapped=False):
     tokens, width = rows.shape
     units = bias.shape[1]
     total = full((tokens, width))
     return call(
-        partial(feed_kernel, len(weights) > 1, len(sums) > 0, len(made) > 0),
+        partial(feed_kernel, len(weights) > 1, len(sums) > 0, len(made) > 0, swapped),
         1,
         (1,),
         [total, total] + [full(weight.shape) for weight in weights] + [full((1, units))]
@@ -376,7 +392,7 @@
         seen = (column <= row) & (column >= start)
         bias = jnp.where(seen, 0.0, MASKED)
 
-        @pl.loop(0, width // PAIR)
+        @pl.loop(0, width // PAIR, unroll=3)
         def _(pair):
             lanes = pl.ds(pl.multiple_of(pair * PAIR, PAIR), PAIR)
             queries = q_ref[:, lanes]
@@ -418,7 +434,7 @@
             made_ref[to, :, width:2 * width] = dk_s[rows, :].astype(BF16)
             value_grad = dv_s[rows, :]
             made_ref[to, :, 2 * width:] = value_grad[:, :fresh].astype(BF16)
-            skip_ref[to] = value_grad.T[fresh:, :].astype(BF16)
+            skip_ref[to] = packed_rows(value_grad.T[fresh:, :].astype(BF16))
 
 
 def weight_kernel(ids, norm_ref, made_ref, keep_ref, send_ref, sums_ref, made_s):
@@ -431,14 +447,15 @@
     near = pl.multiple_of(ids[CORE] * half, 32)
     far = pl.multiple_of(half - ids[CORE] * half, 32)
     for target, start in ((keep_ref, near), (send_ref, far)):
-        target[:half, :] = made_s[pl.ds(start, half), :].astype(BF16)
-        target[half:, :] = jnp.zeros((target.shape[0] - half, width), BF16)
+        target[...] = made_s[pl.ds(start, half), :].astype(BF16)
     sums_ref[...] = jnp.sum(grads.astype(F32), axis=0, keepdims=True)
 
 
 def input_kernel(
-    own_ref, other_ref, w_own_ref, w_other_ref, x_ref, mg_ref, gain_ref, grad_ref, small_ref
+    ids, own_ref, other_ref, w_own_ref, w_other_ref, x_ref, mg_ref, skip_own_ref, skip_other_ref,
+    gain_ref, *refs
 ):
+    grad_refs, small_ref = refs[:-1], refs[-1]
     p = pl.program_id(0)
     first = None
     for made_ref, weight in ((own_ref, w_own_ref), (other_ref, w_other_ref)):
@@ -446,7 +463,15 @@
         part = nt(made_ref[:, :width], weight[:width, :]) + nn(made_ref[:, width:], weight[width:, :])
         first = part if first is None else first + part
     scaled, inverse = normed(x_ref[...].astype(F32))
-    grad_ref[...] = (mg_ref[...] + norm_back(first, scaled, inverse, vector(gain_ref))).astype(BF16)
+    tokens, each = x_ref.shape[0], skip_own_ref.shape[0]
+    made = (mg_ref[...] + norm_back(first, scaled, inverse, vector(gain_ref))).astype(BF16)
+    for distance, grad_ref in enumerate(grad_refs):
+
+        @pl.when(p == distance)
+        def _():
+            grad_ref[:tokens, :] = made
+            grad_ref[tokens:tokens + each, :] = skip_own_ref[...]
+            grad_ref[tokens + each:, :] = skip_other_ref[...]
     sums = jnp.concatenate(
         [jnp.sum(value, axis=0, keepdims=True) for value in (first * scaled, first)], axis=0
     )
@@ -471,10 +496,16 @@
         for index in group:
             ref = refs[place]
             place += 1
-            value = (ref[...] if index is None else ref[index]).astype(F32)
+            if isinstance(index, str):
+                value = ref[...].astype(F32)
+                value = jnp.where(ids[OUTER] % 2 == int(index), value, jnp.zeros_like(value))
+            else:
+                value = (ref[...] if index is None else ref[index]).astype(F32)
             total = value if total is None else total + value
         total_s[row:row + total.shape[0], :] = total
         row += total.shape[0]
+    if row < total_s.shape[0]:
+        total_s[row:, :] = jnp.zeros((total_s.shape[0] - row, total_s.shape[1]), F32)
     for out, start in zip(outs, starts):
         at = start(ids)
         if not isinstance(at, int):
@@ -482,11 +513,11 @@
         out[...] = total_s[pl.ds(at, out.shape[0]), :].astype(BF16)
 
 
-def fold(ids, groups, starts, count):
+def fold(ids, groups, starts, count, rows=0):
     arrays = [entry[0] for group in groups for entry in group]
     indices = tuple(tuple(entry[1] for entry in group) for group in groups)
     width = arrays[0].shape[-1]
-    rows = sum(group[0][0].shape[-2] for group in groups)
+    rows = max(rows, sum(group[0][0].shape[-2] for group in groups))
     return call(
         partial(fold_kernel, indices, starts),
         1,
@@ -500,89 +531,112 @@
     )(ids, *arrays)
 
 
-def join_kernel(ends, ids, *refs):
-    for ref, end in zip(refs[:-1], ends):
-        rows = ref.shape[0]
-        refs[-1][pl.ds(pl.multiple_of(end(ids) * rows, 8), rows), :] = ref[...]
-
-
-def join(ids, pieces, ends):
-    rows, width = pieces[0].shape
-    spec = full((rows, width))
+def spread_sum_kernel(ids, parts_ref, spread_ref):
+    total = jnp.sum(parts_ref[...].astype(F32), axis=0).astype(BF16)
+    for index in range(parts_ref.shape[0]):
+        spread_ref[index] = total
+
+
+def spread_sum(ids, parts):
     return call(
-        partial(join_kernel, ends),
+        spread_sum_kernel,
         1,
         (1,),
-        [spec] * len(pieces),
-        [full((rows * len(pieces), width))],
-        [shape_of((rows * len(pieces), width), BF16)],
+        [full(parts.shape)],
+        [full(parts.shape)],
+        [shape_of(parts.shape, BF16)],
         micros=2.5,
-        name="join",
-    )(ids, *pieces)[0]
-
-
-def both_halves(ids, bit, mine, theirs):
-    first = ids[bit] == 0
-    return jnp.where(first, mine, theirs), jnp.where(first, theirs, mine)
-
-
-def place_feed_kernel(ids, mine_ref, theirs_ref, up_ref, down_ref, out_ref):
+        name="spread_sum",
+    )(ids, parts)[0]
+
+
+def collect_kernel(ids, *refs):
+    grad_ref, skip_ref = refs[-2:]
+    for distance, ref in enumerate(refs[:-2]):
+        place = ids[MINE] ^ distance
+        grad_ref[place] = ref[:BLOCK, :].astype(F32)
+        for side in range(2):
+            rows = ref[BLOCK + side * HEAD:BLOCK + (side + 1) * HEAD, :].astype(F32)
+            column = ((ids[TP] ^ side) * SPAN + place) * BLOCK
+            columns = pl.ds(pl.multiple_of(column, BLOCK), BLOCK)
+            for index in range(rows.shape[1] // BLOCK):
+                skip_ref[index * HEAD:(index + 1) * HEAD, columns] = rows[
+                    :, index * BLOCK:(index + 1) * BLOCK
+                ]
+
+
+def collect(ids, pieces):
+    rows, width = pieces[0].shape
+    features = width // BLOCK * HEAD
+    return call(
+        collect_kernel,
+        1,
+        (1,),
+        [full((rows, width))] * len(pieces),
+        [full((SPAN, BLOCK, width)), full((features, 2 * SPAN * BLOCK))],
+        [shape_of((SPAN, BLOCK, width), F32), shape_of((features, 2 * SPAN * BLOCK), F32)],
+        micros=5,
+        name="collect",
+    )(ids, *pieces)
+
+
+def place_feed_kernel(ids, mine_ref, theirs_ref, up_ref, down_ref):
     units = down_ref.shape[0]
     here = pl.program_id(0) == ids[CORE]
     whole = jnp.where(here, mine_ref[...], theirs_ref[...]).astype(F32)
     up_ref[...] = whole[:units].T
-    down_ref[...] = whole[units:2 * units]
-    out_ref[...] = whole[2 * units:]
-
-
-def place_feed(ids, mine, theirs, units):
+    down_ref[...] = whole[units:]
+
+
+def place_feed(ids, mine, theirs):
     rows, width = mine.shape
-    size = units // 2
-    out_rows = rows - 2 * size
     return call(
         place_feed_kernel,
         1,
         (2,),
         [full((rows, width))] * 2,
         [
-            pl.BlockSpec((width, size), lambda h, ids: (0, h)),
-            pl.BlockSpec((size, width), lambda h, ids: (h, 0)),
-            pl.BlockSpec((out_rows, width), lambda h, ids: (h, 0)),
-        ],
-        [
-            shape_of((width, units), F32), shape_of((units, width), F32),
-            shape_of((2 * out_rows, width), F32),
-        ],
+            pl.BlockSpec((width, rows // 2), lambda h, ids: (0, h)),
+            pl.BlockSpec((rows // 2, width), lambda h, ids: (h, 0)),
+        ],
+        [shape_of((width, rows), F32), shape_of((rows, width), F32)],
         micros=8,
         name="place_feed",
     )(ids, mine, theirs)
 
 
-def place_qkv_kernel(ids, mine, mine_far, theirs, theirs_far, q_ref, k_ref, v_ref):
+def place_qkv_kernel(ids, mine_ref, theirs_ref, q_ref, k_ref, v_ref, out_ref):
     half = q_ref.shape[1]
     split = (q_ref.shape[0] + v_ref.shape[0]) // 2
-    near = jnp.concatenate(both_halves(ids, LINK, mine[...], mine_far[...]), axis=0)
-    far = jnp.concatenate(both_halves(ids, LINK, theirs[...], theirs_far[...]), axis=0)
-    low, high = [value[:split].astype(F32) for value in both_halves(ids, CORE, near, far)]
+    half_out = out_ref.shape[0] // 2
+    first = ids[CORE] == 0
+    mine, theirs = mine_ref[...], theirs_ref[...]
+    low = jnp.where(first, mine, theirs).astype(F32)
+    high = jnp.where(first, theirs, mine).astype(F32)
+    out_ref[:half_out, :] = low[split:split + half_out]
+    out_ref[half_out:, :] = high[split:split + half_out]
     rest = q_ref.shape[0] - split
     for ref, columns in ((q_ref, slice(0, half)), (k_ref, slice(half, 2 * half))):
-        ref[:split, :] = low[:, columns]
+        ref[:split, :] = low[:split, columns]
         ref[split:, :] = high[:rest, columns]
-    v_ref[...] = high[rest:]
-
-
-def place_qkv(ids, pieces, half, fresh):
-    rows, width = pieces[0].shape
+    v_ref[...] = high[rest:split]
+
+
+def place_qkv(ids, mine, theirs, half, fresh):
+    rows, width = mine.shape
     return call(
         place_qkv_kernel,
         1,
         (1,),
-        [full((rows, width))] * 4,
-        [full((width, half)), full((width, half)), full((fresh, width))],
-        [shape_of((width, half), F32), shape_of((width, half), F32), shape_of((fresh, width), F32)],
+        [full((rows, width))] * 2,
+        [full((width, half)), full((width, half)), full((fresh, width)), full((half, width))],
+        [
+            shape_of((width, half), F32), shape_of((width, half), F32),
+            shape_of((fresh, width), F32), shape_of((half, width), F32),
+        ],
         micros=4,
         name="place_qkv",
-    )(ids, *pieces)
+    )(ids, mine, theirs)
 
 
 def tie(value, *others):
@@ -628,11 +682,9 @@
     member = seq_index % SPAN
     group = seq_index // SPAN
     core = seq_index % 2
-    pair_bit = seq_index // 2 % 2
     members = [[g * SPAN + m for m in range(SPAN)] for g in range(seq_count // SPAN)]
-    alike = [list(range(m, seq_count, SPAN)) for m in range(SPAN)]
     same_core = [list(range(c, seq_count, 2)) for c in range(2)]
-    pieces = seq_count // SPAN
+    others = seq_count // 2
     local_seq = tp_index * (batch // tp_count) + member
 
     def swap_seq(value, distance):
@@ -680,7 +732,10 @@
         axis=0,
     )
     ids = jnp.concatenate(
-        [jnp.stack([core, pair_bit, group]).astype(jnp.int32), holders, ends[:DOCS - 1]]
+        [
+            jnp.stack([core, member, group, tp_index]).astype(jnp.int32), holders,
+            ends[:DOCS - 1],
+        ]
     ).astype(jnp.int32)
 
     qkv_own = jnp.concatenate(
@@ -695,11 +750,17 @@
     )
     early_near = swap_tp(early_sent)
     layer_in, skip_values = lax.optimization_barrier((layer_in, skip_values, early_sent))[:2]
-    blocks_in = to_seqs(layer_in.reshape(SPAN, BLOCK, width))
-    skip_split = skip_values.T.reshape(fresh, batch, BLOCK).transpose(1, 0, 2)
-    skip_split = skip_split.reshape(tp_count, batch // tp_count, fresh, BLOCK)
-    skip_mine = lax.dynamic_index_in_dim(skip_split, tp_index, 0, keepdims=False)
-    skip_theirs = swap_tp(lax.dynamic_index_in_dim(skip_split, 1 - tp_index, 0, keepdims=False))
+    thirds = fresh // HEAD
+    skip_sent = skip_values.T.reshape(thirds, HEAD, tp_count, SPAN, BLOCK)
+    skip_sent = skip_sent.transpose(3, 2, 1, 0, 4).reshape(SPAN, tp_count * HEAD, thirds * BLOCK)
+    blocks_in = to_seqs(
+        jnp.concatenate([layer_in.reshape(SPAN, BLOCK, width), skip_sent], axis=1)
+    )
+    skip_other = swap_tp(
+        lax.dynamic_slice(
+            blocks_in, (0, BLOCK + (1 - tp_index) * HEAD, 0), (SPAN, HEAD, width)
+        )
+    )
     up_bias_half = rows_of(up_bias, core * side, side)
     bias_own = jnp.concatenate([query_bias, value_bias, up_bias_half])
     bias_other = swap_tp(bias_own)
@@ -708,13 +769,10 @@
          rows_of(down_weight, core * side, side)], 0,
     )
     feed_own, ids = lax.optimization_barrier((feed_own, ids))
-    early_near, skip_theirs, bias_other = lax.optimization_barrier(
-        (early_near, skip_theirs, bias_other, feed_own)
-    )[:3]
+    early_near, bias_other = lax.optimization_barrier((early_near, bias_other, feed_own))[:2]
     early_far = swap_core(early_near)
     up_part = rows_of(feed_own, group % 2 * (side // 2), side // 2)
     up_near = swap_tp(tie(up_part, early_near))
-    down_sent = tie(feed_own[side:], early_near)
 
     qkv_bias = jnp.stack([bias_own[:half + fresh], bias_other[:half + fresh]])
     own_shape = (SPAN, BLOCK, width)
@@ -742,13 +800,10 @@
         name="project",
     )(ids, blocks_in, qkv_own, early_near, early_far, qkv_bias, gain_attention, shift_attention)
 
-    skip_blocks = to_seqs(
-        tie(jnp.concatenate([skip_mine, skip_theirs], axis=1), blocks_in)
-    )
-    grad_blocks = to_seqs(tie(out_grad.reshape(SPAN, BLOCK, width), skip_blocks))
+    grad_blocks = to_seqs(tie(out_grad.reshape(SPAN, BLOCK, width), queries))
     up_near = tie(up_near, queries)
     up_far = swap_seq(up_near, SPAN)
-    down_other = swap_tp(down_sent)
+    down_other = swap_tp(tie(feed_own[side:], queries))
     lse_spec = pl.BlockSpec((head_rows, BLOCK), lambda p, *_: (0, p))
     values, attended, log_total, middle, norm_two = call(
         attend_kernel,
@@ -756,7 +811,12 @@
         (SPAN,),
         [
             placed(width), in_rows(width), full(flat),
-            pl.BlockSpec((2, BLOCK, fresh), lambda p, *_: (0, p, 0)), placed(BLOCK, 2 * fresh),
+            pl.BlockSpec((2, BLOCK, fresh), lambda p, *_: (0, p, 0)),
+            pl.BlockSpec(
+                (None, HEAD, width),
+                lambda p, ids: (member_at(p, ids), BLOCK // HEAD + ids[TP], 0),
+            ),
+            placed(width, HEAD),
             full((half, width)), full((half, width)), full((width,)), full((width,)),
             full((width,)),
         ],
@@ -769,8 +829,8 @@
         micros=27,
         name="attend",
     )(
-        ids, blocks_in, queries, keys, fresh_values, skip_blocks, out_weight, out_other,
-        out_bias, gain_feed, shift_feed,
+        ids, blocks_in, queries, keys, fresh_values, blocks_in, skip_other, out_weight,
+        out_other,        out_bias, gain_feed, shift_feed,
     )
     rows_mine = norm_two.reshape(flat)
     grads_mine = grad_blocks.reshape(flat)
@@ -785,57 +845,33 @@
     )
     rows_theirs = tie(rows_theirs, out_mine)
     out_theirs, back_theirs, bias_two, *made_other = feed(
-        ids, rows_theirs, grads_theirs, feed_other, bias_there, (), (made_other,), PARTS
-    )
-    cross_feed = [swap_tp(made_other[0])]
+        ids, rows_theirs, grads_theirs, feed_other, bias_there, (), (made_other,), PARTS, True
+    )
+    cross_one = swap_tp(made_other[0])
+    given = swap_seq(made_other[3], SPAN)
     out_theirs, back_theirs, bias_three, made_own = feed(
         ids, rows_theirs, grads_theirs, (feed_own,), tie(bias_here, made_other[0]),
         (out_theirs, back_theirs),
     )
     out_given = swap_core(out_theirs)
     back_given = swap_core(back_theirs)
-    cross_feed.append(swap_tp(tie(made_other[1], cross_feed[0], out_theirs)))
+    cross_two = swap_tp(tie(made_other[1], cross_one, out_theirs))
+    given, kept = lax.optimization_barrier((given, made_other[2], out_theirs))[:2]
+    pair_sum, = fold(ids, [[(kept, None), (given, None)]], [lambda ids: 0], kept.shape[0])
     out_mine, back_mine, bias_four, *made_own = feed(
-        ids, rows_mine, grads_mine, (feed_own,), tie(bias_here, cross_feed[0]),
+        ids, rows_mine, grads_mine, (feed_own,), tie(bias_here, cross_one, pair_sum),
         (out_mine, back_mine), (made_own,), PARTS,
     )
-    cross_feed.append(swap_tp(tie(made_other[2], cross_feed[1], out_mine)))
-
-    def begin(groups, rows):
-        kept, sent = fold(
-            ids, groups,
-            [lambda ids: ids[LINK] * (rows // 2), lambda ids: (1 - ids[LINK]) * (rows // 2)],
-            rows // 2,
-        )
-        return kept, swap_seq(sent, 2)
-
-    def inner(kept, given):
-        rows = kept.shape[0] // pieces
-        groups = [[(kept, None), (given, None)]]
-        if pieces > 4:
-            whole, = fold(ids, groups, [lambda ids: 0], kept.shape[0])
-            whole = whole.reshape(pieces, rows, width)
-            return [lax.all_to_all(whole, "seq", 0, 0, tiled=True, axis_index_groups=alike)]
-        cut = fold(
-            ids, groups,
-            [lambda ids, k=k: (ids[OUTER] ^ k) * rows for k in range(pieces)], rows,
-        )
-        return [cut[0]] + [swap_seq(cut[k], SPAN * k) for k in range(1, pieces)]
-
-    def outer(parts):
-        if pieces > 4:
-            piece = jnp.sum(parts[0].astype(F32), axis=0, keepdims=True).astype(BF16)
-            spread = jnp.broadcast_to(piece, parts[0].shape)
-            return [lax.all_to_all(spread, "seq", 0, 0, tiled=True, axis_index_groups=alike)]
-        piece, = fold(
-            ids, [[(part, None) for part in parts]], [lambda ids: 0], parts[0].shape[0]
-        )
-        return [piece] + [swap_seq(piece, SPAN * k) for k in range(1, pieces)]
-
-    def joined(spread):
-        if pieces > 4:
-            return spread[0].reshape(-1, width)
-        return join(ids, spread, [lambda ids, k=k: ids[OUTER] ^ k for k in range(pieces)])
+    cross_three = swap_tp(tie(pair_sum, cross_two, out_mine))
+
+    def scatter(value):
+        parts = value.reshape(others, value.shape[0] // others, width)
+        return lax.all_to_all(parts, "seq", 0, 0, tiled=True, axis_index_groups=same_core)
+
+    def gather(parts):
+        spread = spread_sum(ids, parts)
+        whole = lax.all_to_all(spread, "seq", 0, 0, tiled=True, axis_index_groups=same_core)
+        return whole.reshape(-1, width)
 
     layer_blocks, middle_grad, att_grad, out_keep, out_send, small_two = call(
         residual_kernel,
@@ -859,152 +895,154 @@
         micros=12.5,
         name="residual",
     )(
-        ids, tie(out_mine, cross_feed[1]), out_given, back_mine, back_given, grads_mine, middle, attended, out_weight,
+        ids, tie(out_mine, cross_two), out_given, back_mine, back_given, grads_mine, middle, attended, out_weight,
         out_other, gain_feed, down_bias,
     )
     sent_given = swap_core(out_send)
     out_total = (out_keep.astype(F32) + sent_given.astype(F32)).astype(BF16)
-    out_total = tie(out_total, cross_feed[2])
-    cross_feed.append(swap_tp(tie(made_other[3], cross_feed[2])))
-    cross_out = swap_tp(out_total[1])
-
-    def attend_back(which, query_rows):
-        return call(
-            partial(attend_back_kernel, which * (heads // 2)),
+    cross_three = tie(cross_three, att_grad)
+    ready_feed, = fold(
+        ids,
+        [
+            [(made_own[0], None), (cross_one, None)],
+            [(made_own[1], None), (cross_two, None)],
+            [(made_own[2], None), (cross_three, "0")],
+            [(made_own[3], None), (cross_three, "1")],
+        ],
+        [lambda ids: 0],
+        2 * side,
+    )
+    total_feed = lax.psum(ready_feed, "seq", axis_index_groups=same_core)
+    def rest():
+        cross_out = swap_tp(out_total[1])
+
+        def attend_back(which, query_rows):
+            return call(
+                partial(attend_back_kernel, which * (heads // 2)),
+                1,
+                (SPAN,),
+                [
+                    pl.BlockSpec((BLOCK, half), lambda p, *_: (p, which)),
+                    pl.BlockSpec((tokens, half), lambda p, *_: (0, which)),
+                    pl.BlockSpec((tokens, half), lambda p, *_: (0, which)),
+                    placed(half, column=which), placed(half, column=which), lse_spec,
+                ],
+                [full((SPAN, BLOCK, packed)), full((SPAN, HEAD, width))],
+                [shape_of((SPAN, BLOCK, packed), BF16), shape_of((SPAN, HEAD, width), BF16)],
+                scratch=[
+                    pltpu.VMEM((BLOCK, half), BF16), pltpu.VMEM((tokens, half), F32),
+                    pltpu.VMEM((tokens, half), F32), pltpu.VMEM((8, BLOCK), F32),
+                ],
+                micros=17.5,
+                name="attend_back",
+            )(
+                ids, query_rows, keys, values, attended, att_grad,
+                log_total,
+            )
+
+        qkv_rows = packed // 2
+        last_rows = -(-(qkv_rows + half // 2) // 64) * 64
+
+        def weights(made):
+            return call(
+                weight_kernel,
+                1,
+                (1,),
+                [full(flat), full((tokens, packed))],
+                [full((qkv_rows, width)), full((qkv_rows, width)), full((1, packed))],
+                [
+                    shape_of((qkv_rows, width), BF16), shape_of((qkv_rows, width), BF16),
+                    shape_of((1, packed), F32),
+                ],
+                scratch=[pltpu.VMEM((packed, width), F32)],
+                micros=6,
+                name="weights",
+            )(ids, norm_one.reshape(flat), made.reshape(tokens, packed))
+
+        layer_out = to_seqs(layer_blocks).reshape(flat)
+        grads_other, skip_made = attend_back(1, queries)
+        keep_other, send_other, sums_other = weights(tie(grads_other, cross_out))
+        given_other = swap_core(send_other)
+        total_other, = fold(
+            ids, [[(keep_other, None), (given_other, None)]], [lambda ids: 0], qkv_rows
+        )
+        cross_other = swap_tp(total_other)
+        grads_own, skip_own = attend_back(0, tie(queries, total_other, layer_out))
+        skip_theirs = swap_tp(tie(skip_made, grads_own))
+        keep_own, send_own, sums_own = weights(tie(grads_own, cross_other))
+        given_own = swap_core(send_own)
+
+        ready_qkv, = fold(
+            ids,
+            [
+                [(keep_own, None), (given_own, None), (cross_other, None)],
+                [(out_total, 0), (cross_out, None)],
+            ],
+            [lambda ids: 0],
+            last_rows,
+            last_rows,
+        )
+        parts_qkv = scatter(ready_qkv)
+        def by_distance(columns, rows=BLOCK):
+            return pl.BlockSpec((None, rows, columns), lambda p, ids: (ids[MINE] ^ p, 0, 0))
+
+        *input_blocks, small_one = call(
+            input_kernel,
             1,
             (SPAN,),
             [
-                pl.BlockSpec((BLOCK, half), lambda p, *_: (p, which)),
-                pl.BlockSpec((tokens, half), lambda p, *_: (0, which)),
-                pl.BlockSpec((tokens, half), lambda p, *_: (0, which)),
-                placed(half, column=which), placed(half, column=which), lse_spec,
+                by_distance(packed), by_distance(packed), full((packed, width)),
+                full((packed, width)), by_distance(width), by_distance(width),
+                by_distance(width, HEAD), by_distance(width, HEAD), full((width,)),
             ],
-            [full((SPAN, BLOCK, packed)), full((SPAN, fresh, BLOCK))],
-            [shape_of((SPAN, BLOCK, packed), BF16), shape_of((SPAN, fresh, BLOCK), BF16)],
-            scratch=[
-                pltpu.VMEM((BLOCK, half), BF16), pltpu.VMEM((tokens, half), F32),
-                pltpu.VMEM((tokens, half), F32), pltpu.VMEM((8, BLOCK), F32),
-            ],
-            micros=17.5,
-            name="attend_back",
+            [full((BLOCK + 2 * HEAD, width))] * SPAN + [full((2, width))],
+            [shape_of((BLOCK + 2 * HEAD, width), BF16)] * SPAN + [shape_of((2, width), F32)],
+            micros=9,
+            name="input",
         )(
-            ids, query_rows, keys, values, attended, att_grad,
-            log_total,
+            ids, tie(grads_own, ready_qkv), grads_other, qkv_own, qkv_other, blocks_in, middle_grad,
+            skip_own, skip_theirs, gain_attention,
         )
-
-    qkv_rows = -(-packed // 128) * 64
-
-    def weights(made):
-        return call(
-            weight_kernel,
-            1,
-            (1,),
-            [full(flat), full((tokens, packed))],
-            [full((qkv_rows, width)), full((qkv_rows, width)), full((1, packed))],
-            [
-                shape_of((qkv_rows, width), BF16), shape_of((qkv_rows, width), BF16),
-                shape_of((1, packed), F32),
-            ],
-            scratch=[pltpu.VMEM((packed, width), F32)],
-            micros=6,
-            name="weights",
-        )(ids, norm_one.reshape(flat), made.reshape(tokens, packed))
-
-    layer_out = to_seqs(tie(layer_blocks, out_total)).reshape(flat)
-    grads_other, skip_other = attend_back(1, tie(queries, out_total))
-    cross_feed[3], cross_out = lax.optimization_barrier(
-        (cross_feed[3], cross_out, grads_other)
+        back = [input_blocks[0]] + [
+            swap_seq(input_blocks[distance], distance) for distance in range(1, SPAN)
+        ]
+        shared = jnp.concatenate([small_one.reshape(-1), small_two.reshape(-1)])
+        widened = lambda value: jnp.where(
+            lax.broadcasted_iota(jnp.int32, (2, 1), 0) == core, value, 0.0
+        ).reshape(-1)
+        split_own = jnp.concatenate([sums_own.reshape(-1), widened(bias_three + bias_four)])
+        split_other = jnp.concatenate([sums_other.reshape(-1), widened(bias_one + bias_two)])
+        vector_own = jnp.concatenate([shared, split_own])
+        vector_other = jnp.concatenate([shared, split_other])
+
+        vectors = vector_own + swap_tp(vector_other)
+        for distance in [1] + [SPAN << bit for bit in range((seq_count // SPAN).bit_length() - 1)]:
+            vectors = vectors + swap_seq(vectors, distance)
+        parts_qkv, *back = lax.optimization_barrier((parts_qkv, vectors, *back))
+        vectors = back.pop(0)
+        return (layer_out, parts_qkv, vectors, *back)
+
+    shapes = jax.eval_shape(rest)
+    results = lax.cond(
+        jnp.min(lengths) > 0, rest, lambda: tuple(jnp.zeros(s.shape, s.dtype) for s in shapes)
+    )
+    layer_out, parts_qkv, vectors, *back = results
+    late = ids + (vectors[0] * 0.0).astype(jnp.int32)
+    whole_qkv = gather(parts_qkv)
+    total_feed = tie(total_feed, late)
+    far_feed = swap_core(total_feed)
+    input_grad, skip_grad = collect(ids, back)
+    input_grad, skip_grad = input_grad.reshape(flat), skip_grad.T
+    vectors = vectors + swap_seq(vectors, 2)
+    grad_up_weight, grad_down_weight = place_feed(late, total_feed, far_feed)
+    whole_qkv, vectors = lax.optimization_barrier(
+        (whole_qkv, vectors, grad_up_weight, input_grad, skip_grad)
     )[:2]
-    ready_feed, = fold(
-        ids,
-        [[(mine, None), (theirs, None)] for mine, theirs in zip(made_own, cross_feed)]
-        + [[(out_total, 0), (cross_out, None)]],
-        [lambda ids: 0],
-        2 * side + half // 2,
-    )
-    total_feed = lax.psum(ready_feed, "seq", axis_index_groups=same_core)
-    keep_other, send_other, sums_other = weights(tie(grads_other, ready_feed, layer_out))
-    given_other = swap_core(send_other)
-    skip_theirs = swap_tp(skip_other)
-    total_other, = fold(
-        ids, [[(keep_other, None), (given_other, None)]], [lambda ids: 0], qkv_rows
-    )
-    cross_other = swap_tp(total_other)
-    grads_own, skip_own = attend_back(0, tie(queries, total_other))
-    keep_own, send_own, sums_own = weights(tie(grads_own, cross_other))
-    given_own = swap_core(send_own)
-
-    input_blocks, small_one = call(
-        input_kernel,
-        0,
-        (SPAN,),
-        [
-            by_block(packed), by_block(packed), full((packed, width)), full((packed, width)),
-            by_block(width), by_block(width), full((width,)),
-        ],
-        [by_block(width), full((2, width))],
-        [shape_of(own_shape, BF16), shape_of((2, width), F32)],
-        micros=9,
-        name="input",
-    )(
-        tie(grads_own, keep_own), grads_other, qkv_own, qkv_other, blocks_in, middle_grad,
-        gain_attention,
-    )
-    given_own, skip_theirs = lax.optimization_barrier((given_own, skip_theirs, input_blocks))[:2]
-    kept_qkv, given_y_qkv = begin(
-        [[(keep_own, None), (given_own, None), (cross_other, None)]], qkv_rows
-    )
-    input_blocks = tie(input_blocks, kept_qkv)
-    input_back = to_seqs(input_blocks)
-    shared = jnp.concatenate([small_one.reshape(-1), small_two.reshape(-1)])
-    widened = lambda value: jnp.where(
-        lax.broadcasted_iota(jnp.int32, (2, 1), 0) == core, value, 0.0
-    ).reshape(-1)
-    split_own = jnp.concatenate([sums_own.reshape(-1), widened(bias_three + bias_four)])
-    split_other = jnp.concatenate([sums_other.reshape(-1), widened(bias_one + bias_two)])
-    vector_own = jnp.concatenate([shared, split_own])
-    vector_other = jnp.concatenate([shared, split_other])
-
-    distances = [1 << bit for bit in range(seq_count.bit_length() - 1)]
-    crossed = swap_tp(tie(vector_other, kept_qkv))
-
-    def step(values, vectors, given):
-        values = list(values)
-        held = lax.optimization_barrier(tuple(values) + (vectors, given))
-        return list(held[:-2]), held[-2] + held[-1]
-
-    (given_y_qkv,), vectors = step([given_y_qkv], vector_own, crossed)
-    parts_qkv = inner(kept_qkv, given_y_qkv)
-    given = swap_seq(vectors, distances[0])
-    parts_qkv, vectors = step(parts_qkv, vectors, given)
-    spread_qkv = outer(parts_qkv)
-    given = swap_seq(vectors, distances[1])
-    spread_qkv, vectors = step(spread_qkv, vectors, given)
-    whole_qkv = joined(spread_qkv)
-    far_qkv = swap_seq(whole_qkv, 2)
-    near_theirs = swap_core(whole_qkv)
-    given = swap_seq(vectors, distances[2])
-    (far_qkv,), vectors = step([far_qkv], vectors, given)
-    far_theirs = swap_core(far_qkv)
-    for distance in distances[3:]:
-        vectors = vectors + swap_seq(vectors, distance)
-    pieces_qkv = (whole_qkv, far_qkv, near_theirs, far_theirs)
-    grad_query, grad_key, grad_value = place_qkv(ids, pieces_qkv, half, fresh)
+    grad_query, grad_key, grad_value, grad_out_weight = place_qkv(
+        ids, whole_qkv, swap_core(whole_qkv), half, fresh
+    )
     shared = vectors[:6 * width].reshape(6, width)
     split = vectors[6 * width:]
-
-    input_back, skip_theirs = lax.optimization_barrier((input_back, skip_theirs))
-    input_grad = input_back.reshape(flat).astype(F32)
-    skip_back = to_seqs(jnp.concatenate([skip_own, skip_theirs], axis=1))
-    skip_halves = skip_back.reshape(SPAN, 2, fresh, BLOCK).transpose(1, 0, 2, 3)
-    skip_halves = either(tp_index, skip_halves, skip_halves[::-1])
-    skip_grad = skip_halves.reshape(batch, fresh, BLOCK).transpose(1, 0, 2)
-    skip_grad = skip_grad.reshape(fresh, batch * BLOCK).astype(F32).T
-
-    total_feed = tie(total_feed, *pieces_qkv, skip_back)
-    grad_up_weight, grad_down_weight, grad_out_weight = place_feed(
-        ids, total_feed, swap_core(total_feed), units
-    )
 
     return (
         layer_out,

time: 387 us -> 364 us (0.941)
  starting transfers between devices: 63.4 us -> 47.4 us
  other arithmetic: 13.2 us -> 8.46 us
    psum x1, waiting for transfers between devices: 13 us -> 1.04 us  [per_device(): total_feed = lax.psum(ready_feed, 'seq', axis_index_groups=same_core)]
    all_to_all x6 -> x3, starting transfers between devices: 23.7 us -> 12.1 us  [to_seqs(): lax.all_to_all(value, 'seq', 0, 0, tiled=True, axis_index_groups=members)]
    all_to_all x0 -> x2, waiting for transfers between devices: none -> 10.2 us  [the longest x1 10.2 us: gather(): lax.all_to_all(spread, 'seq', 0, 0, tiled=True, axis_index_groups=same_core)]
    ppermute x13 -> x12, waiting for transfers between devices: 19.8 us -> 10.7 us  [swap_tp(): return lax.ppermute(value, 'tp', [(i, i ^ 1) for i in range(tp_count)])]
    all_to_all x0 -> x2, starting transfers between devices: none -> 8.42 us  [the longest x1 4.75 us: scatter(): lax.all_to_all(parts, 'seq', 0, 0, tiled=True, axis_index_groups=same_core)]
    ppermute x13 -> x12, starting transfers between devices: 20.7 us -> 13.7 us  [swap_tp(): return lax.ppermute(value, 'tp', [(i, i ^ 1) for i in range(tp_count)])]
    pallas_call x7 -> x8, Pallas kernels: 68.7 us -> 75.1 us  [the longest x4 52.9 us: feed(): call(partial(feed_kernel, len(weights) > 1, len(sums) > 0, len(made) > 0,...]
    ppermute x24 -> x19, starting transfers between devices: 19 us -> 12.9 us  [swap_seq(): lax.ppermute(value, 'seq', [(i, i ^ distance) for i in range(seq_count)])]
  transfers between devices with their start and end apart: 44 -> 37, of which waited for: 16 -> 16; matrix products, arithmetic and copies ran while one was open for 7% -> 6% of each run, Pallas kernels for 43% -> 46%
where the time goes in v3:
time: 364 us; the launch traced here: 358 us
  Pallas kernels  188 us (52%)
  waiting for transfers between devices  68.9 us (19%)
  starting transfers between devices  47.4 us (13%)
  local copies, waits for them, and re-layouts  28.6 us (8%)
  between operations  16.4 us (5%)
  other arithmetic  8.46 us (2%)
    pallas_call x4, Pallas kernels, feed(): call(partial(feed_kernel, len(weights) > 1, len(sums) > 0, len(made) > 0,...  52.9 us
    ppermute x19, waiting for transfers between devices, swap_seq(): lax.ppermute(value, 'seq', [(i, i ^ distance) for i in range(seq_count)])  37.3 us
    pallas_call x2, Pallas kernels, attend_back(): call(partial(attend_back_kernel, which * (heads // 2)), 1, (SPAN,), [pl.B...  34.8 us
    pallas_call x1, Pallas kernels, per_device(): call(attend_kernel, 1, (SPAN,), [placed(width), in_rows(width), full(flat...  24.7 us
    pallas_call x4, Pallas kernels, fold(): call(partial(fold_kernel, indices, starts), 1, (1,), [full(array.shape) f...  14 us
    ppermute x12, starting transfers between devices, swap_tp(): return lax.ppermute(value, 'tp', [(i, i ^ 1) for i in range(tp_count)])  13.7 us
    ppermute x19, starting transfers between devices, swap_seq(): lax.ppermute(value, 'seq', [(i, i ^ distance) for i in range(seq_count)])  12.9 us
    pallas_call x1, Pallas kernels, per_device(): call(residual_kernel, 1, (SPAN,), [in_rows(width)] * 5 + [by_block(width)...  12.1 us
  transfers between devices with their start and end apart: 37, of which 16 were waited for; matrix products, arithmetic and copies ran while one was open for 6% of the time, Pallas kernels for 46%

profile of v3, /device:TPU:0, one launch (start us, length us, event | category | flops | bytes accessed | tf_op | source)
XLA Modules:
  0.0 357.8 jit_solution(2909426823817828778)
XLA Ops:
  17.9 4.6 %all-to-all-start.2 = ((bf16[4,384,768]{2,1,0:T(8,128)(2,1)}), bf16[4,384,768]{2,1,0:T(8,128)(2,1)}, u32[]{:S(2)}, u32[]{:S(2)}) async-start(bf16[4,384,768]{2,1,0:T(8,128)(2,1)} %pad_maximum_fusion.1), calls=%async_computation.2 | async-start | bytes 4718592 | tf_op jit(solution)/shard_map/all_to_all | solution.py:700
  29.9 7.5 %collective-permute-done.13 = f32[1344]{0:T(1024)} collective-permute-done((f32[1344]{0:T(1024)}, f32[1344]{0:T(1024)}, u32[]{:S(2)}, u32[]{:S(2)}) %collective-permute-start.13) | collective-permute-done | bytes 5408 | tf_op jit(solution)/shard_map/ppermute | solution.py:697
  41.4 9.7 %all-to-all-done.2.x_ref.skip_own_ref = bf16[4,384,768]{2,1,0:T(8,128)(2,1)} async-done(((bf16[4,384,768]{2,1,0:T(8,128)(2,1)}), bf16[4,384,768]{2,1,0:T(8,128)(2,1)}, u32[]{:S(2)}, u32[]{:S(2)}) %all-to-all-start.2) | async-done | bytes 2359328 | tf_op jit(solution)/shard_map/all_to_all | solution.py:700
  52.4 9.7 %project.1 = (bf16[4,256,768]{2,1,0:T(8,128)(2,1)}, bf16[1024,768]{1,0:T(8,128)(2,1)}, bf16[1024,768]{1,0:T(8,128)(2,1)}, bf16[2,1024,192]{2,1,0:T(8,128)(2,1)},...) custom-call(s32[11]{0:T(128)} %concatenate.34.ids, bf16[4,384,768]{2,1,0:T(8,128)(2,1)} %all-to-all-done.2.x_ref.skip_own_ref, ...), custom_call_target="tpu_custom_call" | custom-call | flops 10350000128 | bytes 10350000 | tf_op jit(solution)/shard_map/project/pallas_call | solution.py:781
  70.9 24.7 %attend.1 = (bf16[1024,768]{1,0:T(8,128)(2,1)}, bf16[4,256,768]{2,1,0:T(8,128)(2,1)}, f32[16,1024]{1,0:T(8,128)}, f32[4,256,768]{2,1,0:T(8,128)}, bf16[4,256,768]{2,1,0:T(8,128)(2,1)}) custom-call(s32[11]{0:T(128)S(1)} %copy-done.19, bf16[4,384,768]{2,1,0:T(8,128)(2,1)} %all-to-all-done.2.x_ref.skip_own_ref, bf16[1024,768]{1,0:T(8,128)(2,1)} %get-tuple-element.189.q_ref, ...), custom_call_target="tpu_custom_call" | custom-call | flops 31050000384 | bytes 31050000 | tf_op jit(solution)/shard_map/attend/pallas_call | solution.py:808
  98.2 12.4 %feed.4 = (bf16[1024,768]{1,0:T(8,128)(2,1)}, bf16[1024,768]{1,0:T(8,128)(2,1)}, f32[1,768]{1,0:T(1,128)S(1)}, bf16[1536,768]{1,0:T(8,128)(2,1)}) custom-call(s32[11]{0:T(128)S(1)} %copy-done.19, bf16[1024,768]{1,0:T(8,128)(2,1)} %bitcast.48, bf16[1024,768]{1,0:T(8,128)(2,1)} %bitcast.35, bf16[384,768]{1,0:T(8,128)(2,1)} %copy-done.26, ...), custom_call_target="tpu_custom_call" | custom-call | flops 16099999744 | bytes 16100000 | tf_op jit(solution)/shard_map/feed/pallas_call | solution.py:296
  111.7 13.2 %feed.5 = (bf16[1024,768]{1,0:T(8,128)(2,1)}, bf16[1024,768]{1,0:T(8,128)(2,1)}, f32[1,768]{1,0:T(1,128)S(1)}, bf16[384,768]{1,0:T(8,128)(2,1)}, bf16[384,768]{1...) custom-call(s32[11]{0:T(128)S(1)} %copy-done.19, ...), custom_call_target="tpu_custom_call" | custom-call | flops 16099999744 | bytes 16100000 | tf_op jit(solution)/shard_map/feed/pallas_call | solution.py:296
  125.7 13.4 %feed.6 = (bf16[1024,768]{1,0:T(8,128)(2,1)}, bf16[1024,768]{1,0:T(8,128)(2,1)}, f32[1,768]{1,0:T(1,128)S(1)}, bf16[1536,768]{1,0:T(8,128)(2,1)}) custom-call(s32[11]{0:T(128)S(1)} %copy-done.19, bf16[1024,768]{1,0:T(8,128)(2,1)} %collective-permute-done.16.refs_0_, bf16[1024,768]{1,0:T(8,128)(2,1)} %copy-done.22, bf16[1536,768]{1,0:T(8,128)(2,1)} %copy-done.2, ...), custom_call_target="tpu_custom_call" | custom-call | flops 16099999744 | bytes 16100000 | tf_op jit(solution)/shard_map/feed/pallas_call | solution.py:296
  146.0 13.9 %feed.7 = (bf16[1024,768]{1,0:T(8,128)(2,1)}, bf16[1024,768]{1,0:T(8,128)(2,1)}, f32[1,768]{1,0:T(1,128)S(1)}, bf16[384,768]{1,0:T(8,128)(2,1)}, bf16[384,768]{1...) custom-call(s32[11]{0:T(128)S(1)} %copy-done.19, bf16[1024,768]{1,0:T(8,128)(2,1)} %bitcast.49, ...), custom_call_target="tpu_custom_call" | custom-call | flops 16099999744 | bytes 16100000 | tf_op jit(solution)/shard_map/feed/pallas_call | solution.py:296
  162.2 12.1 %residual.1 = (bf16[4,256,768]{2,1,0:T(8,128)(2,1)}, f32[4,256,768]{2,1,0:T(8,128)}, bf16[4,256,768]{2,1,0:T(8,128)(2,1)}, bf16[2,192,768]{2,1,0:T(8,128)(2,1)},...) custom-call(s32[11]{0:T(128)S(1)} %copy-done.19, bf16[1024,768]{1,0:T(8,128)(2,1)} %get-tuple-element.216.out_a, ...), custom_call_target="tpu_custom_call" | custom-call | flops 14375000064 | bytes 14375000 | tf_op jit(solution)/shard_map/residual/pallas_call | solution.py:876
  175.2 4.9 %fold.7 = bf16[1536,768]{1,0:T(8,128)(2,1)} custom-call(s32[11]{0:T(128)S(1)} %copy-done.19, bf16[384,768]{1,0:T(8,128)(2,1)} %get-tuple-element.244.refs_0_, bf16[384,768]{1,0:T(8,128)(2,1)} %copy-done.27, bf16[384,768]{1,0:T(8,128)(2,1)} %get-tuple-element.245.refs_2_, bf16[384,768]{1,0:T(8,128)(2,1)} %copy-done.30, ...), custom_call_target="tpu_custom_call" | custom-call | flops 4024999936 | bytes 4025000 | tf_op jit(solution)/shard_map/fold/pallas_call | solution.py:521
  183.3 121.6 %conditional.1 = (bf16[1024,768]{1,0:T(8,128)(2,1)S(1)}, bf16[8,88,768]{2,1,0:T(8,128)(2,1)}, f32[7104]{0:T(1024)S(1)}, bf16[384,768]{1,0:T(8,128)(2,1)}, bf16[3...) conditional(s32[]{:T(128)} %convert_element_type.18, () %tuple.39, ...), branch_computations={%region_3.4_spmd, %region_4.5_spmd} | conditional | flops 72450031616 | bytes 138468224 | solution.py:1026
  189.8 17.2 %attend_back.2 = (bf16[4,256,960]{2,1,0:T(8,128)(2,1)}, bf16[4,64,768]{2,1,0:T(8,128)(2,1)}) custom-call(s32[11]{0:T(128)S(1)} %get-tuple-element.43.ids, bf16[1024,768]{1,0:T(8,128)(2,1)} %get-tuple-element.56.q_ref, bf16[1024,768]{1,0:T(8,128)(2,1)} %get-tuple-element.46.k_ref, bf16[1024,768]{1,0:T(8,128)(2,1)} %get-tuple-element.47.v_ref, ...), custom_call_target="tpu_custom_call" | custom-call | flops 20124999680 | bytes 20125000 | tf_op jit(solution)/shard_map/cond/branch_1_fun/attend_back/pallas_call | solution.py:920
  207.0 5.1 %weights.2 = (bf16[480,768]{1,0:T(8,128)(2,1)}, bf16[480,768]{1,0:T(8,128)(2,1)}, f32[1,960]{1,0:T(1,128)}) custom-call(s32[11]{0:T(128)S(1)} %get-tuple-element.43.ids, bf16[1024,768]{1,0:T(8,128)(2,1)S(1)} %bitcast.53, bf16[1024,960]{1,0:T(8,128)(2,1)} %bitcast.51), custom_call_target="tpu_custom_call" | custom-call | flops 6899999744 | bytes 6900000 | tf_op jit(solution)/shard_map/cond/branch_1_fun/weights/pallas_call | solution.py:947
  218.9 17.6 %attend_back.3 = (bf16[4,256,960]{2,1,0:T(8,128)(2,1)}, bf16[4,64,768]{2,1,0:T(8,128)(2,1)}) custom-call(s32[11]{0:T(128)S(1)} %get-tuple-element.43.ids, bf16[1024,768]{1,0:T(8,128)(2,1)} %get-tuple-element.56.q_ref, bf16[1024,768]{1,0:T(8,128)(2,1)} %get-tuple-element.46.k_ref, bf16[1024,768]{1,0:T(8,128)(2,1)} %get-tuple-element.47.v_ref, ...), custom_call_target="tpu_custom_call" | custom-call | flops 20124999680 | bytes 20125000 | tf_op jit(solution)/shard_map/cond/branch_1_fun/attend_back/pallas_call | solution.py:920
  237.1 5.1 %weights.3 = (bf16[480,768]{1,0:T(8,128)(2,1)}, bf16[480,768]{1,0:T(8,128)(2,1)}, f32[1,960]{1,0:T(1,128)}) custom-call(s32[11]{0:T(128)S(1)} %get-tuple-element.43.ids, bf16[1024,768]{1,0:T(8,128)(2,1)S(1)} %bitcast.54, bf16[1024,960]{1,0:T(8,128)(2,1)} %bitcast.52), custom_call_target="tpu_custom_call" | custom-call | flops 6899999744 | bytes 6900000 | tf_op jit(solution)/shard_map/cond/branch_1_fun/weights/pallas_call | solution.py:947
  249.0 4.8 %all-to-all-start.1 = ((bf16[8,88,768]{2,1,0:T(8,128)(2,1)}), bf16[8,88,768]{2,1,0:T(8,128)(2,1)}, u32[]{:S(2)}, u32[]{:S(2)}) async-start(bf16[8,88,768]{2,1,0:T(8,128)(2,1)} %bitcast.39), calls=%async_computation.1 | async-start | bytes 2162688 | tf_op jit(solution)/shard_map/cond/branch_1_fun/all_to_all | solution.py:869
  254.5 10.4 %input.1 = (bf16[384,768]{1,0:T(8,128)(2,1)}, bf16[384,768]{1,0:T(8,128)(2,1)}, bf16[384,768]{1,0:T(8,128)(2,1)}, bf16[384,768]{1,0:T(8,128)(2,1)}, f32[2,768]{1,0:T(2,128)}) custom-call(s32[11]{0:T(128)S(1)} %get-tuple-element.43.ids, bf16[4,256,960]{2,1,0:T(8,128)(2,1)} %get-tuple-element.61.own_ref, bf16[4,256,960]{2,1,0:T(8,128)(2,1)} %get-tuple-element.53.other_ref, ...), custom_call_target="tpu_custom_call" | custom-call | flops 10350000128 | bytes 10350000 | tf_op jit(solution)/shard_map/cond/branch_1_fun/input/pallas_call | solution.py:989
  274.9 6.5 %collective-permute-done.7 = f32[7104]{0:T(1024)S(1)} collective-permute-done((f32[7104]{0:T(1024)S(1)}, f32[7104]{0:T(1024)S(1)}, u32[]{:S(2)}, u32[]{:S(2)}) %collective-permute-start.7) | collective-permute-done | bytes 28448 | tf_op jit(solution)/shard_map/cond/branch_1_fun/ppermute | solution.py:691
  285.1 13.7 %collective-permute-done.8 = f32[7104]{0:T(1024)S(1)} collective-permute-done((f32[7104]{0:T(1024)S(1)}, f32[7104]{0:T(1024)S(1)}, u32[]{:S(2)}, u32[]{:S(2)}) %collective-permute-start.8) | collective-permute-done | bytes 28448 | tf_op jit(solution)/shard_map/cond/branch_1_fun/ppermute | solution.py:691
  298.8 5.8 %collective-permute-done.11 = bf16[384,768]{1,0:T(8,128)(2,1)} collective-permute-done((bf16[384,768]{1,0:T(8,128)(2,1)}, bf16[384,768]{1,0:T(8,128)(2,1)}, u32[]{:S(2)}, u32[]{:S(2)}) %collective-permute-start.11) | collective-permute-done | bytes 589856 | tf_op jit(solution)/shard_map/cond/branch_1_fun/ppermute | solution.py:691
  316.3 4.6 %collect.1 = (f32[4,256,768]{2,1,0:T(8,128)}, f32[192,2048]{1,0:T(8,128)}) custom-call(s32[11]{0:T(128)S(1)} %copy-done.19, bf16[384,768]{1,0:T(8,128)(2,1)} %get-tuple-element.236.refs_0_, bf16[384,768]{1,0:T(8,128)(2,1)} %get-tuple-element.237.refs_1_, bf16[384,768]{1,0:T(8,128)(2,1)} %get-tuple-element.238.refs_2_, ...), custom_call_target="tpu_custom_call" | custom-call | flops 5750000128 | bytes 5750000 | tf_op jit(solution)/shard_map/collect/pallas_call | solution.py:571
  324.2 7.1 %place_feed.1 = (f32[768,1536]{1,0:T(8,128)}, f32[1536,768]{1,0:T(8,128)}) custom-call(s32[11]{0:T(128)} %broadcast_add_fusion.ids, bf16[1536,768]{1,0:T(8,128)(2,1)} %all-reduce.2.cloned.1.call-done.mine_ref, bf16[1536,768]{1,0:T(8,128)(2,1)} %collective-permute-done.29.theirs_ref), custom_call_target="tpu_custom_call" | custom-call | flops 9200000000 | bytes 9200000 | tf_op jit(solution)/shard_map/place_feed/pallas_call | solution.py:593
  331.3 10.2 %all-to-all-done.4 = bf16[8,88,768]{2,1,0:T(8,128)(2,1)S(1)} async-done(((bf16[8,88,768]{2,1,0:T(8,128)(2,1)}), bf16[8,88,768]{2,1,0:T(8,128)(2,1)S(1)}, u32[]{:S(2)}, u32[]{:S(2)}) %all-to-all-start.4) | async-done | bytes 1081376 | tf_op jit(solution)/shard_map/all_to_all | solution.py:873
  (207 shorter events, 106.9 us)
Async XLA Ops:
  11.1 26.2 %collective-permute-start.12 = (bf16[672,768]{1,0:T(8,128)(2,1)}, bf16[672,768]{1,0:T(8,128)(2,1)}, u32[]{:S(2)}, u32[]{:S(2)}) collective-permute-start(bf16[672,768]{1,0:T(8,128)(2,1)} %pad_maximum_fusion.3), channel_id=1, source_target_pairs={{0,1},{1,0},{2,3},{3,2},{4,5},{5,4},{6,7},{7,6},{8,9},{9,8},{10,11... | collective-permute-start | bytes 3096584 | tf_op jit(solution)/shard_map/ppermute | solution.py:697
  17.9 33.2 %all-to-all-start.2 = ((bf16[4,384,768]{2,1,0:T(8,128)(2,1)}), bf16[4,384,768]{2,1,0:T(8,128)(2,1)}, u32[]{:S(2)}, u32[]{:S(2)}) async-start(bf16[4,384,768]{2,1,0:T(8,128)(2,1)} %pad_maximum_fusion.1), calls=%async_computation.2 | async-start | bytes 4718592 | tf_op jit(solution)/shard_map/all_to_all | solution.py:700
  37.4 15.1 %collective-permute-start.14 = (bf16[672,768]{1,0:T(8,128)(2,1)}, bf16[672,768]{1,0:T(8,128)(2,1)}, u32[]{:S(2)}, u32[]{:S(2)}) collective-permute-start(bf16[672,768]{1,0:T(8,128)(2,1)} %collective-permute-done.12.near_ref), channel_id=1, source_target_pairs={{0,2},{2,0},{4,6},{6,4},{8,10},{10,8},{12,14},{14,12},{16,18},{18,... | collective-permute-start | bytes 3096584 | tf_op jit(solution)/shard_map/ppermute | solution.py:691
  39.0 23.1 %collective-permute-start.17 = (bf16[384,768]{1,0:T(8,128)(2,1)}, bf16[384,768]{1,0:T(8,128)(2,1)S(1)}, u32[]{:S(2)}, u32[]{:S(2)}) collective-permute-start(bf16[384,768]{1,0:T(8,128)(2,1)} %constant_dynamic-slice_fusion), channel_id=1, source_target_pairs={{0,1},{1,0},{2,3},{3,2},{4,5},{5,4},{6,7},{7,6},{8,9},{9,8},{10,11... | collective-permute-start | bytes 1769480 | tf_op jit(solution)/shard_map/ppermute | solution.py:697
  52.1 18.0 %collective-permute-start.15 = (bf16[4,64,768]{2,1,0:T(8,128)(2,1)S(1)}, bf16[4,64,768]{2,1,0:T(8,128)(2,1)S(1)}, u32[]{:S(2)}, u32[]{:S(2)}) collective-permute-start(bf16[4,64,768]{2,1,0:T(8,128)(2,1)S(1)} %constant_dynamic-slice_fusion.1), channel_id=1, source_target_pairs={{0,1},{1,0},{2,3},{3,2},{4,5},{5,4},{6,7},{7,6},{8,9},{9,8},{10,11... | collective-permute-start | bytes 1179656 | tf_op jit(solution)/shard_map/ppermute | solution.py:697
  62.9 32.8 %all-to-all-start.3 = ((bf16[4,256,768]{2,1,0:T(8,128)(2,1)}), bf16[4,256,768]{2,1,0:T(8,128)(2,1)S(1)}, u32[]{:S(2)}, u32[]{:S(2)}) async-start(bf16[4,256,768]{2,1,0:T(8,128)(2,1)} %bitcast.19), calls=%async_computation.3 | async-start | bytes 3145728 | tf_op jit(solution)/shard_map/all_to_all | solution.py:700
  66.5 241.1 %all-reduce.2.cloned.1.call-start = ((), (), s32[]{:S(2)}) async-start(), calls=%async_computation.5 | async-start | bytes 4718592 | tf_op jit(solution)/shard_map/psum | solution.py:915
  66.7 31.4 %collective-permute-start.18 = (bf16[384,768]{1,0:T(8,128)(2,1)}, bf16[384,768]{1,0:T(8,128)(2,1)}, u32[]{:S(2)}, u32[]{:S(2)}) collective-permute-start(bf16[384,768]{1,0:T(8,128)(2,1)} %copy-done.26), channel_id=1, source_target_pairs={{0,8},{2,10},{4,12},{6,14},{8,0},{10,2},{12,4},{14,6},{16,24},{18,... | collective-permute-start | bytes 1769480 | tf_op jit(solution)/shard_map/ppermute | solution.py:691
  68.6 29.5 %collective-permute-start.19 = (bf16[768,768]{1,0:T(8,128)(2,1)S(1)}, bf16[768,768]{1,0:T(8,128)(2,1)}, u32[]{:S(2)}, u32[]{:S(2)}) collective-permute-start(bf16[768,768]{1,0:T(8,128)(2,1)S(1)} %slice.66), channel_id=1, source_target_pairs={{0,1},{1,0},{2,3},{3,2},{4,5},{5,4},{6,7},{7,6},{8,9},{9,8},{10,11... | collective-permute-start | bytes 3538952 | tf_op jit(solution)/shard_map/ppermute | solution.py:697
  125.0 19.5 %collective-permute-start.21 = (bf16[384,768]{1,0:T(8,128)(2,1)}, bf16[384,768]{1,0:T(8,128)(2,1)S(1)}, u32[]{:S(2)}, u32[]{:S(2)}) collective-permute-start(bf16[384,768]{1,0:T(8,128)(2,1)} %get-tuple-element.201), channel_id=1, source_target_pairs={{0,1},{1,0},{2,3},{3,2},{4,5},{5,4},{6,7},{7,6},{8,9},{9,8},{10,11... | collective-permute-start | bytes 1769480 | tf_op jit(solution)/shard_map/ppermute | solution.py:697
  125.5 15.3 %collective-permute-start.22 = (bf16[384,768]{1,0:T(8,128)(2,1)}, bf16[384,768]{1,0:T(8,128)(2,1)S(1)}, u32[]{:S(2)}, u32[]{:S(2)}) collective-permute-start(bf16[384,768]{1,0:T(8,128)(2,1)} %get-tuple-element.202), channel_id=1, source_target_pairs={{0,8},{2,10},{4,12},{6,14},{8,0},{10,2},{12,4},{14,6},{16,24},{18,... | collective-permute-start | bytes 1769480 | tf_op jit(solution)/shard_map/ppermute | solution.py:691
  139.1 21.4 %collective-permute-start.25 = (bf16[1024,768]{1,0:T(8,128)(2,1)}, bf16[1024,768]{1,0:T(8,128)(2,1)S(1)}, u32[]{:S(2)}, u32[]{:S(2)}) collective-permute-start(bf16[1024,768]{1,0:T(8,128)(2,1)} %get-tuple-element.218), channel_id=1, source_target_pairs={{0,2},{2,0},{4,6},{6,4},{8,10},{10,8},{12,14},{14,12},{16,18},{18,... | collective-permute-start | bytes 4718600 | tf_op jit(solution)/shard_map/ppermute | solution.py:691
  139.1 21.4 %collective-permute-start.24 = (bf16[1024,768]{1,0:T(8,128)(2,1)}, bf16[1024,768]{1,0:T(8,128)(2,1)S(1)}, u32[]{:S(2)}, u32[]{:S(2)}) collective-permute-start(bf16[1024,768]{1,0:T(8,128)(2,1)} %get-tuple-element.207), channel_id=1, source_target_pairs={{0,2},{2,0},{4,6},{6,4},{8,10},{10,8},{12,14},{14,12},{16,18},{18,... | collective-permute-start | bytes 4718600 | tf_op jit(solution)/shard_map/ppermute | solution.py:691
  144.5 15.4 %collective-permute-start.23 = (bf16[384,768]{1,0:T(8,128)(2,1)S(1)}, bf16[384,768]{1,0:T(8,128)(2,1)S(1)}, u32[]{:S(2)}, u32[]{:S(2)}) collective-permute-start(bf16[384,768]{1,0:T(8,128)(2,1)S(1)} %copy-done.28), channel_id=1, source_target_pairs={{0,1},{1,0},{2,3},{3,2},{4,5},{5,4},{6,7},{7,6},{8,9},{9,8},{10,11... | collective-permute-start | bytes 1769480 | tf_op jit(solution)/shard_map/ppermute | solution.py:697
  183.3 35.5 %all-to-all-start = ((bf16[4,256,768]{2,1,0:T(8,128)(2,1)}), bf16[4,256,768]{2,1,0:T(8,128)(2,1)S(1)}, u32[]{:S(2)}, u32[]{:S(2)}) async-start(bf16[4,256,768]{2,1,0:T(8,128)(2,1)} %get-tuple-element.42), calls=%async_computation | async-start | bytes 3145728 | tf_op jit(solution)/shard_map/cond/branch_1_fun/all_to_all | solution.py:700
  188.2 18.7 %collective-permute-start = (bf16[192,768]{1,0:T(8,128)(2,1)S(1)}, bf16[192,768]{1,0:T(8,128)(2,1)S(1)}, u32[]{:S(2)}, u32[]{:S(2)}) collective-permute-start(bf16[192,768]{1,0:T(8,128)(2,1)S(1)} %slice_bitcast_fusion), channel_id=1, source_target_pairs={{0,1},{1,0},{2,3},{3,2},{4,5},{5,4},{6,7},{7,6},{8,9},{9,8},{10,11... | collective-permute-start | bytes 884744 | tf_op jit(solution)/shard_map/cond/branch_1_fun/ppermute | solution.py:697
  218.3 18.8 %collective-permute-start.2 = (bf16[480,768]{1,0:T(8,128)(2,1)}, bf16[480,768]{1,0:T(8,128)(2,1)}, u32[]{:S(2)}, u32[]{:S(2)}) collective-permute-start(bf16[480,768]{1,0:T(8,128)(2,1)} %fold.4), channel_id=1, source_target_pairs={{0,1},{1,0},{2,3},{3,2},{4,5},{5,4},{6,7},{7,6},{8,9},{9,8},{10,11... | collective-permute-start | bytes 2211848 | tf_op jit(solution)/shard_map/cond/branch_1_fun/ppermute | solution.py:697
  249.0 55.6 %all-to-all-start.1 = ((bf16[8,88,768]{2,1,0:T(8,128)(2,1)}), bf16[8,88,768]{2,1,0:T(8,128)(2,1)}, u32[]{:S(2)}, u32[]{:S(2)}) async-start(bf16[8,88,768]{2,1,0:T(8,128)(2,1)} %bitcast.39), calls=%async_computation.1 | async-start | bytes 2162688 | tf_op jit(solution)/shard_map/cond/branch_1_fun/all_to_all | solution.py:869
  265.0 33.8 %collective-permute-start.9 = (bf16[384,768]{1,0:T(8,128)(2,1)}, bf16[384,768]{1,0:T(8,128)(2,1)}, u32[]{:S(2)}, u32[]{:S(2)}) collective-permute-start(bf16[384,768]{1,0:T(8,128)(2,1)} %get-tuple-element.80), channel_id=1, source_target_pairs={{0,2},{2,0},{4,6},{6,4},{8,10},{10,8},{12,14},{14,12},{16,18},{18,... | collective-permute-start | bytes 1769480 | tf_op jit(solution)/shard_map/cond/branch_1_fun/ppermute | solution.py:691
  265.1 33.7 %collective-permute-start.10 = (bf16[384,768]{1,0:T(8,128)(2,1)}, bf16[384,768]{1,0:T(8,128)(2,1)}, u32[]{:S(2)}, u32[]{:S(2)}) collective-permute-start(bf16[384,768]{1,0:T(8,128)(2,1)} %get-tuple-element.81), channel_id=1, source_target_pairs={{0,4},{2,6},{4,0},{6,2},{8,12},{10,14},{12,8},{14,10},{16,20},{18,... | collective-permute-start | bytes 1769480 | tf_op jit(solution)/shard_map/cond/branch_1_fun/ppermute | solution.py:691
  267.1 37.5 %collective-permute-start.11 = (bf16[384,768]{1,0:T(8,128)(2,1)}, bf16[384,768]{1,0:T(8,128)(2,1)}, u32[]{:S(2)}, u32[]{:S(2)}) collective-permute-start(bf16[384,768]{1,0:T(8,128)(2,1)} %get-tuple-element.82), channel_id=1, source_target_pairs={{0,6},{2,4},{4,2},{6,0},{8,14},{10,12},{12,10},{14,8},{16,22},{18,... | collective-permute-start | bytes 1769480 | tf_op jit(solution)/shard_map/cond/branch_1_fun/ppermute | solution.py:691
  281.4 17.3 %collective-permute-start.8 = (f32[7104]{0:T(1024)S(1)}, f32[7104]{0:T(1024)S(1)}, u32[]{:S(2)}, u32[]{:S(2)}) collective-permute-start(f32[7104]{0:T(1024)S(1)} %add.58), channel_id=1, source_target_pairs={{0,16},{2,18},{4,20},{6,22},{8,24},{10,26},{12,28},{14,30},{16,0},... | collective-permute-start | bytes 85256 | tf_op jit(solution)/shard_map/cond/branch_1_fun/ppermute | solution.py:691
  307.6 16.5 %collective-permute-start.29 = (bf16[1536,768]{1,0:T(8,128)(2,1)}, bf16[1536,768]{1,0:T(8,128)(2,1)}, u32[]{:S(2)}, u32[]{:S(2)}) collective-permute-start(bf16[1536,768]{1,0:T(8,128)(2,1)} %all-reduce.2.cloned.1.call-done.mine_ref), channel_id=1, source_target_pairs={{0,2},{2,0},{4,6},{6,4},{8,10},{10,8},{12,14},{14,12},{16,18},{18,... | collective-permute-start | bytes 7077896 | tf_op jit(solution)/shard_map/ppermute | solution.py:691
  310.6 30.8 %all-to-all-start.4 = ((bf16[8,88,768]{2,1,0:T(8,128)(2,1)}), bf16[8,88,768]{2,1,0:T(8,128)(2,1)S(1)}, u32[]{:S(2)}, u32[]{:S(2)}) async-start(bf16[8,88,768]{2,1,0:T(8,128)(2,1)} %spread_sum.1), calls=%async_computation.4 | async-start | bytes 2162688 | tf_op jit(solution)/shard_map/all_to_all | solution.py:873
  (55 other events, 406.5 us)
Sparse Core Ops, SparseCore 0:
  180.2 127.3 all-reduce.1

commit v4 on v3

--- a/solution.py
+++ b/solution.py
@@ -219,7 +219,7 @@
         + nn(attended[:, half:], other_ref[...])
         + vector(bias_ref)
     )
-    middle_ref[...] = middle
+    middle_ref[...] = middle.astype(BF16)
     scaled, _ = normed(middle)
     norm_ref[...] = (scaled * vector(gain_ref) + vector(shift_ref)).astype(BF16)
 
@@ -315,15 +315,15 @@
 ):
     p = pl.program_id(0)
     half = own_ref.shape[0]
-    middle = middle_ref[...]
+    middle = middle_ref[...].astype(F32)
     summed = lambda refs: sum(ref[...].astype(F32) for ref in refs)
     layer_ref[...] = (middle + summed((out_a, out_b)) + vector(down_bias_ref)).astype(BF16)
     scaled, inverse = normed(middle)
     second = summed((back_a, back_b))
     out_grad = grad_ref[...].astype(F32)
     middle_grad = out_grad + norm_back(second, scaled, inverse, vector(gain_ref))
-    mg_ref[...] = middle_grad
     low = middle_grad.astype(BF16)
+    mg_ref[...] = low
     ga_ref[:, :half] = nt(low, own_ref[...]).astype(BF16)
     ga_ref[:, half:] = nt(low, other_ref[...]).astype(BF16)
     weight_grad = tn(att_ref[...], low)
@@ -464,7 +464,7 @@
         first = part if first is None else first + part
     scaled, inverse = normed(x_ref[...].astype(F32))
     tokens, each = x_ref.shape[0], skip_own_ref.shape[0]
-    made = (mg_ref[...] + norm_back(first, scaled, inverse, vector(gain_ref))).astype(BF16)
+    made = (mg_ref[...].astype(F32) + norm_back(first, scaled, inverse, vector(gain_ref))).astype(BF16)
     for distance, grad_ref in enumerate(grad_refs):
 
         @pl.when(p == distance)
@@ -753,14 +753,7 @@
     thirds = fresh // HEAD
     skip_sent = skip_values.T.reshape(thirds, HEAD, tp_count, SPAN, BLOCK)
     skip_sent = skip_sent.transpose(3, 2, 1, 0, 4).reshape(SPAN, tp_count * HEAD, thirds * BLOCK)
-    blocks_in = to_seqs(
-        jnp.concatenate([layer_in.reshape(SPAN, BLOCK, width), skip_sent], axis=1)
-    )
-    skip_other = swap_tp(
-        lax.dynamic_slice(
-            blocks_in, (0, BLOCK + (1 - tp_index) * HEAD, 0), (SPAN, HEAD, width)
-        )
-    )
+    blocks_in = to_seqs(layer_in.reshape(SPAN, BLOCK, width))
     up_bias_half = rows_of(up_bias, core * side, side)
     bias_own = jnp.concatenate([query_bias, value_bias, up_bias_half])
     bias_other = swap_tp(bias_own)
@@ -769,7 +762,10 @@
          rows_of(down_weight, core * side, side)], 0,
     )
     feed_own, ids = lax.optimization_barrier((feed_own, ids))
-    early_near, bias_other = lax.optimization_barrier((early_near, bias_other, feed_own))[:2]
+    early_near, bias_other, skip_sent = lax.optimization_barrier(
+        (early_near, bias_other, skip_sent, feed_own)
+    )[:3]
+    skip_in = to_seqs(tie(skip_sent, blocks_in))
     early_far = swap_core(early_near)
     up_part = rows_of(feed_own, group % 2 * (side // 2), side // 2)
     up_near = swap_tp(tie(up_part, early_near))
@@ -800,10 +796,16 @@
         name="project",
     )(ids, blocks_in, qkv_own, early_near, early_far, qkv_bias, gain_attention, shift_attention)
 
-    grad_blocks = to_seqs(tie(out_grad.reshape(SPAN, BLOCK, width), queries))
+    grad_blocks = to_seqs(tie(out_grad.reshape(SPAN, BLOCK, width), queries, skip_in))
     up_near = tie(up_near, queries)
     up_far = swap_seq(up_near, SPAN)
-    down_other = swap_tp(tie(feed_own[side:], queries))
+    skip_in = tie(skip_in, queries)
+    skip_other = swap_tp(
+        lax.dynamic_slice(
+            skip_in, (0, (1 - tp_index) * HEAD, 0), (SPAN, HEAD, width)
+        )
+    )
+    down_other = swap_tp(tie(feed_own[side:], skip_in))
     lse_spec = pl.BlockSpec((head_rows, BLOCK), lambda p, *_: (0, p))
     values, attended, log_total, middle, norm_two = call(
         attend_kernel,
@@ -814,7 +816,7 @@
             pl.BlockSpec((2, BLOCK, fresh), lambda p, *_: (0, p, 0)),
             pl.BlockSpec(
                 (None, HEAD, width),
-                lambda p, ids: (member_at(p, ids), BLOCK // HEAD + ids[TP], 0),
+                lambda p, ids: (member_at(p, ids), ids[TP], 0),
             ),
             placed(width, HEAD),
             full((half, width)), full((half, width)), full((width,)), full((width,)),
@@ -823,13 +825,13 @@
         [full(flat), placed(width), lse_spec, placed(width), placed(width)],
         [
             shape_of(flat, BF16), shape_of(own_shape, BF16), shape_of((head_rows, tokens), F32),
-            shape_of(own_shape, F32), shape_of(own_shape, BF16),
+            shape_of(own_shape, BF16), shape_of(own_shape, BF16),
         ],
         scratch=[pltpu.VMEM((BLOCK, width), BF16), pltpu.VMEM((BLOCK, 128), F32)],
         micros=27,
         name="attend",
     )(
-        ids, blocks_in, queries, keys, fresh_values, blocks_in, skip_other, out_weight,
+        ids, blocks_in, queries, keys, fresh_values, skip_in, skip_other, out_weight,
         out_other,        out_bias, gain_feed, shift_feed,
     )
     rows_mine = norm_two.reshape(flat)
@@ -887,7 +889,7 @@
             full((2, half // 2, width)), full((2, half // 2, width)), full((4, width)),
         ],
         [
-            shape_of(own_shape, BF16), shape_of(own_shape, F32), shape_of(own_shape, BF16),
+            shape_of(own_shape, BF16), shape_of(own_shape, BF16), shape_of(own_shape, BF16),
             shape_of((2, half // 2, width), BF16), shape_of((2, half // 2, width), BF16),
             shape_of((4, width), F32),
         ],

time: 364 us -> 362 us (level)
  waiting for transfers between devices: 68.9 us -> 59.7 us
  starting transfers between devices: 47.4 us -> 54.2 us
    all_to_all x3 -> x4, waiting for transfers between devices: 9.7 us -> 2.05 us  [to_seqs(): lax.all_to_all(value, 'seq', 0, 0, tiled=True, axis_index_groups=members)]
    all_to_all x3 -> x4, starting transfers between devices: 12.1 us -> 15.3 us  [to_seqs(): lax.all_to_all(value, 'seq', 0, 0, tiled=True, axis_index_groups=members)]
    unnamed x62 -> x58, local copies, waits for them, and re-layouts: 10 us -> 8.29 us
  transfers between devices with their start and end apart: 37 -> 38, of which waited for: 16 -> 15; matrix products, arithmetic and copies ran while one was open for 6% -> 7% of each run, Pallas kernels for 46% -> 46%
where the time goes in v4:
time: 362 us; the launch traced here: 356 us
  Pallas kernels  187 us (52%)
  waiting for transfers between devices  59.7 us (16%)
  starting transfers between devices  54.2 us (15%)
  local copies, waits for them, and re-layouts  30.5 us (8%)
  between operations  16.4 us (5%)
  other arithmetic  7.81 us (2%)
    pallas_call x4, Pallas kernels, feed(): call(partial(feed_kernel, len(weights) > 1, len(sums) > 0, len(made) > 0,...  52.9 us
    pallas_call x2, Pallas kernels, attend_back(): call(partial(attend_back_kernel, which * (heads // 2)), 1, (SPAN,), [pl.B...  34.8 us
    ppermute x19, waiting for transfers between devices, swap_seq(): lax.ppermute(value, 'seq', [(i, i ^ distance) for i in range(seq_count)])  34.7 us
    pallas_call x1, Pallas kernels, per_device(): call(attend_kernel, 1, (SPAN,), [placed(width), in_rows(width), full(flat...  24.3 us
    all_to_all x4, starting transfers between devices, to_seqs(): lax.all_to_all(value, 'seq', 0, 0, tiled=True, axis_index_groups=members)  15.3 us
    ppermute x19, starting transfers between devices, swap_seq(): lax.ppermute(value, 'seq', [(i, i ^ distance) for i in range(seq_count)])  15.1 us
    ppermute x12, starting transfers between devices, swap_tp(): return lax.ppermute(value, 'tp', [(i, i ^ 1) for i in range(tp_count)])  14.6 us
    pallas_call x4, Pallas kernels, fold(): call(partial(fold_kernel, indices, starts), 1, (1,), [full(array.shape) f...  14 us
  transfers between devices with their start and end apart: 38, of which 15 were waited for; matrix products, arithmetic and copies ran while one was open for 7% of the time, Pallas kernels for 46%

profile of v4, /device:TPU:0, one launch (start us, length us, event | category | flops | bytes accessed | tf_op | source)
XLA Modules:
  0.0 355.7 jit_solution(13682731313574928374)
XLA Ops:
  14.9 4.4 %all-to-all-start.2 = ((bf16[4,256,768]{2,1,0:T(8,128)(2,1)}), bf16[4,256,768]{2,1,0:T(8,128)(2,1)}, u32[]{:S(2)}, u32[]{:S(2)}) async-start(bf16[4,256,768]{2,1,0:T(8,128)(2,1)} %bitcast.15), calls=%async_computation.2 | async-start | bytes 3145728 | tf_op jit(solution)/shard_map/all_to_all | solution.py:700
  32.1 5.3 %collective-permute-done.13 = f32[1344]{0:T(1024)} collective-permute-done((f32[1344]{0:T(1024)}, f32[1344]{0:T(1024)}, u32[]{:S(2)}, u32[]{:S(2)}) %collective-permute-start.13) | collective-permute-done | bytes 5408 | tf_op jit(solution)/shard_map/ppermute | solution.py:697
  44.9 9.5 %project.1 = (bf16[4,256,768]{2,1,0:T(8,128)(2,1)}, bf16[1024,768]{1,0:T(8,128)(2,1)}, bf16[1024,768]{1,0:T(8,128)(2,1)}, bf16[2,1024,192]{2,1,0:T(8,128)(2,1)},...) custom-call(s32[11]{0:T(128)S(1)} %concatenate.31.ids, bf16[4,256,768]{2,1,0:T(8,128)(2,1)} %all-to-all-done.2.x_ref, ...), custom_call_target="tpu_custom_call" | custom-call | flops 10350000128 | bytes 10350000 | tf_op jit(solution)/shard_map/project/pallas_call | solution.py:777
  67.9 24.3 %attend.1 = (bf16[1024,768]{1,0:T(8,128)(2,1)}, bf16[4,256,768]{2,1,0:T(8,128)(2,1)}, f32[16,1024]{1,0:T(8,128)S(1)}, bf16[4,256,768]{2,1,0:T(8,128)(2,1)}, bf16[4,256,768]{2,1,0:T(8,128)(2,1)}) custom-call(s32[11]{0:T(128)S(1)} %copy-done.19, bf16[4,256,768]{2,1,0:T(8,128)(2,1)} %all-to-all-done.2.x_ref, bf16[1024,768]{1,0:T(8,128)(2,1)} %get-tuple-element.192.q_ref, ...), custom_call_target="tpu_custom_call" | custom-call | flops 31050000384 | bytes 31050000 | tf_op jit(solution)/shard_map/attend/pallas_call | solution.py:810
  94.8 12.4 %feed.4 = (bf16[1024,768]{1,0:T(8,128)(2,1)}, bf16[1024,768]{1,0:T(8,128)(2,1)}, f32[1,768]{1,0:T(1,128)S(1)}, bf16[1536,768]{1,0:T(8,128)(2,1)}) custom-call(s32[11]{0:T(128)S(1)} %copy-done.19, bf16[1024,768]{1,0:T(8,128)(2,1)} %bitcast.48, bf16[1024,768]{1,0:T(8,128)(2,1)} %bitcast.36, bf16[384,768]{1,0:T(8,128)(2,1)} %collective-permute-done.17.refs_2_, ...), custom_call_target="tpu_custom_call" | custom-call | flops 16099999744 | bytes 16100000 | tf_op jit(solution)/shard_map/feed/pallas_call | solution.py:296
  108.4 13.2 %feed.5 = (bf16[1024,768]{1,0:T(8,128)(2,1)}, bf16[1024,768]{1,0:T(8,128)(2,1)}, f32[1,768]{1,0:T(1,128)S(1)}, bf16[384,768]{1,0:T(8,128)(2,1)}, bf16[384,768]{1...) custom-call(s32[11]{0:T(128)S(1)} %copy-done.19, ...), custom_call_target="tpu_custom_call" | custom-call | flops 16099999744 | bytes 16100000 | tf_op jit(solution)/shard_map/feed/pallas_call | solution.py:296
  124.1 13.4 %feed.6 = (bf16[1024,768]{1,0:T(8,128)(2,1)}, bf16[1024,768]{1,0:T(8,128)(2,1)}, f32[1,768]{1,0:T(1,128)S(1)}, bf16[1536,768]{1,0:T(8,128)(2,1)}) custom-call(s32[11]{0:T(128)S(1)} %copy-done.19, bf16[1024,768]{1,0:T(8,128)(2,1)} %collective-permute-done.16.refs_0_, bf16[1024,768]{1,0:T(8,128)(2,1)} %copy-done.22, bf16[1536,768]{1,0:T(8,128)(2,1)} %copy-done.2, ...), custom_call_target="tpu_custom_call" | custom-call | flops 16099999744 | bytes 16100000 | tf_op jit(solution)/shard_map/feed/pallas_call | solution.py:296
  143.5 13.9 %feed.7 = (bf16[1024,768]{1,0:T(8,128)(2,1)}, bf16[1024,768]{1,0:T(8,128)(2,1)}, f32[1,768]{1,0:T(1,128)S(1)}, bf16[384,768]{1,0:T(8,128)(2,1)}, bf16[384,768]{1...) custom-call(s32[11]{0:T(128)S(1)} %copy-done.19, bf16[1024,768]{1,0:T(8,128)(2,1)} %bitcast.49, ...), custom_call_target="tpu_custom_call" | custom-call | flops 16099999744 | bytes 16100000 | tf_op jit(solution)/shard_map/feed/pallas_call | solution.py:296
  160.4 11.6 %residual.1 = (bf16[4,256,768]{2,1,0:T(8,128)(2,1)}, bf16[4,256,768]{2,1,0:T(8,128)(2,1)}, bf16[4,256,768]{2,1,0:T(8,128)(2,1)}, bf16[2,192,768]{2,1,0:T(8,128)(...) custom-call(s32[11]{0:T(128)S(1)} %copy-done.19, bf16[1024,768]{1,0:T(8,128)(2,1)} %get-tuple-element.222.out_a, ...), custom_call_target="tpu_custom_call" | custom-call | flops 14375000064 | bytes 14375000 | tf_op jit(solution)/shard_map/residual/pallas_call | solution.py:878
  173.3 4.9 %fold.7 = bf16[1536,768]{1,0:T(8,128)(2,1)} custom-call(s32[11]{0:T(128)S(1)} %copy-done.19, bf16[384,768]{1,0:T(8,128)(2,1)} %get-tuple-element.250.refs_0_, bf16[384,768]{1,0:T(8,128)(2,1)} %copy-done.26, bf16[384,768]{1,0:T(8,128)(2,1)} %get-tuple-element.251.refs_2_, bf16[384,768]{1,0:T(8,128)(2,1)} %copy-done.29, ...), custom_call_target="tpu_custom_call" | custom-call | flops 4024999936 | bytes 4025000 | tf_op jit(solution)/shard_map/fold/pallas_call | solution.py:521
  181.4 119.8 %conditional.1 = (bf16[1024,768]{1,0:T(8,128)(2,1)S(1)}, bf16[8,88,768]{2,1,0:T(8,128)(2,1)}, f32[7104]{0:T(1024)S(1)}, bf16[384,768]{1,0:T(8,128)(2,1)}, bf16[3...) conditional(s32[]{:T(128)} %convert_element_type.18, () %tuple.41, ...), branch_computations={%region_3.4_spmd, %region_4.5_spmd} | conditional | flops 72450031616 | bytes 138468224 | solution.py:1028
  186.9 17.2 %attend_back.2 = (bf16[4,256,960]{2,1,0:T(8,128)(2,1)}, bf16[4,64,768]{2,1,0:T(8,128)(2,1)}) custom-call(s32[11]{0:T(128)S(1)} %get-tuple-element.43.ids, bf16[1024,768]{1,0:T(8,128)(2,1)} %get-tuple-element.56.q_ref, bf16[1024,768]{1,0:T(8,128)(2,1)} %get-tuple-element.46.k_ref, bf16[1024,768]{1,0:T(8,128)(2,1)} %get-tuple-element.47.v_ref, ...), custom_call_target="tpu_custom_call" | custom-call | flops 20124999680 | bytes 20125000 | tf_op jit(solution)/shard_map/cond/branch_1_fun/attend_back/pallas_call | solution.py:922
  204.1 5.1 %weights.2 = (bf16[480,768]{1,0:T(8,128)(2,1)}, bf16[480,768]{1,0:T(8,128)(2,1)}, f32[1,960]{1,0:T(1,128)}) custom-call(s32[11]{0:T(128)S(1)} %get-tuple-element.43.ids, bf16[1024,768]{1,0:T(8,128)(2,1)S(1)} %bitcast.53, bf16[1024,960]{1,0:T(8,128)(2,1)} %bitcast.51), custom_call_target="tpu_custom_call" | custom-call | flops 6899999744 | bytes 6900000 | tf_op jit(solution)/shard_map/cond/branch_1_fun/weights/pallas_call | solution.py:949
  216.8 17.6 %attend_back.3 = (bf16[4,256,960]{2,1,0:T(8,128)(2,1)}, bf16[4,64,768]{2,1,0:T(8,128)(2,1)}) custom-call(s32[11]{0:T(128)S(1)} %get-tuple-element.43.ids, bf16[1024,768]{1,0:T(8,128)(2,1)} %get-tuple-element.56.q_ref, bf16[1024,768]{1,0:T(8,128)(2,1)} %get-tuple-element.46.k_ref, bf16[1024,768]{1,0:T(8,128)(2,1)} %get-tuple-element.47.v_ref, ...), custom_call_target="tpu_custom_call" | custom-call | flops 20124999680 | bytes 20125000 | tf_op jit(solution)/shard_map/cond/branch_1_fun/attend_back/pallas_call | solution.py:922
  234.4 5.1 %weights.3 = (bf16[480,768]{1,0:T(8,128)(2,1)}, bf16[480,768]{1,0:T(8,128)(2,1)}, f32[1,960]{1,0:T(1,128)}) custom-call(s32[11]{0:T(128)S(1)} %get-tuple-element.43.ids, bf16[1024,768]{1,0:T(8,128)(2,1)S(1)} %bitcast.54, bf16[1024,960]{1,0:T(8,128)(2,1)} %bitcast.52), custom_call_target="tpu_custom_call" | custom-call | flops 6899999744 | bytes 6900000 | tf_op jit(solution)/shard_map/cond/branch_1_fun/weights/pallas_call | solution.py:949
  246.3 4.7 %all-to-all-start.1 = ((bf16[8,88,768]{2,1,0:T(8,128)(2,1)}), bf16[8,88,768]{2,1,0:T(8,128)(2,1)}, u32[]{:S(2)}, u32[]{:S(2)}) async-start(bf16[8,88,768]{2,1,0:T(8,128)(2,1)} %bitcast.39), calls=%async_computation.1 | async-start | bytes 2162688 | tf_op jit(solution)/shard_map/cond/branch_1_fun/all_to_all | solution.py:871
  251.8 10.3 %input.1 = (bf16[384,768]{1,0:T(8,128)(2,1)}, bf16[384,768]{1,0:T(8,128)(2,1)}, bf16[384,768]{1,0:T(8,128)(2,1)}, bf16[384,768]{1,0:T(8,128)(2,1)}, f32[2,768]{1,0:T(2,128)}) custom-call(s32[11]{0:T(128)S(1)} %get-tuple-element.43.ids, bf16[4,256,960]{2,1,0:T(8,128)(2,1)} %get-tuple-element.61.own_ref, bf16[4,256,960]{2,1,0:T(8,128)(2,1)} %get-tuple-element.53.other_ref, ...), custom_call_target="tpu_custom_call" | custom-call | flops 10350000128 | bytes 10350000 | tf_op jit(solution)/shard_map/cond/branch_1_fun/input/pallas_call | solution.py:991
  272.1 11.7 %collective-permute-done.7 = f32[7104]{0:T(1024)S(1)} collective-permute-done((f32[7104]{0:T(1024)S(1)}, f32[7104]{0:T(1024)S(1)}, u32[]{:S(2)}, u32[]{:S(2)}) %collective-permute-start.7) | collective-permute-done | bytes 28448 | tf_op jit(solution)/shard_map/cond/branch_1_fun/ppermute | solution.py:691
  287.3 13.5 %collective-permute-done.8 = f32[7104]{0:T(1024)S(1)} collective-permute-done((f32[7104]{0:T(1024)S(1)}, f32[7104]{0:T(1024)S(1)}, u32[]{:S(2)}, u32[]{:S(2)}) %collective-permute-start.8) | collective-permute-done | bytes 28448 | tf_op jit(solution)/shard_map/cond/branch_1_fun/ppermute | solution.py:691
  307.8 4.3 %all-to-all-start.5 = ((bf16[8,88,768]{2,1,0:T(8,128)(2,1)}), bf16[8,88,768]{2,1,0:T(8,128)(2,1)S(1)}, u32[]{:S(2)}, u32[]{:S(2)}) async-start(bf16[8,88,768]{2,1,0:T(8,128)(2,1)} %spread_sum.1), calls=%async_computation.5 | async-start | bytes 2162688 | tf_op jit(solution)/shard_map/all_to_all | solution.py:875
  314.1 4.6 %collect.1 = (f32[4,256,768]{2,1,0:T(8,128)}, f32[192,2048]{1,0:T(8,128)}) custom-call(s32[11]{0:T(128)S(1)} %copy-done.19, bf16[384,768]{1,0:T(8,128)(2,1)} %get-tuple-element.242.refs_0_, bf16[384,768]{1,0:T(8,128)(2,1)} %get-tuple-element.243.refs_1_, bf16[384,768]{1,0:T(8,128)(2,1)} %get-tuple-element.244.refs_2_, ...), custom_call_target="tpu_custom_call" | custom-call | flops 5750000128 | bytes 5750000 | tf_op jit(solution)/shard_map/collect/pallas_call | solution.py:571
  321.8 7.1 %place_feed.1 = (f32[768,1536]{1,0:T(8,128)}, f32[1536,768]{1,0:T(8,128)}) custom-call(s32[11]{0:T(128)} %broadcast_add_fusion.ids, bf16[1536,768]{1,0:T(8,128)(2,1)} %all-reduce.2.cloned.1.call-done.mine_ref, bf16[1536,768]{1,0:T(8,128)(2,1)} %collective-permute-done.29.theirs_ref), custom_call_target="tpu_custom_call" | custom-call | flops 9200000000 | bytes 9200000 | tf_op jit(solution)/shard_map/place_feed/pallas_call | solution.py:593
  328.9 10.3 %all-to-all-done.5 = bf16[8,88,768]{2,1,0:T(8,128)(2,1)S(1)} async-done(((bf16[8,88,768]{2,1,0:T(8,128)(2,1)}), bf16[8,88,768]{2,1,0:T(8,128)(2,1)S(1)}, u32[]{:S(2)}, u32[]{:S(2)}) %all-to-all-start.5) | async-done | bytes 1081376 | tf_op jit(solution)/shard_map/all_to_all | solution.py:875
  342.9 4.2 %place_qkv.1 = (f32[768,384]{1,0:T(8,128)}, f32[768,384]{1,0:T(8,128)}, f32[192,768]{1,0:T(8,128)}, f32[384,768]{1,0:T(8,128)}) custom-call(s32[11]{0:T(128)S(1)} %copy-done.19, bf16[704,768]{1,0:T(8,128)(2,1)} %bitcast.41, bf16[704,768]{1,0:T(8,128)(2,1)} %copy-done.23), custom_call_target="tpu_custom_call" | custom-call | flops 4600000000 | bytes 4600000 | tf_op jit(solution)/shard_map/place_qkv/pallas_call | solution.py:627
  (204 shorter events, 110.3 us)
Async XLA Ops:
  11.2 26.2 %collective-permute-start.12 = (bf16[672,768]{1,0:T(8,128)(2,1)}, bf16[672,768]{1,0:T(8,128)(2,1)}, u32[]{:S(2)}, u32[]{:S(2)}) collective-permute-start(bf16[672,768]{1,0:T(8,128)(2,1)} %pad_maximum_fusion.2), channel_id=1, source_target_pairs={{0,1},{1,0},{2,3},{3,2},{4,5},{5,4},{6,7},{7,6},{8,9},{9,8},{10,11... | collective-permute-start | bytes 3096584 | tf_op jit(solution)/shard_map/ppermute | solution.py:697
  14.9 22.5 %collective-permute-start.13 = (f32[1344]{0:T(1024)}, f32[1344]{0:T(1024)}, u32[]{:S(2)}, u32[]{:S(2)}) collective-permute-start(f32[1344]{0:T(1024)} %concatenate.35), channel_id=1, source_target_pairs={{0,1},{1,0},{2,3},{3,2},{4,5},{5,4},{6,7},{7,6},{8,9},{9,8},{10,11... | collective-permute-start | bytes 16136 | tf_op jit(solution)/shard_map/ppermute | solution.py:697
  14.9 26.5 %all-to-all-start.2 = ((bf16[4,256,768]{2,1,0:T(8,128)(2,1)}), bf16[4,256,768]{2,1,0:T(8,128)(2,1)}, u32[]{:S(2)}, u32[]{:S(2)}) async-start(bf16[4,256,768]{2,1,0:T(8,128)(2,1)} %bitcast.15), calls=%async_computation.2 | async-start | bytes 3145728 | tf_op jit(solution)/shard_map/all_to_all | solution.py:700
  39.0 19.0 %collective-permute-start.17 = (bf16[384,768]{1,0:T(8,128)(2,1)}, bf16[384,768]{1,0:T(8,128)(2,1)}, u32[]{:S(2)}, u32[]{:S(2)}) collective-permute-start(bf16[384,768]{1,0:T(8,128)(2,1)} %constant_dynamic-slice_fusion), channel_id=1, source_target_pairs={{0,1},{1,0},{2,3},{3,2},{4,5},{5,4},{6,7},{7,6},{8,9},{9,8},{10,11... | collective-permute-start | bytes 1769480 | tf_op jit(solution)/shard_map/ppermute | solution.py:697
  41.3 15.1 %all-to-all-start.3 = ((bf16[4,128,768]{2,1,0:T(8,128)(2,1)}), bf16[4,128,768]{2,1,0:T(8,128)(2,1)S(1)}, u32[]{:S(2)}, u32[]{:S(2)}) async-start(bf16[4,128,768]{2,1,0:T(8,128)(2,1)} %reshape.129), calls=%async_computation.3 | async-start | bytes 1572864 | tf_op jit(solution)/shard_map/all_to_all | solution.py:700
  57.9 34.4 %all-to-all-start.4 = ((bf16[4,256,768]{2,1,0:T(8,128)(2,1)}), bf16[4,256,768]{2,1,0:T(8,128)(2,1)S(1)}, u32[]{:S(2)}, u32[]{:S(2)}) async-start(bf16[4,256,768]{2,1,0:T(8,128)(2,1)} %bitcast.34), calls=%async_computation.4 | async-start | bytes 3145728 | tf_op jit(solution)/shard_map/all_to_all | solution.py:700
  61.7 243.2 %all-reduce.2.cloned.1.call-start = ((), (), s32[]{:S(2)}) async-start(), calls=%async_computation.6 | async-start | bytes 4718592 | tf_op jit(solution)/shard_map/psum | solution.py:917
  61.9 32.9 %collective-permute-start.18 = (bf16[384,768]{1,0:T(8,128)(2,1)}, bf16[384,768]{1,0:T(8,128)(2,1)}, u32[]{:S(2)}, u32[]{:S(2)}) collective-permute-start(bf16[384,768]{1,0:T(8,128)(2,1)} %collective-permute-done.17.refs_2_), channel_id=1, source_target_pairs={{0,8},{2,10},{4,12},{6,14},{8,0},{10,2},{12,4},{14,6},{16,24},{18,... | collective-permute-start | bytes 1769480 | tf_op jit(solution)/shard_map/ppermute | solution.py:691
  63.8 31.0 %collective-permute-start.19 = (bf16[768,768]{1,0:T(8,128)(2,1)S(1)}, bf16[768,768]{1,0:T(8,128)(2,1)}, u32[]{:S(2)}, u32[]{:S(2)}) collective-permute-start(bf16[768,768]{1,0:T(8,128)(2,1)S(1)} %copy-done.10), channel_id=1, source_target_pairs={{0,1},{1,0},{2,3},{3,2},{4,5},{5,4},{6,7},{7,6},{8,9},{9,8},{10,11... | collective-permute-start | bytes 3538952 | tf_op jit(solution)/shard_map/ppermute | solution.py:697
  121.6 20.0 %collective-permute-start.21 = (bf16[384,768]{1,0:T(8,128)(2,1)}, bf16[384,768]{1,0:T(8,128)(2,1)S(1)}, u32[]{:S(2)}, u32[]{:S(2)}) collective-permute-start(bf16[384,768]{1,0:T(8,128)(2,1)} %get-tuple-element.207), channel_id=1, source_target_pairs={{0,1},{1,0},{2,3},{3,2},{4,5},{5,4},{6,7},{7,6},{8,9},{9,8},{10,11... | collective-permute-start | bytes 1769480 | tf_op jit(solution)/shard_map/ppermute | solution.py:697
  121.6 16.4 %collective-permute-start.22 = (bf16[384,768]{1,0:T(8,128)(2,1)}, bf16[384,768]{1,0:T(8,128)(2,1)S(1)}, u32[]{:S(2)}, u32[]{:S(2)}) collective-permute-start(bf16[384,768]{1,0:T(8,128)(2,1)} %get-tuple-element.208), channel_id=1, source_target_pairs={{0,8},{2,10},{4,12},{6,14},{8,0},{10,2},{12,4},{14,6},{16,24},{18,... | collective-permute-start | bytes 1769480 | tf_op jit(solution)/shard_map/ppermute | solution.py:691
  137.5 21.2 %collective-permute-start.25 = (bf16[1024,768]{1,0:T(8,128)(2,1)}, bf16[1024,768]{1,0:T(8,128)(2,1)S(1)}, u32[]{:S(2)}, u32[]{:S(2)}) collective-permute-start(bf16[1024,768]{1,0:T(8,128)(2,1)} %get-tuple-element.224), channel_id=1, source_target_pairs={{0,2},{2,0},{4,6},{6,4},{8,10},{10,8},{12,14},{14,12},{16,18},{18,... | collective-permute-start | bytes 4718600 | tf_op jit(solution)/shard_map/ppermute | solution.py:691
  137.5 21.3 %collective-permute-start.24 = (bf16[1024,768]{1,0:T(8,128)(2,1)}, bf16[1024,768]{1,0:T(8,128)(2,1)S(1)}, u32[]{:S(2)}, u32[]{:S(2)}) collective-permute-start(bf16[1024,768]{1,0:T(8,128)(2,1)} %get-tuple-element.213), channel_id=1, source_target_pairs={{0,2},{2,0},{4,6},{6,4},{8,10},{10,8},{12,14},{14,12},{16,18},{18,... | collective-permute-start | bytes 4718600 | tf_op jit(solution)/shard_map/ppermute | solution.py:691
  141.6 15.8 %collective-permute-start.23 = (bf16[384,768]{1,0:T(8,128)(2,1)S(1)}, bf16[384,768]{1,0:T(8,128)(2,1)S(1)}, u32[]{:S(2)}, u32[]{:S(2)}) collective-permute-start(bf16[384,768]{1,0:T(8,128)(2,1)S(1)} %copy-done.27), channel_id=1, source_target_pairs={{0,1},{1,0},{2,3},{3,2},{4,5},{5,4},{6,7},{7,6},{8,9},{9,8},{10,11... | collective-permute-start | bytes 1769480 | tf_op jit(solution)/shard_map/ppermute | solution.py:697
  181.4 35.4 %all-to-all-start = ((bf16[4,256,768]{2,1,0:T(8,128)(2,1)}), bf16[4,256,768]{2,1,0:T(8,128)(2,1)S(1)}, u32[]{:S(2)}, u32[]{:S(2)}) async-start(bf16[4,256,768]{2,1,0:T(8,128)(2,1)} %get-tuple-element.42), calls=%async_computation | async-start | bytes 3145728 | tf_op jit(solution)/shard_map/cond/branch_1_fun/all_to_all | solution.py:700
  186.2 17.9 %collective-permute-start = (bf16[192,768]{1,0:T(8,128)(2,1)S(1)}, bf16[192,768]{1,0:T(8,128)(2,1)S(1)}, u32[]{:S(2)}, u32[]{:S(2)}) collective-permute-start(bf16[192,768]{1,0:T(8,128)(2,1)S(1)} %slice_bitcast_fusion), channel_id=1, source_target_pairs={{0,1},{1,0},{2,3},{3,2},{4,5},{5,4},{6,7},{7,6},{8,9},{9,8},{10,11... | collective-permute-start | bytes 884744 | tf_op jit(solution)/shard_map/cond/branch_1_fun/ppermute | solution.py:697
  215.5 18.9 %collective-permute-start.2 = (bf16[480,768]{1,0:T(8,128)(2,1)}, bf16[480,768]{1,0:T(8,128)(2,1)}, u32[]{:S(2)}, u32[]{:S(2)}) collective-permute-start(bf16[480,768]{1,0:T(8,128)(2,1)} %fold.4), channel_id=1, source_target_pairs={{0,1},{1,0},{2,3},{3,2},{4,5},{5,4},{6,7},{7,6},{8,9},{9,8},{10,11... | collective-permute-start | bytes 2211848 | tf_op jit(solution)/shard_map/cond/branch_1_fun/ppermute | solution.py:697
  246.3 54.6 %all-to-all-start.1 = ((bf16[8,88,768]{2,1,0:T(8,128)(2,1)}), bf16[8,88,768]{2,1,0:T(8,128)(2,1)}, u32[]{:S(2)}, u32[]{:S(2)}) async-start(bf16[8,88,768]{2,1,0:T(8,128)(2,1)} %bitcast.39), calls=%async_computation.1 | async-start | bytes 2162688 | tf_op jit(solution)/shard_map/cond/branch_1_fun/all_to_all | solution.py:871
  262.1 38.7 %collective-permute-start.9 = (bf16[384,768]{1,0:T(8,128)(2,1)}, bf16[384,768]{1,0:T(8,128)(2,1)}, u32[]{:S(2)}, u32[]{:S(2)}) collective-permute-start(bf16[384,768]{1,0:T(8,128)(2,1)} %get-tuple-element.80), channel_id=1, source_target_pairs={{0,2},{2,0},{4,6},{6,4},{8,10},{10,8},{12,14},{14,12},{16,18},{18,... | collective-permute-start | bytes 1769480 | tf_op jit(solution)/shard_map/cond/branch_1_fun/ppermute | solution.py:691
  262.2 38.7 %collective-permute-start.10 = (bf16[384,768]{1,0:T(8,128)(2,1)}, bf16[384,768]{1,0:T(8,128)(2,1)}, u32[]{:S(2)}, u32[]{:S(2)}) collective-permute-start(bf16[384,768]{1,0:T(8,128)(2,1)} %get-tuple-element.81), channel_id=1, source_target_pairs={{0,4},{2,6},{4,0},{6,2},{8,12},{10,14},{12,8},{14,10},{16,20},{18,... | collective-permute-start | bytes 1769480 | tf_op jit(solution)/shard_map/cond/branch_1_fun/ppermute | solution.py:691
  264.3 36.6 %collective-permute-start.11 = (bf16[384,768]{1,0:T(8,128)(2,1)}, bf16[384,768]{1,0:T(8,128)(2,1)}, u32[]{:S(2)}, u32[]{:S(2)}) collective-permute-start(bf16[384,768]{1,0:T(8,128)(2,1)} %get-tuple-element.82), channel_id=1, source_target_pairs={{0,6},{2,4},{4,2},{6,0},{8,14},{10,12},{12,10},{14,8},{16,22},{18,... | collective-permute-start | bytes 1769480 | tf_op jit(solution)/shard_map/cond/branch_1_fun/ppermute | solution.py:691
  283.8 17.1 %collective-permute-start.8 = (f32[7104]{0:T(1024)S(1)}, f32[7104]{0:T(1024)S(1)}, u32[]{:S(2)}, u32[]{:S(2)}) collective-permute-start(f32[7104]{0:T(1024)S(1)} %add.56), channel_id=1, source_target_pairs={{0,16},{2,18},{4,20},{6,22},{8,24},{10,26},{12,28},{14,30},{16,0},... | collective-permute-start | bytes 85256 | tf_op jit(solution)/shard_map/cond/branch_1_fun/ppermute | solution.py:691
  304.9 16.9 %collective-permute-start.29 = (bf16[1536,768]{1,0:T(8,128)(2,1)}, bf16[1536,768]{1,0:T(8,128)(2,1)}, u32[]{:S(2)}, u32[]{:S(2)}) collective-permute-start(bf16[1536,768]{1,0:T(8,128)(2,1)} %all-reduce.2.cloned.1.call-done.mine_ref), channel_id=1, source_target_pairs={{0,2},{2,0},{4,6},{6,4},{8,10},{10,8},{12,14},{14,12},{16,18},{18,... | collective-permute-start | bytes 7077896 | tf_op jit(solution)/shard_map/ppermute | solution.py:691
  307.8 31.4 %all-to-all-start.5 = ((bf16[8,88,768]{2,1,0:T(8,128)(2,1)}), bf16[8,88,768]{2,1,0:T(8,128)(2,1)S(1)}, u32[]{:S(2)}, u32[]{:S(2)}) async-start(bf16[8,88,768]{2,1,0:T(8,128)(2,1)} %spread_sum.1), calls=%async_computation.5 | async-start | bytes 2162688 | tf_op jit(solution)/shard_map/all_to_all | solution.py:875
  (54 other events, 466.8 us)
Sparse Core Ops, SparseCore 0:
  178.3 126.5 all-reduce.1

commit v5 on v4

--- a/solution.py
+++ b/solution.py
@@ -189,7 +189,7 @@
         bias = jnp.where(seen, 0.0, MASKED)
         head_lane = lax.broadcasted_iota(jnp.int32, (1, 128), 1)
 
-        @pl.loop(0, width // PAIR, unroll=3)
+        @pl.loop(0, width // PAIR, unroll=6)
         def _(pair):
             lanes = pl.ds(pl.multiple_of(pair * PAIR, PAIR), PAIR)
             queries = q_ref[:, lanes]

time: 362 us -> 361 us (level)
  Pallas kernels: 187 us -> 179 us
  starting transfers between devices: 54.2 us -> 58.7 us
    pallas_call x1, Pallas kernels: 24.3 us -> 19.7 us  [per_device(): call(attend_kernel, 1, (SPAN,), [placed(width), in_rows(width), full(flat...]
    ppermute x12, waiting for transfers between devices: 10.7 us -> 14.6 us  [swap_tp(): return lax.ppermute(value, 'tp', [(i, i ^ 1) for i in range(tp_count)])]
  transfers between devices with their start and end apart: 38 -> 38, of which waited for: 15 -> 17; matrix products, arithmetic and copies ran while one was open for 7% -> 7% of each run, Pallas kernels for 46% -> 44%
where the time goes in v5:
time: 361 us; the launch traced here: 355 us
  Pallas kernels  179 us (50%)
  waiting for transfers between devices  62.7 us (17%)
  starting transfers between devices  58.7 us (16%)
  local copies, waits for them, and re-layouts  30.5 us (8%)
  between operations  16.4 us (5%)
  other arithmetic  7.81 us (2%)
    pallas_call x4, Pallas kernels, feed(): call(partial(feed_kernel, len(weights) > 1, len(sums) > 0, len(made) > 0,...  52.9 us
    ppermute x19, waiting for transfers between devices, swap_seq(): lax.ppermute(value, 'seq', [(i, i ^ distance) for i in range(seq_count)])  33.9 us
    pallas_call x2, Pallas kernels, attend_back(): call(partial(attend_back_kernel, which * (heads // 2)), 1, (SPAN,), [pl.B...  31.7 us
    pallas_call x1, Pallas kernels, per_device(): call(attend_kernel, 1, (SPAN,), [placed(width), in_rows(width), full(flat...  19.7 us
    ppermute x12, starting transfers between devices, swap_tp(): return lax.ppermute(value, 'tp', [(i, i ^ 1) for i in range(tp_count)])  17.2 us
    ppermute x19, starting transfers between devices, swap_seq(): lax.ppermute(value, 'seq', [(i, i ^ distance) for i in range(seq_count)])  15.6 us
    all_to_all x4, starting transfers between devices, to_seqs(): lax.all_to_all(value, 'seq', 0, 0, tiled=True, axis_index_groups=members)  15.3 us
    ppermute x12, waiting for transfers between devices, swap_tp(): return lax.ppermute(value, 'tp', [(i, i ^ 1) for i in range(tp_count)])  14.6 us
  transfers between devices with their start and end apart: 38, of which 17 were waited for; matrix products, arithmetic and copies ran while one was open for 7% of the time, Pallas kernels for 44%

profile of v5, /device:TPU:0, one launch (start us, length us, event | category | flops | bytes accessed | tf_op | source)
XLA Modules:
  0.0 355.3 jit_solution(11693015940811150765)
XLA Ops:
  14.9 4.4 %all-to-all-start.2 = ((bf16[4,256,768]{2,1,0:T(8,128)(2,1)}), bf16[4,256,768]{2,1,0:T(8,128)(2,1)}, u32[]{:S(2)}, u32[]{:S(2)}) async-start(bf16[4,256,768]{2,1,0:T(8,128)(2,1)} %bitcast.15), calls=%async_computation.2 | async-start | bytes 3145728 | tf_op jit(solution)/shard_map/all_to_all | solution.py:700
  32.1 5.3 %collective-permute-done.13 = f32[1344]{0:T(1024)} collective-permute-done((f32[1344]{0:T(1024)}, f32[1344]{0:T(1024)}, u32[]{:S(2)}, u32[]{:S(2)}) %collective-permute-start.13) | collective-permute-done | bytes 5408 | tf_op jit(solution)/shard_map/ppermute | solution.py:697
  44.9 9.5 %project.1 = (bf16[4,256,768]{2,1,0:T(8,128)(2,1)}, bf16[1024,768]{1,0:T(8,128)(2,1)}, bf16[1024,768]{1,0:T(8,128)(2,1)}, bf16[2,1024,192]{2,1,0:T(8,128)(2,1)},...) custom-call(s32[11]{0:T(128)S(1)} %concatenate.31.ids, bf16[4,256,768]{2,1,0:T(8,128)(2,1)} %all-to-all-done.2.x_ref, ...), custom_call_target="tpu_custom_call" | custom-call | flops 10350000128 | bytes 10350000 | tf_op jit(solution)/shard_map/project/pallas_call | solution.py:777
  67.9 19.7 %attend.1 = (bf16[1024,768]{1,0:T(8,128)(2,1)}, bf16[4,256,768]{2,1,0:T(8,128)(2,1)}, f32[16,1024]{1,0:T(8,128)S(1)}, bf16[4,256,768]{2,1,0:T(8,128)(2,1)}, bf16[4,256,768]{2,1,0:T(8,128)(2,1)}) custom-call(s32[11]{0:T(128)S(1)} %copy-done.19, bf16[4,256,768]{2,1,0:T(8,128)(2,1)} %all-to-all-done.2.x_ref, bf16[1024,768]{1,0:T(8,128)(2,1)} %get-tuple-element.192.q_ref, ...), custom_call_target="tpu_custom_call" | custom-call | flops 31050000384 | bytes 31050000 | tf_op jit(solution)/shard_map/attend/pallas_call | solution.py:810
  92.6 12.4 %feed.4 = (bf16[1024,768]{1,0:T(8,128)(2,1)}, bf16[1024,768]{1,0:T(8,128)(2,1)}, f32[1,768]{1,0:T(1,128)S(1)}, bf16[1536,768]{1,0:T(8,128)(2,1)}) custom-call(s32[11]{0:T(128)S(1)} %copy-done.19, bf16[1024,768]{1,0:T(8,128)(2,1)} %bitcast.48, bf16[1024,768]{1,0:T(8,128)(2,1)} %bitcast.36, bf16[384,768]{1,0:T(8,128)(2,1)} %collective-permute-done.17.refs_2_, ...), custom_call_target="tpu_custom_call" | custom-call | flops 16099999744 | bytes 16100000 | tf_op jit(solution)/shard_map/feed/pallas_call | solution.py:296
  106.1 13.2 %feed.5 = (bf16[1024,768]{1,0:T(8,128)(2,1)}, bf16[1024,768]{1,0:T(8,128)(2,1)}, f32[1,768]{1,0:T(1,128)S(1)}, bf16[384,768]{1,0:T(8,128)(2,1)}, bf16[384,768]{1...) custom-call(s32[11]{0:T(128)S(1)} %copy-done.19, ...), custom_call_target="tpu_custom_call" | custom-call | flops 16099999744 | bytes 16100000 | tf_op jit(solution)/shard_map/feed/pallas_call | solution.py:296
  122.9 13.4 %feed.6 = (bf16[1024,768]{1,0:T(8,128)(2,1)}, bf16[1024,768]{1,0:T(8,128)(2,1)}, f32[1,768]{1,0:T(1,128)S(1)}, bf16[1536,768]{1,0:T(8,128)(2,1)}) custom-call(s32[11]{0:T(128)S(1)} %copy-done.19, bf16[1024,768]{1,0:T(8,128)(2,1)} %collective-permute-done.16.refs_0_, bf16[1024,768]{1,0:T(8,128)(2,1)} %copy-done.22, bf16[1536,768]{1,0:T(8,128)(2,1)} %copy-done.2, ...), custom_call_target="tpu_custom_call" | custom-call | flops 16099999744 | bytes 16100000 | tf_op jit(solution)/shard_map/feed/pallas_call | solution.py:296
  142.4 13.9 %feed.7 = (bf16[1024,768]{1,0:T(8,128)(2,1)}, bf16[1024,768]{1,0:T(8,128)(2,1)}, f32[1,768]{1,0:T(1,128)S(1)}, bf16[384,768]{1,0:T(8,128)(2,1)}, bf16[384,768]{1...) custom-call(s32[11]{0:T(128)S(1)} %copy-done.19, bf16[1024,768]{1,0:T(8,128)(2,1)} %bitcast.49, ...), custom_call_target="tpu_custom_call" | custom-call | flops 16099999744 | bytes 16100000 | tf_op jit(solution)/shard_map/feed/pallas_call | solution.py:296
  159.3 11.6 %residual.1 = (bf16[4,256,768]{2,1,0:T(8,128)(2,1)}, bf16[4,256,768]{2,1,0:T(8,128)(2,1)}, bf16[4,256,768]{2,1,0:T(8,128)(2,1)}, bf16[2,192,768]{2,1,0:T(8,128)(...) custom-call(s32[11]{0:T(128)S(1)} %copy-done.19, bf16[1024,768]{1,0:T(8,128)(2,1)} %get-tuple-element.222.out_a, ...), custom_call_target="tpu_custom_call" | custom-call | flops 14375000064 | bytes 14375000 | tf_op jit(solution)/shard_map/residual/pallas_call | solution.py:878
  172.1 4.9 %fold.7 = bf16[1536,768]{1,0:T(8,128)(2,1)} custom-call(s32[11]{0:T(128)S(1)} %copy-done.19, bf16[384,768]{1,0:T(8,128)(2,1)} %get-tuple-element.250.refs_0_, bf16[384,768]{1,0:T(8,128)(2,1)} %copy-done.26, bf16[384,768]{1,0:T(8,128)(2,1)} %get-tuple-element.251.refs_2_, bf16[384,768]{1,0:T(8,128)(2,1)} %copy-done.29, ...), custom_call_target="tpu_custom_call" | custom-call | flops 4024999936 | bytes 4025000 | tf_op jit(solution)/shard_map/fold/pallas_call | solution.py:521
  180.3 120.7 %conditional.1 = (bf16[1024,768]{1,0:T(8,128)(2,1)S(1)}, bf16[8,88,768]{2,1,0:T(8,128)(2,1)}, f32[7104]{0:T(1024)S(1)}, bf16[384,768]{1,0:T(8,128)(2,1)}, bf16[3...) conditional(s32[]{:T(128)} %convert_element_type.18, () %tuple.41, ...), branch_computations={%region_3.4_spmd, %region_4.5_spmd} | conditional | flops 72450031616 | bytes 138468224 | solution.py:1028
  185.9 15.6 %attend_back.2 = (bf16[4,256,960]{2,1,0:T(8,128)(2,1)}, bf16[4,64,768]{2,1,0:T(8,128)(2,1)}) custom-call(s32[11]{0:T(128)S(1)} %get-tuple-element.43.ids, bf16[1024,768]{1,0:T(8,128)(2,1)} %get-tuple-element.56.q_ref, bf16[1024,768]{1,0:T(8,128)(2,1)} %get-tuple-element.46.k_ref, bf16[1024,768]{1,0:T(8,128)(2,1)} %get-tuple-element.47.v_ref, ...), custom_call_target="tpu_custom_call" | custom-call | flops 20124999680 | bytes 20125000 | tf_op jit(solution)/shard_map/cond/branch_1_fun/attend_back/pallas_call | solution.py:922
  201.5 5.1 %weights.2 = (bf16[480,768]{1,0:T(8,128)(2,1)}, bf16[480,768]{1,0:T(8,128)(2,1)}, f32[1,960]{1,0:T(1,128)}) custom-call(s32[11]{0:T(128)S(1)} %get-tuple-element.43.ids, bf16[1024,768]{1,0:T(8,128)(2,1)S(1)} %bitcast.53, bf16[1024,960]{1,0:T(8,128)(2,1)} %bitcast.51), custom_call_target="tpu_custom_call" | custom-call | flops 6899999744 | bytes 6900000 | tf_op jit(solution)/shard_map/cond/branch_1_fun/weights/pallas_call | solution.py:949
  215.5 16.1 %attend_back.3 = (bf16[4,256,960]{2,1,0:T(8,128)(2,1)}, bf16[4,64,768]{2,1,0:T(8,128)(2,1)}) custom-call(s32[11]{0:T(128)S(1)} %get-tuple-element.43.ids, bf16[1024,768]{1,0:T(8,128)(2,1)} %get-tuple-element.56.q_ref, bf16[1024,768]{1,0:T(8,128)(2,1)} %get-tuple-element.46.k_ref, bf16[1024,768]{1,0:T(8,128)(2,1)} %get-tuple-element.47.v_ref, ...), custom_call_target="tpu_custom_call" | custom-call | flops 20124999680 | bytes 20125000 | tf_op jit(solution)/shard_map/cond/branch_1_fun/attend_back/pallas_call | solution.py:922
  232.8 5.1 %weights.3 = (bf16[480,768]{1,0:T(8,128)(2,1)}, bf16[480,768]{1,0:T(8,128)(2,1)}, f32[1,960]{1,0:T(1,128)}) custom-call(s32[11]{0:T(128)S(1)} %get-tuple-element.43.ids, bf16[1024,768]{1,0:T(8,128)(2,1)S(1)} %bitcast.54, bf16[1024,960]{1,0:T(8,128)(2,1)} %bitcast.52), custom_call_target="tpu_custom_call" | custom-call | flops 6899999744 | bytes 6900000 | tf_op jit(solution)/shard_map/cond/branch_1_fun/weights/pallas_call | solution.py:949
  244.7 6.0 %all-to-all-start.1 = ((bf16[8,88,768]{2,1,0:T(8,128)(2,1)}), bf16[8,88,768]{2,1,0:T(8,128)(2,1)}, u32[]{:S(2)}, u32[]{:S(2)}) async-start(bf16[8,88,768]{2,1,0:T(8,128)(2,1)} %bitcast.39), calls=%async_computation.1 | async-start | bytes 2162688 | tf_op jit(solution)/shard_map/cond/branch_1_fun/all_to_all | solution.py:871
  251.6 10.3 %input.1 = (bf16[384,768]{1,0:T(8,128)(2,1)}, bf16[384,768]{1,0:T(8,128)(2,1)}, bf16[384,768]{1,0:T(8,128)(2,1)}, bf16[384,768]{1,0:T(8,128)(2,1)}, f32[2,768]{1,0:T(2,128)}) custom-call(s32[11]{0:T(128)S(1)} %get-tuple-element.43.ids, bf16[4,256,960]{2,1,0:T(8,128)(2,1)} %get-tuple-element.61.own_ref, bf16[4,256,960]{2,1,0:T(8,128)(2,1)} %get-tuple-element.53.other_ref, ...), custom_call_target="tpu_custom_call" | custom-call | flops 10350000128 | bytes 10350000 | tf_op jit(solution)/shard_map/cond/branch_1_fun/input/pallas_call | solution.py:991
  271.9 11.5 %collective-permute-done.7 = f32[7104]{0:T(1024)S(1)} collective-permute-done((f32[7104]{0:T(1024)S(1)}, f32[7104]{0:T(1024)S(1)}, u32[]{:S(2)}, u32[]{:S(2)}) %collective-permute-start.7) | collective-permute-done | bytes 28448 | tf_op jit(solution)/shard_map/cond/branch_1_fun/ppermute | solution.py:691
  286.9 13.6 %collective-permute-done.8 = f32[7104]{0:T(1024)S(1)} collective-permute-done((f32[7104]{0:T(1024)S(1)}, f32[7104]{0:T(1024)S(1)}, u32[]{:S(2)}, u32[]{:S(2)}) %collective-permute-start.8) | collective-permute-done | bytes 28448 | tf_op jit(solution)/shard_map/cond/branch_1_fun/ppermute | solution.py:691
  307.4 4.3 %all-to-all-start.5 = ((bf16[8,88,768]{2,1,0:T(8,128)(2,1)}), bf16[8,88,768]{2,1,0:T(8,128)(2,1)S(1)}, u32[]{:S(2)}, u32[]{:S(2)}) async-start(bf16[8,88,768]{2,1,0:T(8,128)(2,1)} %spread_sum.1), calls=%async_computation.5 | async-start | bytes 2162688 | tf_op jit(solution)/shard_map/all_to_all | solution.py:875
  313.7 4.6 %collect.1 = (f32[4,256,768]{2,1,0:T(8,128)}, f32[192,2048]{1,0:T(8,128)}) custom-call(s32[11]{0:T(128)S(1)} %copy-done.19, bf16[384,768]{1,0:T(8,128)(2,1)} %get-tuple-element.242.refs_0_, bf16[384,768]{1,0:T(8,128)(2,1)} %get-tuple-element.243.refs_1_, bf16[384,768]{1,0:T(8,128)(2,1)} %get-tuple-element.244.refs_2_, ...), custom_call_target="tpu_custom_call" | custom-call | flops 5750000128 | bytes 5750000 | tf_op jit(solution)/shard_map/collect/pallas_call | solution.py:571
  321.4 7.1 %place_feed.1 = (f32[768,1536]{1,0:T(8,128)}, f32[1536,768]{1,0:T(8,128)}) custom-call(s32[11]{0:T(128)} %broadcast_add_fusion.ids, bf16[1536,768]{1,0:T(8,128)(2,1)} %all-reduce.2.cloned.1.call-done.mine_ref, bf16[1536,768]{1,0:T(8,128)(2,1)} %collective-permute-done.29.theirs_ref), custom_call_target="tpu_custom_call" | custom-call | flops 9200000000 | bytes 9200000 | tf_op jit(solution)/shard_map/place_feed/pallas_call | solution.py:593
  328.6 10.3 %all-to-all-done.5 = bf16[8,88,768]{2,1,0:T(8,128)(2,1)S(1)} async-done(((bf16[8,88,768]{2,1,0:T(8,128)(2,1)}), bf16[8,88,768]{2,1,0:T(8,128)(2,1)S(1)}, u32[]{:S(2)}, u32[]{:S(2)}) %all-to-all-start.5) | async-done | bytes 1081376 | tf_op jit(solution)/shard_map/all_to_all | solution.py:875
  342.5 4.2 %place_qkv.1 = (f32[768,384]{1,0:T(8,128)}, f32[768,384]{1,0:T(8,128)}, f32[192,768]{1,0:T(8,128)}, f32[384,768]{1,0:T(8,128)}) custom-call(s32[11]{0:T(128)S(1)} %copy-done.19, bf16[704,768]{1,0:T(8,128)(2,1)} %bitcast.41, bf16[704,768]{1,0:T(8,128)(2,1)} %copy-done.23), custom_call_target="tpu_custom_call" | custom-call | flops 4600000000 | bytes 4600000 | tf_op jit(solution)/shard_map/place_qkv/pallas_call | solution.py:627
  (204 shorter events, 116.4 us)
Async XLA Ops:
  11.2 26.2 %collective-permute-start.12 = (bf16[672,768]{1,0:T(8,128)(2,1)}, bf16[672,768]{1,0:T(8,128)(2,1)}, u32[]{:S(2)}, u32[]{:S(2)}) collective-permute-start(bf16[672,768]{1,0:T(8,128)(2,1)} %pad_maximum_fusion.2), channel_id=1, source_target_pairs={{0,1},{1,0},{2,3},{3,2},{4,5},{5,4},{6,7},{7,6},{8,9},{9,8},{10,11... | collective-permute-start | bytes 3096584 | tf_op jit(solution)/shard_map/ppermute | solution.py:697
  14.9 22.5 %collective-permute-start.13 = (f32[1344]{0:T(1024)}, f32[1344]{0:T(1024)}, u32[]{:S(2)}, u32[]{:S(2)}) collective-permute-start(f32[1344]{0:T(1024)} %concatenate.35), channel_id=1, source_target_pairs={{0,1},{1,0},{2,3},{3,2},{4,5},{5,4},{6,7},{7,6},{8,9},{9,8},{10,11... | collective-permute-start | bytes 16136 | tf_op jit(solution)/shard_map/ppermute | solution.py:697
  14.9 26.5 %all-to-all-start.2 = ((bf16[4,256,768]{2,1,0:T(8,128)(2,1)}), bf16[4,256,768]{2,1,0:T(8,128)(2,1)}, u32[]{:S(2)}, u32[]{:S(2)}) async-start(bf16[4,256,768]{2,1,0:T(8,128)(2,1)} %bitcast.15), calls=%async_computation.2 | async-start | bytes 3145728 | tf_op jit(solution)/shard_map/all_to_all | solution.py:700
  39.0 19.0 %collective-permute-start.17 = (bf16[384,768]{1,0:T(8,128)(2,1)}, bf16[384,768]{1,0:T(8,128)(2,1)}, u32[]{:S(2)}, u32[]{:S(2)}) collective-permute-start(bf16[384,768]{1,0:T(8,128)(2,1)} %constant_dynamic-slice_fusion), channel_id=1, source_target_pairs={{0,1},{1,0},{2,3},{3,2},{4,5},{5,4},{6,7},{7,6},{8,9},{9,8},{10,11... | collective-permute-start | bytes 1769480 | tf_op jit(solution)/shard_map/ppermute | solution.py:697
  57.9 29.8 %all-to-all-start.4 = ((bf16[4,256,768]{2,1,0:T(8,128)(2,1)}), bf16[4,256,768]{2,1,0:T(8,128)(2,1)S(1)}, u32[]{:S(2)}, u32[]{:S(2)}) async-start(bf16[4,256,768]{2,1,0:T(8,128)(2,1)} %bitcast.34), calls=%async_computation.4 | async-start | bytes 3145728 | tf_op jit(solution)/shard_map/all_to_all | solution.py:700
  61.7 242.8 %all-reduce.2.cloned.1.call-start = ((), (), s32[]{:S(2)}) async-start(), calls=%async_computation.6 | async-start | bytes 4718592 | tf_op jit(solution)/shard_map/psum | solution.py:917
  61.9 28.3 %collective-permute-start.18 = (bf16[384,768]{1,0:T(8,128)(2,1)}, bf16[384,768]{1,0:T(8,128)(2,1)}, u32[]{:S(2)}, u32[]{:S(2)}) collective-permute-start(bf16[384,768]{1,0:T(8,128)(2,1)} %collective-permute-done.17.refs_2_), channel_id=1, source_target_pairs={{0,8},{2,10},{4,12},{6,14},{8,0},{10,2},{12,4},{14,6},{16,24},{18,... | collective-permute-start | bytes 1769480 | tf_op jit(solution)/shard_map/ppermute | solution.py:691
  63.8 28.8 %collective-permute-start.19 = (bf16[768,768]{1,0:T(8,128)(2,1)S(1)}, bf16[768,768]{1,0:T(8,128)(2,1)}, u32[]{:S(2)}, u32[]{:S(2)}) collective-permute-start(bf16[768,768]{1,0:T(8,128)(2,1)S(1)} %copy-done.10), channel_id=1, source_target_pairs={{0,1},{1,0},{2,3},{3,2},{4,5},{5,4},{6,7},{7,6},{8,9},{9,8},{10,11... | collective-permute-start | bytes 3538952 | tf_op jit(solution)/shard_map/ppermute | solution.py:697
  87.6 17.4 %collective-permute-start.16 = (bf16[1024,768]{1,0:T(8,128)(2,1)}, bf16[1024,768]{1,0:T(8,128)(2,1)}, u32[]{:S(2)}, u32[]{:S(2)}) collective-permute-start(bf16[1024,768]{1,0:T(8,128)(2,1)} %bitcast.47), channel_id=1, source_target_pairs={{0,2},{2,0},{4,6},{6,4},{8,10},{10,8},{12,14},{14,12},{16,18},{18,... | collective-permute-start | bytes 4718600 | tf_op jit(solution)/shard_map/ppermute | solution.py:691
  87.7 17.3 %collective-permute-start.20 = (bf16[1024,768]{1,0:T(8,128)(2,1)S(1)}, bf16[1024,768]{1,0:T(8,128)(2,1)S(1)}, u32[]{:S(2)}, u32[]{:S(2)}) collective-permute-start(bf16[1024,768]{1,0:T(8,128)(2,1)S(1)} %bitcast.35), channel_id=1, source_target_pairs={{0,2},{2,0},{4,6},{6,4},{8,10},{10,8},{12,14},{14,12},{16,18},{18,... | collective-permute-start | bytes 4718600 | tf_op jit(solution)/shard_map/ppermute | solution.py:691
  119.4 21.0 %collective-permute-start.21 = (bf16[384,768]{1,0:T(8,128)(2,1)}, bf16[384,768]{1,0:T(8,128)(2,1)S(1)}, u32[]{:S(2)}, u32[]{:S(2)}) collective-permute-start(bf16[384,768]{1,0:T(8,128)(2,1)} %get-tuple-element.207), channel_id=1, source_target_pairs={{0,1},{1,0},{2,3},{3,2},{4,5},{5,4},{6,7},{7,6},{8,9},{9,8},{10,11... | collective-permute-start | bytes 1769480 | tf_op jit(solution)/shard_map/ppermute | solution.py:697
  120.2 16.7 %collective-permute-start.22 = (bf16[384,768]{1,0:T(8,128)(2,1)}, bf16[384,768]{1,0:T(8,128)(2,1)S(1)}, u32[]{:S(2)}, u32[]{:S(2)}) collective-permute-start(bf16[384,768]{1,0:T(8,128)(2,1)} %get-tuple-element.208), channel_id=1, source_target_pairs={{0,8},{2,10},{4,12},{6,14},{8,0},{10,2},{12,4},{14,6},{16,24},{18,... | collective-permute-start | bytes 1769480 | tf_op jit(solution)/shard_map/ppermute | solution.py:691
  136.3 21.3 %collective-permute-start.25 = (bf16[1024,768]{1,0:T(8,128)(2,1)}, bf16[1024,768]{1,0:T(8,128)(2,1)S(1)}, u32[]{:S(2)}, u32[]{:S(2)}) collective-permute-start(bf16[1024,768]{1,0:T(8,128)(2,1)} %get-tuple-element.224), channel_id=1, source_target_pairs={{0,2},{2,0},{4,6},{6,4},{8,10},{10,8},{12,14},{14,12},{16,18},{18,... | collective-permute-start | bytes 4718600 | tf_op jit(solution)/shard_map/ppermute | solution.py:691
  136.3 21.3 %collective-permute-start.24 = (bf16[1024,768]{1,0:T(8,128)(2,1)}, bf16[1024,768]{1,0:T(8,128)(2,1)S(1)}, u32[]{:S(2)}, u32[]{:S(2)}) collective-permute-start(bf16[1024,768]{1,0:T(8,128)(2,1)} %get-tuple-element.213), channel_id=1, source_target_pairs={{0,2},{2,0},{4,6},{6,4},{8,10},{10,8},{12,14},{14,12},{16,18},{18,... | collective-permute-start | bytes 4718600 | tf_op jit(solution)/shard_map/ppermute | solution.py:691
  180.3 35.2 %all-to-all-start = ((bf16[4,256,768]{2,1,0:T(8,128)(2,1)}), bf16[4,256,768]{2,1,0:T(8,128)(2,1)S(1)}, u32[]{:S(2)}, u32[]{:S(2)}) async-start(bf16[4,256,768]{2,1,0:T(8,128)(2,1)} %get-tuple-element.42), calls=%async_computation | async-start | bytes 3145728 | tf_op jit(solution)/shard_map/cond/branch_1_fun/all_to_all | solution.py:700
  185.1 16.5 %collective-permute-start = (bf16[192,768]{1,0:T(8,128)(2,1)S(1)}, bf16[192,768]{1,0:T(8,128)(2,1)S(1)}, u32[]{:S(2)}, u32[]{:S(2)}) collective-permute-start(bf16[192,768]{1,0:T(8,128)(2,1)S(1)} %slice_bitcast_fusion), channel_id=1, source_target_pairs={{0,1},{1,0},{2,3},{3,2},{4,5},{5,4},{6,7},{7,6},{8,9},{9,8},{10,11... | collective-permute-start | bytes 884744 | tf_op jit(solution)/shard_map/cond/branch_1_fun/ppermute | solution.py:697
  212.8 20.0 %collective-permute-start.2 = (bf16[480,768]{1,0:T(8,128)(2,1)}, bf16[480,768]{1,0:T(8,128)(2,1)}, u32[]{:S(2)}, u32[]{:S(2)}) collective-permute-start(bf16[480,768]{1,0:T(8,128)(2,1)} %fold.4), channel_id=1, source_target_pairs={{0,1},{1,0},{2,3},{3,2},{4,5},{5,4},{6,7},{7,6},{8,9},{9,8},{10,11... | collective-permute-start | bytes 2211848 | tf_op jit(solution)/shard_map/cond/branch_1_fun/ppermute | solution.py:697
  244.7 55.9 %all-to-all-start.1 = ((bf16[8,88,768]{2,1,0:T(8,128)(2,1)}), bf16[8,88,768]{2,1,0:T(8,128)(2,1)}, u32[]{:S(2)}, u32[]{:S(2)}) async-start(bf16[8,88,768]{2,1,0:T(8,128)(2,1)} %bitcast.39), calls=%async_computation.1 | async-start | bytes 2162688 | tf_op jit(solution)/shard_map/cond/branch_1_fun/all_to_all | solution.py:871
  261.9 38.7 %collective-permute-start.9 = (bf16[384,768]{1,0:T(8,128)(2,1)}, bf16[384,768]{1,0:T(8,128)(2,1)}, u32[]{:S(2)}, u32[]{:S(2)}) collective-permute-start(bf16[384,768]{1,0:T(8,128)(2,1)} %get-tuple-element.80), channel_id=1, source_target_pairs={{0,2},{2,0},{4,6},{6,4},{8,10},{10,8},{12,14},{14,12},{16,18},{18,... | collective-permute-start | bytes 1769480 | tf_op jit(solution)/shard_map/cond/branch_1_fun/ppermute | solution.py:691
  261.9 38.7 %collective-permute-start.10 = (bf16[384,768]{1,0:T(8,128)(2,1)}, bf16[384,768]{1,0:T(8,128)(2,1)}, u32[]{:S(2)}, u32[]{:S(2)}) collective-permute-start(bf16[384,768]{1,0:T(8,128)(2,1)} %get-tuple-element.81), channel_id=1, source_target_pairs={{0,4},{2,6},{4,0},{6,2},{8,12},{10,14},{12,8},{14,10},{16,20},{18,... | collective-permute-start | bytes 1769480 | tf_op jit(solution)/shard_map/cond/branch_1_fun/ppermute | solution.py:691
  264.1 36.6 %collective-permute-start.11 = (bf16[384,768]{1,0:T(8,128)(2,1)}, bf16[384,768]{1,0:T(8,128)(2,1)}, u32[]{:S(2)}, u32[]{:S(2)}) collective-permute-start(bf16[384,768]{1,0:T(8,128)(2,1)} %get-tuple-element.82), channel_id=1, source_target_pairs={{0,6},{2,4},{4,2},{6,0},{8,14},{10,12},{12,10},{14,8},{16,22},{18,... | collective-permute-start | bytes 1769480 | tf_op jit(solution)/shard_map/cond/branch_1_fun/ppermute | solution.py:691
  283.3 17.3 %collective-permute-start.8 = (f32[7104]{0:T(1024)S(1)}, f32[7104]{0:T(1024)S(1)}, u32[]{:S(2)}, u32[]{:S(2)}) collective-permute-start(f32[7104]{0:T(1024)S(1)} %add.56), channel_id=1, source_target_pairs={{0,16},{2,18},{4,20},{6,22},{8,24},{10,26},{12,28},{14,30},{16,0},... | collective-permute-start | bytes 85256 | tf_op jit(solution)/shard_map/cond/branch_1_fun/ppermute | solution.py:691
  304.5 16.9 %collective-permute-start.29 = (bf16[1536,768]{1,0:T(8,128)(2,1)}, bf16[1536,768]{1,0:T(8,128)(2,1)}, u32[]{:S(2)}, u32[]{:S(2)}) collective-permute-start(bf16[1536,768]{1,0:T(8,128)(2,1)} %all-reduce.2.cloned.1.call-done.mine_ref), channel_id=1, source_target_pairs={{0,2},{2,0},{4,6},{6,4},{8,10},{10,8},{12,14},{14,12},{16,18},{18,... | collective-permute-start | bytes 7077896 | tf_op jit(solution)/shard_map/ppermute | solution.py:691
  307.4 31.4 %all-to-all-start.5 = ((bf16[8,88,768]{2,1,0:T(8,128)(2,1)}), bf16[8,88,768]{2,1,0:T(8,128)(2,1)S(1)}, u32[]{:S(2)}, u32[]{:S(2)}) async-start(bf16[8,88,768]{2,1,0:T(8,128)(2,1)} %spread_sum.1), calls=%async_computation.5 | async-start | bytes 2162688 | tf_op jit(solution)/shard_map/all_to_all | solution.py:875
  (54 other events, 467.9 us)
Sparse Core Ops, SparseCore 0:
  177.2 127.2 all-reduce.1

commit v6 on v5

--- a/solution.py
+++ b/solution.py
@@ -857,14 +857,14 @@
     )
     out_given = swap_core(out_theirs)
     back_given = swap_core(back_theirs)
-    cross_two = swap_tp(tie(made_other[1], cross_one, out_theirs))
+    cross_two = swap_tp(made_other[1])
     given, kept = lax.optimization_barrier((given, made_other[2], out_theirs))[:2]
     pair_sum, = fold(ids, [[(kept, None), (given, None)]], [lambda ids: 0], kept.shape[0])
     out_mine, back_mine, bias_four, *made_own = feed(
         ids, rows_mine, grads_mine, (feed_own,), tie(bias_here, cross_one, pair_sum),
         (out_mine, back_mine), (made_own,), PARTS,
     )
-    cross_three = swap_tp(tie(pair_sum, cross_two, out_mine))
+    cross_three = swap_tp(pair_sum)
 
     def scatter(value):
         parts = value.reshape(others, value.shape[0] // others, width)

time: 361 us -> 360 us (level)
  starting transfers between devices: 58.7 us -> 50.2 us
  Pallas kernels: 179 us -> 185 us
    ppermute x12, starting transfers between devices: 17.2 us -> 10.4 us  [swap_tp(): return lax.ppermute(value, 'tp', [(i, i ^ 1) for i in range(tp_count)])]
    unnamed x58 -> x54, local copies, waits for them, and re-layouts: 8.29 us -> 8.27 us
  transfers between devices with their start and end apart: 38 -> 38, of which waited for: 17 -> 15; matrix products, arithmetic and copies ran while one was open for 7% -> 7% of each run, Pallas kernels for 44% -> 46%
where the time goes in v6:
time: 360 us; the launch traced here: 354 us
  Pallas kernels  185 us (51%)
  waiting for transfers between devices  62.7 us (17%)
  starting transfers between devices  50.2 us (14%)
  local copies, waits for them, and re-layouts  30.5 us (8%)
  between operations  16.5 us (5%)
  other arithmetic  7.9 us (2%)
    pallas_call x4, Pallas kernels, feed(): call(partial(feed_kernel, len(weights) > 1, len(sums) > 0, len(made) > 0,...  53 us
    ppermute x19, waiting for transfers between devices, swap_seq(): lax.ppermute(value, 'seq', [(i, i ^ distance) for i in range(seq_count)])  35.5 us
    pallas_call x2, Pallas kernels, attend_back(): call(partial(attend_back_kernel, which * (heads // 2)), 1, (SPAN,), [pl.B...  34.7 us
    pallas_call x1, Pallas kernels, per_device(): call(attend_kernel, 1, (SPAN,), [placed(width), in_rows(width), full(flat...  23.2 us
    all_to_all x4, starting transfers between devices, to_seqs(): lax.all_to_all(value, 'seq', 0, 0, tiled=True, axis_index_groups=members)  15.5 us
    ppermute x19, starting transfers between devices, swap_seq(): lax.ppermute(value, 'seq', [(i, i ^ distance) for i in range(seq_count)])  14 us
    pallas_call x4, Pallas kernels, fold(): call(partial(fold_kernel, indices, starts), 1, (1,), [full(array.shape) f...  14 us
    ppermute x12, waiting for transfers between devices, swap_tp(): return lax.ppermute(value, 'tp', [(i, i ^ 1) for i in range(tp_count)])  12.8 us
  transfers between devices with their start and end apart: 38, of which 15 were waited for; matrix products, arithmetic and copies ran while one was open for 7% of the time, Pallas kernels for 46%

profile of v6, /device:TPU:0, one launch (start us, length us, event | category | flops | bytes accessed | tf_op | source)
XLA Modules:
  0.0 353.6 jit_solution(7770234816872859177)
XLA Ops:
  14.9 4.4 %all-to-all-start.2 = ((bf16[4,256,768]{2,1,0:T(8,128)(2,1)}), bf16[4,256,768]{2,1,0:T(8,128)(2,1)}, u32[]{:S(2)}, u32[]{:S(2)}) async-start(bf16[4,256,768]{2,1,0:T(8,128)(2,1)} %bitcast.15), calls=%async_computation.2 | async-start | bytes 3145728 | tf_op jit(solution)/shard_map/all_to_all | solution.py:700
  32.2 5.3 %collective-permute-done.13 = f32[1344]{0:T(1024)} collective-permute-done((f32[1344]{0:T(1024)}, f32[1344]{0:T(1024)}, u32[]{:S(2)}, u32[]{:S(2)}) %collective-permute-start.13) | collective-permute-done | bytes 5408 | tf_op jit(solution)/shard_map/ppermute | solution.py:697
  44.9 9.5 %project.1 = (bf16[4,256,768]{2,1,0:T(8,128)(2,1)}, bf16[1024,768]{1,0:T(8,128)(2,1)}, bf16[1024,768]{1,0:T(8,128)(2,1)}, bf16[2,1024,192]{2,1,0:T(8,128)(2,1)},...) custom-call(s32[11]{0:T(128)S(1)} %concatenate.31.ids, bf16[4,256,768]{2,1,0:T(8,128)(2,1)} %all-to-all-done.2.x_ref, ...), custom_call_target="tpu_custom_call" | custom-call | flops 10350000128 | bytes 10350000 | tf_op jit(solution)/shard_map/project/pallas_call | solution.py:777
  68.0 23.2 %attend.1 = (bf16[1024,768]{1,0:T(8,128)(2,1)}, bf16[4,256,768]{2,1,0:T(8,128)(2,1)}, f32[16,1024]{1,0:T(8,128)S(1)}, bf16[4,256,768]{2,1,0:T(8,128)(2,1)}, bf16[4,256,768]{2,1,0:T(8,128)(2,1)}) custom-call(s32[11]{0:T(128)S(1)} %copy-done.19, bf16[4,256,768]{2,1,0:T(8,128)(2,1)} %all-to-all-done.2.x_ref, bf16[1024,768]{1,0:T(8,128)(2,1)} %get-tuple-element.190.q_ref, ...), custom_call_target="tpu_custom_call" | custom-call | flops 31050000384 | bytes 31050000 | tf_op jit(solution)/shard_map/attend/pallas_call | solution.py:810
  93.7 12.4 %feed.4 = (bf16[1024,768]{1,0:T(8,128)(2,1)}, bf16[1024,768]{1,0:T(8,128)(2,1)}, f32[1,768]{1,0:T(1,128)S(1)}, bf16[1536,768]{1,0:T(8,128)(2,1)}) custom-call(s32[11]{0:T(128)S(1)} %copy-done.19, bf16[1024,768]{1,0:T(8,128)(2,1)} %bitcast.48, bf16[1024,768]{1,0:T(8,128)(2,1)} %bitcast.36, bf16[384,768]{1,0:T(8,128)(2,1)} %collective-permute-done.17.refs_2_, ...), custom_call_target="tpu_custom_call" | custom-call | flops 16099999744 | bytes 16100000 | tf_op jit(solution)/shard_map/feed/pallas_call | solution.py:296
  107.3 13.2 %feed.5 = (bf16[1024,768]{1,0:T(8,128)(2,1)}, bf16[1024,768]{1,0:T(8,128)(2,1)}, f32[1,768]{1,0:T(1,128)S(1)}, bf16[384,768]{1,0:T(8,128)(2,1)}, bf16[384,768]{1...) custom-call(s32[11]{0:T(128)S(1)} %copy-done.19, ...), custom_call_target="tpu_custom_call" | custom-call | flops 16099999744 | bytes 16100000 | tf_op jit(solution)/shard_map/feed/pallas_call | solution.py:296
  123.0 13.4 %feed.6 = (bf16[1024,768]{1,0:T(8,128)(2,1)}, bf16[1024,768]{1,0:T(8,128)(2,1)}, f32[1,768]{1,0:T(1,128)S(1)}, bf16[1536,768]{1,0:T(8,128)(2,1)}) custom-call(s32[11]{0:T(128)S(1)} %copy-done.19, bf16[1024,768]{1,0:T(8,128)(2,1)} %collective-permute-done.16.refs_0_, bf16[1024,768]{1,0:T(8,128)(2,1)} %copy-done.20, bf16[1536,768]{1,0:T(8,128)(2,1)} %copy-done.2, ...), custom_call_target="tpu_custom_call" | custom-call | flops 16099999744 | bytes 16100000 | tf_op jit(solution)/shard_map/feed/pallas_call | solution.py:296
  141.5 14.0 %feed.7 = (bf16[1024,768]{1,0:T(8,128)(2,1)}, bf16[1024,768]{1,0:T(8,128)(2,1)}, f32[1,768]{1,0:T(1,128)S(1)}, bf16[384,768]{1,0:T(8,128)(2,1)}, bf16[384,768]{1...) custom-call(s32[11]{0:T(128)S(1)} %copy-done.19, bf16[1024,768]{1,0:T(8,128)(2,1)} %bitcast.49, ...), custom_call_target="tpu_custom_call" | custom-call | flops 16099999744 | bytes 16100000 | tf_op jit(solution)/shard_map/feed/pallas_call | solution.py:296
  157.1 11.6 %residual.1 = (bf16[4,256,768]{2,1,0:T(8,128)(2,1)}, bf16[4,256,768]{2,1,0:T(8,128)(2,1)}, bf16[4,256,768]{2,1,0:T(8,128)(2,1)}, bf16[2,192,768]{2,1,0:T(8,128)(...) custom-call(s32[11]{0:T(128)S(1)} %copy-done.19, bf16[1024,768]{1,0:T(8,128)(2,1)} %get-tuple-element.219.out_a, ...), custom_call_target="tpu_custom_call" | custom-call | flops 14375000064 | bytes 14375000 | tf_op jit(solution)/shard_map/residual/pallas_call | solution.py:878
  169.6 4.9 %fold.7 = bf16[1536,768]{1,0:T(8,128)(2,1)} custom-call(s32[11]{0:T(128)S(1)} %copy-done.19, bf16[384,768]{1,0:T(8,128)(2,1)} %get-tuple-element.247.refs_0_, bf16[384,768]{1,0:T(8,128)(2,1)} %copy-done.26, bf16[384,768]{1,0:T(8,128)(2,1)} %get-tuple-element.248.refs_2_, bf16[384,768]{1,0:T(8,128)(2,1)} %copy-done.27, ...), custom_call_target="tpu_custom_call" | custom-call | flops 4024999936 | bytes 4025000 | tf_op jit(solution)/shard_map/fold/pallas_call | solution.py:521
  177.7 121.7 %conditional.1 = (bf16[1024,768]{1,0:T(8,128)(2,1)S(1)}, bf16[8,88,768]{2,1,0:T(8,128)(2,1)}, f32[7104]{0:T(1024)S(1)}, bf16[384,768]{1,0:T(8,128)(2,1)}, bf16[3...) conditional(s32[]{:T(128)} %convert_element_type.18, () %tuple.39, ...), branch_computations={%region_3.4_spmd, %region_4.5_spmd} | conditional | flops 72450031616 | bytes 138468224 | solution.py:1028
  177.7 3.9 %all-to-all-start = ((bf16[4,256,768]{2,1,0:T(8,128)(2,1)}), bf16[4,256,768]{2,1,0:T(8,128)(2,1)S(1)}, u32[]{:S(2)}, u32[]{:S(2)}) async-start(bf16[4,256,768]{2,1,0:T(8,128)(2,1)} %get-tuple-element.42), calls=%async_computation | async-start | bytes 3145728 | tf_op jit(solution)/shard_map/cond/branch_1_fun/all_to_all | solution.py:700
  183.7 17.2 %attend_back.2 = (bf16[4,256,960]{2,1,0:T(8,128)(2,1)}, bf16[4,64,768]{2,1,0:T(8,128)(2,1)}) custom-call(s32[11]{0:T(128)S(1)} %get-tuple-element.43.ids, bf16[1024,768]{1,0:T(8,128)(2,1)} %get-tuple-element.56.q_ref, bf16[1024,768]{1,0:T(8,128)(2,1)} %get-tuple-element.46.k_ref, bf16[1024,768]{1,0:T(8,128)(2,1)} %get-tuple-element.47.v_ref, ...), custom_call_target="tpu_custom_call" | custom-call | flops 20124999680 | bytes 20125000 | tf_op jit(solution)/shard_map/cond/branch_1_fun/attend_back/pallas_call | solution.py:922
  200.9 5.1 %weights.2 = (bf16[480,768]{1,0:T(8,128)(2,1)}, bf16[480,768]{1,0:T(8,128)(2,1)}, f32[1,960]{1,0:T(1,128)}) custom-call(s32[11]{0:T(128)S(1)} %get-tuple-element.43.ids, bf16[1024,768]{1,0:T(8,128)(2,1)S(1)} %bitcast.53, bf16[1024,960]{1,0:T(8,128)(2,1)} %bitcast.51), custom_call_target="tpu_custom_call" | custom-call | flops 6899999744 | bytes 6900000 | tf_op jit(solution)/shard_map/cond/branch_1_fun/weights/pallas_call | solution.py:949
  212.2 17.6 %attend_back.3 = (bf16[4,256,960]{2,1,0:T(8,128)(2,1)}, bf16[4,64,768]{2,1,0:T(8,128)(2,1)}) custom-call(s32[11]{0:T(128)S(1)} %get-tuple-element.43.ids, bf16[1024,768]{1,0:T(8,128)(2,1)} %get-tuple-element.56.q_ref, bf16[1024,768]{1,0:T(8,128)(2,1)} %get-tuple-element.46.k_ref, bf16[1024,768]{1,0:T(8,128)(2,1)} %get-tuple-element.47.v_ref, ...), custom_call_target="tpu_custom_call" | custom-call | flops 20124999680 | bytes 20125000 | tf_op jit(solution)/shard_map/cond/branch_1_fun/attend_back/pallas_call | solution.py:922
  231.1 5.1 %weights.3 = (bf16[480,768]{1,0:T(8,128)(2,1)}, bf16[480,768]{1,0:T(8,128)(2,1)}, f32[1,960]{1,0:T(1,128)}) custom-call(s32[11]{0:T(128)S(1)} %get-tuple-element.43.ids, bf16[1024,768]{1,0:T(8,128)(2,1)S(1)} %bitcast.54, bf16[1024,960]{1,0:T(8,128)(2,1)} %bitcast.52), custom_call_target="tpu_custom_call" | custom-call | flops 6899999744 | bytes 6900000 | tf_op jit(solution)/shard_map/cond/branch_1_fun/weights/pallas_call | solution.py:949
  243.0 6.5 %all-to-all-start.1 = ((bf16[8,88,768]{2,1,0:T(8,128)(2,1)}), bf16[8,88,768]{2,1,0:T(8,128)(2,1)}, u32[]{:S(2)}, u32[]{:S(2)}) async-start(bf16[8,88,768]{2,1,0:T(8,128)(2,1)} %bitcast.39), calls=%async_computation.1 | async-start | bytes 2162688 | tf_op jit(solution)/shard_map/cond/branch_1_fun/all_to_all | solution.py:871
  250.3 10.3 %input.1 = (bf16[384,768]{1,0:T(8,128)(2,1)}, bf16[384,768]{1,0:T(8,128)(2,1)}, bf16[384,768]{1,0:T(8,128)(2,1)}, bf16[384,768]{1,0:T(8,128)(2,1)}, f32[2,768]{1,0:T(2,128)}) custom-call(s32[11]{0:T(128)S(1)} %get-tuple-element.43.ids, bf16[4,256,960]{2,1,0:T(8,128)(2,1)} %get-tuple-element.61.own_ref, bf16[4,256,960]{2,1,0:T(8,128)(2,1)} %get-tuple-element.53.other_ref, ...), custom_call_target="tpu_custom_call" | custom-call | flops 10350000128 | bytes 10350000 | tf_op jit(solution)/shard_map/cond/branch_1_fun/input/pallas_call | solution.py:991
  270.6 10.6 %collective-permute-done.7 = f32[7104]{0:T(1024)S(1)} collective-permute-done((f32[7104]{0:T(1024)S(1)}, f32[7104]{0:T(1024)S(1)}, u32[]{:S(2)}, u32[]{:S(2)}) %collective-permute-start.7) | collective-permute-done | bytes 28448 | tf_op jit(solution)/shard_map/cond/branch_1_fun/ppermute | solution.py:691
  284.8 14.2 %collective-permute-done.8 = f32[7104]{0:T(1024)S(1)} collective-permute-done((f32[7104]{0:T(1024)S(1)}, f32[7104]{0:T(1024)S(1)}, u32[]{:S(2)}, u32[]{:S(2)}) %collective-permute-start.8) | collective-permute-done | bytes 28448 | tf_op jit(solution)/shard_map/cond/branch_1_fun/ppermute | solution.py:691
  311.9 4.6 %collect.1 = (f32[4,256,768]{2,1,0:T(8,128)}, f32[192,2048]{1,0:T(8,128)}) custom-call(s32[11]{0:T(128)S(1)} %copy-done.19, bf16[384,768]{1,0:T(8,128)(2,1)} %get-tuple-element.239.refs_0_, bf16[384,768]{1,0:T(8,128)(2,1)} %get-tuple-element.240.refs_1_, bf16[384,768]{1,0:T(8,128)(2,1)} %get-tuple-element.241.refs_2_, ...), custom_call_target="tpu_custom_call" | custom-call | flops 5750000128 | bytes 5750000 | tf_op jit(solution)/shard_map/collect/pallas_call | solution.py:571
  320.0 7.1 %place_feed.1 = (f32[768,1536]{1,0:T(8,128)}, f32[1536,768]{1,0:T(8,128)}) custom-call(s32[11]{0:T(128)} %broadcast_add_fusion.ids, bf16[1536,768]{1,0:T(8,128)(2,1)} %all-reduce.2.cloned.1.call-done.mine_ref, bf16[1536,768]{1,0:T(8,128)(2,1)} %collective-permute-done.29.theirs_ref), custom_call_target="tpu_custom_call" | custom-call | flops 9200000000 | bytes 9200000 | tf_op jit(solution)/shard_map/place_feed/pallas_call | solution.py:593
  327.1 10.0 %all-to-all-done.5 = bf16[8,88,768]{2,1,0:T(8,128)(2,1)S(1)} async-done(((bf16[8,88,768]{2,1,0:T(8,128)(2,1)}), bf16[8,88,768]{2,1,0:T(8,128)(2,1)S(1)}, u32[]{:S(2)}, u32[]{:S(2)}) %all-to-all-start.5) | async-done | bytes 1081376 | tf_op jit(solution)/shard_map/all_to_all | solution.py:875
  340.9 4.2 %place_qkv.1 = (f32[768,384]{1,0:T(8,128)}, f32[768,384]{1,0:T(8,128)}, f32[192,768]{1,0:T(8,128)}, f32[384,768]{1,0:T(8,128)}) custom-call(s32[11]{0:T(128)S(1)} %copy-done.19, bf16[704,768]{1,0:T(8,128)(2,1)} %bitcast.41, bf16[704,768]{1,0:T(8,128)(2,1)} %copy-done.23), custom_call_target="tpu_custom_call" | custom-call | flops 4600000000 | bytes 4600000 | tf_op jit(solution)/shard_map/place_qkv/pallas_call | solution.py:627
  (200 shorter events, 108.5 us)
Async XLA Ops:
  11.2 26.2 %collective-permute-start.12 = (bf16[672,768]{1,0:T(8,128)(2,1)}, bf16[672,768]{1,0:T(8,128)(2,1)}, u32[]{:S(2)}, u32[]{:S(2)}) collective-permute-start(bf16[672,768]{1,0:T(8,128)(2,1)} %pad_maximum_fusion.2), channel_id=1, source_target_pairs={{0,1},{1,0},{2,3},{3,2},{4,5},{5,4},{6,7},{7,6},{8,9},{9,8},{10,11... | collective-permute-start | bytes 3096584 | tf_op jit(solution)/shard_map/ppermute | solution.py:697
  14.9 22.5 %collective-permute-start.13 = (f32[1344]{0:T(1024)}, f32[1344]{0:T(1024)}, u32[]{:S(2)}, u32[]{:S(2)}) collective-permute-start(f32[1344]{0:T(1024)} %concatenate.35), channel_id=1, source_target_pairs={{0,1},{1,0},{2,3},{3,2},{4,5},{5,4},{6,7},{7,6},{8,9},{9,8},{10,11... | collective-permute-start | bytes 16136 | tf_op jit(solution)/shard_map/ppermute | solution.py:697
  14.9 26.5 %all-to-all-start.2 = ((bf16[4,256,768]{2,1,0:T(8,128)(2,1)}), bf16[4,256,768]{2,1,0:T(8,128)(2,1)}, u32[]{:S(2)}, u32[]{:S(2)}) async-start(bf16[4,256,768]{2,1,0:T(8,128)(2,1)} %bitcast.15), calls=%async_computation.2 | async-start | bytes 3145728 | tf_op jit(solution)/shard_map/all_to_all | solution.py:700
  39.0 19.0 %collective-permute-start.17 = (bf16[384,768]{1,0:T(8,128)(2,1)}, bf16[384,768]{1,0:T(8,128)(2,1)}, u32[]{:S(2)}, u32[]{:S(2)}) collective-permute-start(bf16[384,768]{1,0:T(8,128)(2,1)} %constant_dynamic-slice_fusion), channel_id=1, source_target_pairs={{0,1},{1,0},{2,3},{3,2},{4,5},{5,4},{6,7},{7,6},{8,9},{9,8},{10,11... | collective-permute-start | bytes 1769480 | tf_op jit(solution)/shard_map/ppermute | solution.py:697
  58.0 33.3 %all-to-all-start.4 = ((bf16[4,256,768]{2,1,0:T(8,128)(2,1)}), bf16[4,256,768]{2,1,0:T(8,128)(2,1)S(1)}, u32[]{:S(2)}, u32[]{:S(2)}) async-start(bf16[4,256,768]{2,1,0:T(8,128)(2,1)} %bitcast.34), calls=%async_computation.4 | async-start | bytes 3145728 | tf_op jit(solution)/shard_map/all_to_all | solution.py:700
  61.7 241.6 %all-reduce.2.cloned.1.call-start = ((), (), s32[]{:S(2)}) async-start(), calls=%async_computation.6 | async-start | bytes 4718592 | tf_op jit(solution)/shard_map/psum | solution.py:917
  61.9 31.8 %collective-permute-start.18 = (bf16[384,768]{1,0:T(8,128)(2,1)}, bf16[384,768]{1,0:T(8,128)(2,1)}, u32[]{:S(2)}, u32[]{:S(2)}) collective-permute-start(bf16[384,768]{1,0:T(8,128)(2,1)} %collective-permute-done.17.refs_2_), channel_id=1, source_target_pairs={{0,8},{2,10},{4,12},{6,14},{8,0},{10,2},{12,4},{14,6},{16,24},{18,... | collective-permute-start | bytes 1769480 | tf_op jit(solution)/shard_map/ppermute | solution.py:691
  63.8 29.9 %collective-permute-start.19 = (bf16[768,768]{1,0:T(8,128)(2,1)S(1)}, bf16[768,768]{1,0:T(8,128)(2,1)}, u32[]{:S(2)}, u32[]{:S(2)}) collective-permute-start(bf16[768,768]{1,0:T(8,128)(2,1)S(1)} %copy-done.10), channel_id=1, source_target_pairs={{0,1},{1,0},{2,3},{3,2},{4,5},{5,4},{6,7},{7,6},{8,9},{9,8},{10,11... | collective-permute-start | bytes 3538952 | tf_op jit(solution)/shard_map/ppermute | solution.py:697
  120.5 21.0 %collective-permute-start.21 = (bf16[384,768]{1,0:T(8,128)(2,1)}, bf16[384,768]{1,0:T(8,128)(2,1)S(1)}, u32[]{:S(2)}, u32[]{:S(2)}) collective-permute-start(bf16[384,768]{1,0:T(8,128)(2,1)} %get-tuple-element.205), channel_id=1, source_target_pairs={{0,1},{1,0},{2,3},{3,2},{4,5},{5,4},{6,7},{7,6},{8,9},{9,8},{10,11... | collective-permute-start | bytes 1769480 | tf_op jit(solution)/shard_map/ppermute | solution.py:697
  120.5 16.5 %collective-permute-start.22 = (bf16[384,768]{1,0:T(8,128)(2,1)}, bf16[384,768]{1,0:T(8,128)(2,1)S(1)}, u32[]{:S(2)}, u32[]{:S(2)}) collective-permute-start(bf16[384,768]{1,0:T(8,128)(2,1)} %get-tuple-element.206), channel_id=1, source_target_pairs={{0,8},{2,10},{4,12},{6,14},{8,0},{10,2},{12,4},{14,6},{16,24},{18,... | collective-permute-start | bytes 1769480 | tf_op jit(solution)/shard_map/ppermute | solution.py:691
  121.7 33.8 %collective-permute-start.23 = (bf16[384,768]{1,0:T(8,128)(2,1)}, bf16[384,768]{1,0:T(8,128)(2,1)S(1)}, u32[]{:S(2)}, u32[]{:S(2)}) collective-permute-start(bf16[384,768]{1,0:T(8,128)(2,1)} %get-tuple-element.218), channel_id=1, source_target_pairs={{0,1},{1,0},{2,3},{3,2},{4,5},{5,4},{6,7},{7,6},{8,9},{9,8},{10,11... | collective-permute-start | bytes 1769480 | tf_op jit(solution)/shard_map/ppermute | solution.py:697
  136.4 19.0 %collective-permute-start.25 = (bf16[1024,768]{1,0:T(8,128)(2,1)}, bf16[1024,768]{1,0:T(8,128)(2,1)S(1)}, u32[]{:S(2)}, u32[]{:S(2)}) collective-permute-start(bf16[1024,768]{1,0:T(8,128)(2,1)} %get-tuple-element.221), channel_id=1, source_target_pairs={{0,2},{2,0},{4,6},{6,4},{8,10},{10,8},{12,14},{14,12},{16,18},{18,... | collective-permute-start | bytes 4718600 | tf_op jit(solution)/shard_map/ppermute | solution.py:691
  136.4 19.0 %collective-permute-start.24 = (bf16[1024,768]{1,0:T(8,128)(2,1)}, bf16[1024,768]{1,0:T(8,128)(2,1)S(1)}, u32[]{:S(2)}, u32[]{:S(2)}) collective-permute-start(bf16[1024,768]{1,0:T(8,128)(2,1)} %get-tuple-element.211), channel_id=1, source_target_pairs={{0,2},{2,0},{4,6},{6,4},{8,10},{10,8},{12,14},{14,12},{16,18},{18,... | collective-permute-start | bytes 4718600 | tf_op jit(solution)/shard_map/ppermute | solution.py:691
  140.6 28.2 %collective-permute-start.28 = (bf16[384,768]{1,0:T(8,128)(2,1)}, bf16[384,768]{1,0:T(8,128)(2,1)S(1)}, u32[]{:S(2)}, u32[]{:S(2)}) collective-permute-start(bf16[384,768]{1,0:T(8,128)(2,1)} %fold.6), channel_id=1, source_target_pairs={{0,1},{1,0},{2,3},{3,2},{4,5},{5,4},{6,7},{7,6},{8,9},{9,8},{10,11... | collective-permute-start | bytes 1769480 | tf_op jit(solution)/shard_map/ppermute | solution.py:697
  177.7 34.5 %all-to-all-start = ((bf16[4,256,768]{2,1,0:T(8,128)(2,1)}), bf16[4,256,768]{2,1,0:T(8,128)(2,1)S(1)}, u32[]{:S(2)}, u32[]{:S(2)}) async-start(bf16[4,256,768]{2,1,0:T(8,128)(2,1)} %get-tuple-element.42), calls=%async_computation | async-start | bytes 3145728 | tf_op jit(solution)/shard_map/cond/branch_1_fun/all_to_all | solution.py:700
  182.6 18.2 %collective-permute-start = (bf16[192,768]{1,0:T(8,128)(2,1)S(1)}, bf16[192,768]{1,0:T(8,128)(2,1)S(1)}, u32[]{:S(2)}, u32[]{:S(2)}) collective-permute-start(bf16[192,768]{1,0:T(8,128)(2,1)S(1)} %slice_bitcast_fusion), channel_id=1, source_target_pairs={{0,1},{1,0},{2,3},{3,2},{4,5},{5,4},{6,7},{7,6},{8,9},{9,8},{10,11... | collective-permute-start | bytes 884744 | tf_op jit(solution)/shard_map/cond/branch_1_fun/ppermute | solution.py:697
  212.2 18.9 %collective-permute-start.2 = (bf16[480,768]{1,0:T(8,128)(2,1)}, bf16[480,768]{1,0:T(8,128)(2,1)}, u32[]{:S(2)}, u32[]{:S(2)}) collective-permute-start(bf16[480,768]{1,0:T(8,128)(2,1)} %fold.4), channel_id=1, source_target_pairs={{0,1},{1,0},{2,3},{3,2},{4,5},{5,4},{6,7},{7,6},{8,9},{9,8},{10,11... | collective-permute-start | bytes 2211848 | tf_op jit(solution)/shard_map/cond/branch_1_fun/ppermute | solution.py:697
  243.0 56.0 %all-to-all-start.1 = ((bf16[8,88,768]{2,1,0:T(8,128)(2,1)}), bf16[8,88,768]{2,1,0:T(8,128)(2,1)}, u32[]{:S(2)}, u32[]{:S(2)}) async-start(bf16[8,88,768]{2,1,0:T(8,128)(2,1)} %bitcast.39), calls=%async_computation.1 | async-start | bytes 2162688 | tf_op jit(solution)/shard_map/cond/branch_1_fun/all_to_all | solution.py:871
  260.6 38.4 %collective-permute-start.9 = (bf16[384,768]{1,0:T(8,128)(2,1)}, bf16[384,768]{1,0:T(8,128)(2,1)}, u32[]{:S(2)}, u32[]{:S(2)}) collective-permute-start(bf16[384,768]{1,0:T(8,128)(2,1)} %get-tuple-element.80), channel_id=1, source_target_pairs={{0,2},{2,0},{4,6},{6,4},{8,10},{10,8},{12,14},{14,12},{16,18},{18,... | collective-permute-start | bytes 1769480 | tf_op jit(solution)/shard_map/cond/branch_1_fun/ppermute | solution.py:691
  260.7 38.3 %collective-permute-start.10 = (bf16[384,768]{1,0:T(8,128)(2,1)}, bf16[384,768]{1,0:T(8,128)(2,1)}, u32[]{:S(2)}, u32[]{:S(2)}) collective-permute-start(bf16[384,768]{1,0:T(8,128)(2,1)} %get-tuple-element.81), channel_id=1, source_target_pairs={{0,4},{2,6},{4,0},{6,2},{8,12},{10,14},{12,8},{14,10},{16,20},{18,... | collective-permute-start | bytes 1769480 | tf_op jit(solution)/shard_map/cond/branch_1_fun/ppermute | solution.py:691
  262.8 36.3 %collective-permute-start.11 = (bf16[384,768]{1,0:T(8,128)(2,1)}, bf16[384,768]{1,0:T(8,128)(2,1)}, u32[]{:S(2)}, u32[]{:S(2)}) collective-permute-start(bf16[384,768]{1,0:T(8,128)(2,1)} %get-tuple-element.82), channel_id=1, source_target_pairs={{0,6},{2,4},{4,2},{6,0},{8,14},{10,12},{12,10},{14,8},{16,22},{18,... | collective-permute-start | bytes 1769480 | tf_op jit(solution)/shard_map/cond/branch_1_fun/ppermute | solution.py:691
  281.2 17.9 %collective-permute-start.8 = (f32[7104]{0:T(1024)S(1)}, f32[7104]{0:T(1024)S(1)}, u32[]{:S(2)}, u32[]{:S(2)}) collective-permute-start(f32[7104]{0:T(1024)S(1)} %add.56), channel_id=1, source_target_pairs={{0,16},{2,18},{4,20},{6,22},{8,24},{10,26},{12,28},{14,30},{16,0},... | collective-permute-start | bytes 85256 | tf_op jit(solution)/shard_map/cond/branch_1_fun/ppermute | solution.py:691
  303.3 16.7 %collective-permute-start.29 = (bf16[1536,768]{1,0:T(8,128)(2,1)}, bf16[1536,768]{1,0:T(8,128)(2,1)}, u32[]{:S(2)}, u32[]{:S(2)}) collective-permute-start(bf16[1536,768]{1,0:T(8,128)(2,1)} %all-reduce.2.cloned.1.call-done.mine_ref), channel_id=1, source_target_pairs={{0,2},{2,0},{4,6},{6,4},{8,10},{10,8},{12,14},{14,12},{16,18},{18,... | collective-permute-start | bytes 7077896 | tf_op jit(solution)/shard_map/ppermute | solution.py:691
  306.3 30.9 %all-to-all-start.5 = ((bf16[8,88,768]{2,1,0:T(8,128)(2,1)}), bf16[8,88,768]{2,1,0:T(8,128)(2,1)S(1)}, u32[]{:S(2)}, u32[]{:S(2)}) async-start(bf16[8,88,768]{2,1,0:T(8,128)(2,1)} %spread_sum.1), calls=%async_computation.5 | async-start | bytes 2162688 | tf_op jit(solution)/shard_map/all_to_all | solution.py:875
  (52 other events, 446.9 us)
Sparse Core Ops, SparseCore 0:
  174.6 128.7 all-reduce.1
